TPU v7x, 32 devices: a whole 2x2x4 slice. The times are simulated.
32 devices in a mesh: rep: 2 (over x), shard: 16 (over z, y, core).
Axes of the slice: x: 2, y: 2, z: 4, core: 2. Of those that a mesh axis runs over, the one named last changes fastest.
Arguments:
- tokens: bfloat16 [32, 1024, 1024], P(('rep', 'shard')), may hold values from -6 to 6
- lengths: int32 [32], P(('rep', 'shard')), may hold values from 1 to 1024, 24576 in all
- first_gain: float32 [1024], replicated, may hold values from 0.5 to 1.5
- first_bias: float32 [1024], replicated, may hold values from -1.75 to 1.75
- decay_rates: float32 [16], replicated, may hold values from 0.0005 to 0.05
- state_in: bfloat16 [16, 1024], P(None, 'shard'), may hold values from -0.1875 to 0.1875
- state_out: bfloat16 [16, 1024], P(None, 'shard'), may hold values from -1.5 to 1.5
- skip_gain: float32 [1024], replicated, may hold values from -6 to 6
- query_weight: bfloat16 [1024, 1024], P('shard'), may hold values from -0.1875 to 0.1875
- key_weight: bfloat16 [1024, 1024], P('shard'), may hold values from -0.1875 to 0.1875
- value_weight: bfloat16 [1024, 1024], P('shard'), may hold values from -0.1875 to 0.1875
- output_weight: bfloat16 [1024, 1024], P('shard'), may hold values from -0.5 to 0.5
- second_gain: float32 [1024], replicated, may hold values from 0.5 to 1.5
- second_bias: float32 [1024], replicated, may hold values from -1.75 to 1.75
- up_weight: bfloat16 [1024, 4096], P('shard'), may hold values from -0.1875 to 0.1875
- up_bias: float32 [4096], replicated, may hold values from -1.75 to 1.75
- down_weight: bfloat16 [4096, 1024], P('shard'), may hold values from -0.09375 to 0.09375
- down_bias: float32 [1024], replicated, may hold values from -1.75 to 1.75
- cotangent: bfloat16 [32, 1024, 1024], P(('rep', 'shard')), may hold values from -6 to 6
Outputs:
- result: bfloat16 [32, 1024, 1024], P(('rep', 'shard'))
- grad_tokens: bfloat16 [32, 1024, 1024], P(('rep', 'shard'))
- grad_first_gain: float32 [1024], replicated
- grad_first_bias: float32 [1024], replicated
- grad_decay_rates: float32 [16], replicated
- grad_state_in: float32 [16, 1024], P(None, 'shard')
- grad_state_out: float32 [16, 1024], P(None, 'shard')
- grad_skip_gain: float32 [1024], replicated
- grad_query_weight: float32 [1024, 1024], P('shard')
- grad_key_weight: float32 [1024, 1024], P('shard')
- grad_value_weight: float32 [1024, 1024], P('shard')
- grad_output_weight: float32 [1024, 1024], P('shard')
- grad_second_gain: float32 [1024], replicated
- grad_second_bias: float32 [1024], replicated
- grad_up_weight: float32 [1024, 4096], P('shard')
- grad_up_bias: float32 [4096], replicated
- grad_down_weight: float32 [4096, 1024], P('shard')
- grad_down_bias: float32 [1024], replicated
Inputs may be any that keep to these rules, and one draw needn't show every extreme that they name: `lengths`: live tokens of each sequence; its positions from its length to 1023 are padding; some sequence fills its whole slot.
All inputs are finite; a program needn't handle non-finite values. No bound on the sum of `lengths` on one device may be relied on, other than what follows from the above.
Results may differ from a plain program's by a relative error of at most 0.013.
The roundings to bfloat16 on the way count: a program that leaves them out, or rounds other values in their place, can miss the bound.
Values may be sent and summed in bfloat16 or wider, within the bound.
A program may use at most 256 MiB of HBM per device.

v0:
```python
import jax
import jax.numpy as jnp
from jax import lax
from jax.sharding import PartitionSpec as P

DH = 128
BLK = 512
CTX = 128
NBLK = 2


NORM_EPS = 1e-05
NEG_LARGE = -1e30
HIGHEST = lax.Precision.HIGHEST


def layer_norm(hidden, gain_vec, bias_vec):
    average = jnp.mean(hidden, axis=-1, keepdims=True)
    centred = hidden - average
    spread = jnp.mean(centred * centred, axis=-1, keepdims=True)
    return centred * lax.rsqrt(spread + NORM_EPS) * gain_vec + bias_vec


def state_context(driven_raw, normed, decay_rates, state_out, skip_gain):
    decay_factor = jnp.exp(-decay_rates)
    driven = driven_raw * jnp.sqrt(1.0 - decay_factor * decay_factor)
    factors = jnp.broadcast_to(decay_factor, driven.shape)

    def combine(earlier, subsequent):
        return (earlier[0] * subsequent[0], subsequent[0] * earlier[1] + subsequent[1])

    states = lax.associative_scan(combine, (factors, driven), axis=1)[1]
    seq_count = driven_raw.shape[0]
    state_width = driven_raw.shape[2]
    model_width = normed.shape[2]
    tail_states = states.reshape(seq_count, NBLK, BLK, state_width)[:, :, BLK - CTX :, :]
    skipped = normed.reshape(seq_count, NBLK, BLK, model_width)[:, :, BLK - CTX :, :]
    outputs = (
        jnp.einsum("sbcp,pd->sbcd", tail_states, state_out, precision=HIGHEST) + skip_gain * skipped
    )
    empty_ctx = jnp.zeros((seq_count, 1, CTX, model_width), jnp.float32)
    return jnp.concatenate([empty_ctx, outputs[:, : NBLK - 1]], axis=1)


def block_scores(queries, key_rows, ctx_keys, ctx_valid):
    row_count = queries.shape[0]
    head_count = queries.shape[1] // DH
    query_heads = queries.reshape(row_count, head_count, DH)
    key_heads = jnp.concatenate([ctx_keys, key_rows], 0).reshape(-1, head_count, DH)
    scores = jnp.einsum(
        "qhd,khd->hqk", query_heads, key_heads, preferred_element_type=jnp.float32
    ) * DH ** (-0.5)
    causal = lax.broadcasted_iota(jnp.int32, (row_count, row_count), 0) >= lax.broadcasted_iota(
        jnp.int32, (row_count, row_count), 1
    )
    allowed = jnp.concatenate(
        [jnp.broadcast_to(ctx_valid[None, :], (row_count, ctx_keys.shape[0])), causal], axis=1
    )
    return (jnp.where(allowed[None], scores, NEG_LARGE), query_heads, key_heads)


def attend_forward(block_item):
    queries, key_rows, value_rows, ctx_keys, ctx_values, ctx_valid = block_item
    scores, query_heads, key_heads = block_scores(queries, key_rows, ctx_keys, ctx_valid)
    row_max = jnp.max(scores, axis=-1, keepdims=True)
    expos = jnp.exp(scores - row_max)
    denominator = jnp.sum(expos, axis=-1, keepdims=True)
    weights = (expos / denominator).astype(jnp.bfloat16)
    value_heads = jnp.concatenate([ctx_values, value_rows], 0).reshape(key_heads.shape)
    attended = jnp.einsum("hqk,khd->qhd", weights, value_heads, preferred_element_type=jnp.float32)
    return (
        attended.reshape(queries.shape).astype(jnp.bfloat16),
        (row_max + jnp.log(denominator))[..., 0],
    )


def attend_backward(block_item):
    queries, key_rows, value_rows, ctx_keys, ctx_values, ctx_valid, log_total, grad_attended = (
        block_item
    )
    scores, query_heads, key_heads = block_scores(queries, key_rows, ctx_keys, ctx_valid)
    probs = jnp.exp(scores - log_total[..., None])
    value_heads = jnp.concatenate([ctx_values, value_rows], 0).reshape(key_heads.shape)
    grad_heads = grad_attended.reshape(query_heads.shape)
    grad_probs = jnp.einsum(
        "qhd,khd->hqk", grad_heads, value_heads, preferred_element_type=jnp.float32
    )
    grad_scores = (
        probs * (grad_probs - jnp.sum(probs * grad_probs, axis=-1, keepdims=True))
    ).astype(jnp.bfloat16)
    grad_values = jnp.einsum(
        "hqk,qhd->khd", probs.astype(jnp.bfloat16), grad_heads, preferred_element_type=jnp.float32
    )
    grad_queries = jnp.einsum(
        "hqk,khd->qhd", grad_scores, key_heads, preferred_element_type=jnp.float32
    ) * DH ** (-0.5)
    grad_keys = jnp.einsum(
        "hqk,qhd->khd", grad_scores, query_heads, preferred_element_type=jnp.float32
    ) * DH ** (-0.5)
    ctx_count = ctx_keys.shape[0]
    model_width = queries.shape[1]
    grad_keys = grad_keys.reshape(-1, model_width).astype(jnp.bfloat16)
    grad_values = grad_values.reshape(-1, model_width).astype(jnp.bfloat16)
    return (
        grad_queries.reshape(queries.shape).astype(jnp.bfloat16),
        grad_keys[ctx_count:],
        grad_values[ctx_count:],
        grad_keys[:ctx_count],
        grad_values[:ctx_count],
    )


def per_device(
    tokens,
    lengths,
    first_gain,
    first_bias,
    decay_rates,
    state_in,
    state_out,
    skip_gain,
    query_weight,
    key_weight,
    value_weight,
    output_weight,
    second_gain,
    second_bias,
    up_weight,
    up_bias,
    down_weight,
    down_bias,
    cotangent,
):
    full_query, full_key, full_value, full_output, full_up, full_down, full_in, full_out = (
        lax.all_gather(query_weight, "shard", axis=0, tiled=True),
        lax.all_gather(key_weight, "shard", axis=0, tiled=True),
        lax.all_gather(value_weight, "shard", axis=0, tiled=True),
        lax.all_gather(output_weight, "shard", axis=0, tiled=True),
        lax.all_gather(up_weight, "shard", axis=0, tiled=True),
        lax.all_gather(down_weight, "shard", axis=0, tiled=True),
        lax.all_gather(state_in, "shard", axis=1, tiled=True),
        lax.all_gather(state_out, "shard", axis=1, tiled=True),
    )
    seq_count, seq_len, model_width = tokens.shape
    row_count = seq_count * seq_len
    block_count = seq_count * NBLK
    positions = lax.broadcasted_iota(jnp.int32, (seq_count, seq_len), 1)
    row_mask = (positions < lengths[:, None]).astype(jnp.float32).reshape(row_count, 1)
    block_index = lax.broadcasted_iota(jnp.int32, (seq_count, NBLK, CTX), 1)
    ctx_valid = (block_index > 0).reshape(block_count, CTX)
    token_rows = tokens.astype(jnp.float32)
    normed, first_pullback = jax.vjp(layer_norm, token_rows, first_gain, first_bias)
    rounded = normed.astype(jnp.bfloat16)
    driven_raw = jnp.einsum("std,pd->stp", rounded, full_in, preferred_element_type=jnp.float32)
    context, state_pullback = jax.vjp(
        state_context, driven_raw, normed, decay_rates, full_out.astype(jnp.float32), skip_gain
    )
    ctx_rows = context.astype(jnp.bfloat16).reshape(block_count * CTX, model_width)
    flat_rounded = rounded.reshape(row_count, model_width)
    query_rows = jnp.dot(flat_rounded, full_query, preferred_element_type=jnp.float32).astype(
        jnp.bfloat16
    )
    key_rows = jnp.dot(flat_rounded, full_key, preferred_element_type=jnp.float32).astype(
        jnp.bfloat16
    )
    value_rows = jnp.dot(flat_rounded, full_value, preferred_element_type=jnp.float32).astype(
        jnp.bfloat16
    )
    ctx_keys = jnp.dot(ctx_rows, full_key, preferred_element_type=jnp.float32).astype(jnp.bfloat16)
    ctx_values = jnp.dot(ctx_rows, full_value, preferred_element_type=jnp.float32).astype(
        jnp.bfloat16
    )
    block_inputs = (
        query_rows.reshape(block_count, BLK, model_width),
        key_rows.reshape(block_count, BLK, model_width),
        value_rows.reshape(block_count, BLK, model_width),
        ctx_keys.reshape(block_count, CTX, model_width),
        ctx_values.reshape(block_count, CTX, model_width),
        ctx_valid,
    )
    attended, log_total = lax.map(attend_forward, block_inputs)
    attended_rows = attended.reshape(row_count, model_width)
    residual = token_rows.reshape(row_count, model_width) + jnp.dot(
        attended_rows, full_output, preferred_element_type=jnp.float32
    )
    second, second_pullback = jax.vjp(layer_norm, residual, second_gain, second_bias)
    second_rows = second.astype(jnp.bfloat16)
    hidden = jnp.dot(second_rows, full_up, preferred_element_type=jnp.float32) + up_bias
    active, gelu_pullback = jax.vjp(jax.nn.gelu, hidden)
    active_rows = active.astype(jnp.bfloat16)
    branch = jnp.dot(active_rows, full_down, preferred_element_type=jnp.float32) + down_bias
    result = (
        ((residual + branch) * row_mask)
        .astype(jnp.bfloat16)
        .reshape(seq_count, seq_len, model_width)
    )
    full_query, full_key, full_value, full_output, full_up, full_down, full_in, full_out = (
        lax.all_gather(query_weight, "shard", axis=0, tiled=True),
        lax.all_gather(key_weight, "shard", axis=0, tiled=True),
        lax.all_gather(value_weight, "shard", axis=0, tiled=True),
        lax.all_gather(output_weight, "shard", axis=0, tiled=True),
        lax.all_gather(up_weight, "shard", axis=0, tiled=True),
        lax.all_gather(down_weight, "shard", axis=0, tiled=True),
        lax.all_gather(state_in, "shard", axis=1, tiled=True),
        lax.all_gather(state_out, "shard", axis=1, tiled=True),
    )
    grad_branch = cotangent.reshape(row_count, model_width).astype(jnp.float32) * row_mask
    branch_rounded = grad_branch.astype(jnp.bfloat16)
    grad_down = jnp.einsum(
        "rf,rd->fd", active_rows, branch_rounded, preferred_element_type=jnp.float32
    )
    grad_down_bias = jnp.sum(grad_branch, axis=0)
    grad_active = jnp.einsum(
        "rd,fd->rf", branch_rounded, full_down, preferred_element_type=jnp.float32
    )
    (grad_hidden,) = gelu_pullback(grad_active)
    hidden_rounded = grad_hidden.astype(jnp.bfloat16)
    grad_up = jnp.einsum(
        "rd,rf->df", second_rows, hidden_rounded, preferred_element_type=jnp.float32
    )
    grad_up_bias = jnp.sum(hidden_rounded.astype(jnp.float32), axis=0)
    grad_second = jnp.einsum(
        "rf,df->rd", hidden_rounded, full_up, preferred_element_type=jnp.float32
    )
    grad_residual_part, grad_second_gain, grad_second_bias = second_pullback(grad_second)
    grad_residual = grad_branch + grad_residual_part
    residual_rounded = grad_residual.astype(jnp.bfloat16)
    grad_output = jnp.einsum(
        "rd,re->de", attended_rows, residual_rounded, preferred_element_type=jnp.float32
    )
    grad_attended = jnp.einsum(
        "re,de->rd", residual_rounded, full_output, preferred_element_type=jnp.float32
    ).astype(jnp.bfloat16)
    grad_query_rows, grad_key_rows, grad_value_rows, grad_ctx_keys, grad_ctx_values = lax.map(
        attend_backward,
        block_inputs + (log_total, grad_attended.reshape(block_count, BLK, model_width)),
    )
    grad_query_rows = grad_query_rows.reshape(row_count, model_width)
    grad_key_rows = grad_key_rows.reshape(row_count, model_width)
    grad_value_rows = grad_value_rows.reshape(row_count, model_width)
    grad_ctx_keys = grad_ctx_keys.reshape(block_count * CTX, model_width)
    grad_ctx_values = grad_ctx_values.reshape(block_count * CTX, model_width)
    grad_query = jnp.einsum(
        "rd,re->de", flat_rounded, grad_query_rows, preferred_element_type=jnp.float32
    )
    grad_key = jnp.einsum(
        "rd,re->de", flat_rounded, grad_key_rows, preferred_element_type=jnp.float32
    ) + jnp.einsum("rd,re->de", ctx_rows, grad_ctx_keys, preferred_element_type=jnp.float32)
    grad_value = jnp.einsum(
        "rd,re->de", flat_rounded, grad_value_rows, preferred_element_type=jnp.float32
    ) + jnp.einsum("rd,re->de", ctx_rows, grad_ctx_values, preferred_element_type=jnp.float32)
    grad_normed = (
        jnp.einsum("re,de->rd", grad_query_rows, full_query, preferred_element_type=jnp.float32)
        + jnp.einsum("re,de->rd", grad_key_rows, full_key, preferred_element_type=jnp.float32)
        + jnp.einsum("re,de->rd", grad_value_rows, full_value, preferred_element_type=jnp.float32)
    )
    grad_context = jnp.einsum(
        "re,de->rd", grad_ctx_keys, full_key, preferred_element_type=jnp.float32
    ) + jnp.einsum("re,de->rd", grad_ctx_values, full_value, preferred_element_type=jnp.float32)
    grad_context = grad_context.reshape(seq_count, NBLK, CTX, model_width)
    grad_driven, state_normed, grad_rates, grad_state_out, grad_skip = state_pullback(grad_context)
    grad_in = jnp.einsum(
        "stp,std->pd", grad_driven, rounded, precision=HIGHEST, preferred_element_type=jnp.float32
    )
    state_rounded = jnp.einsum(
        "stp,pd->std", grad_driven, full_in, precision=HIGHEST, preferred_element_type=jnp.float32
    )
    normed_total = (
        grad_normed.reshape(seq_count, seq_len, model_width) + state_rounded + state_normed
    )
    tokens_part, grad_first_gain, grad_first_bias = first_pullback(normed_total)
    grad_tokens = (tokens_part + grad_residual.reshape(seq_count, seq_len, model_width)).astype(
        jnp.bfloat16
    )
    piece_query, piece_key, piece_value, piece_output, piece_up, piece_down, piece_in, piece_out = (
        lax.psum_scatter(grad_query, "shard", scatter_dimension=0, tiled=True),
        lax.psum_scatter(grad_key, "shard", scatter_dimension=0, tiled=True),
        lax.psum_scatter(grad_value, "shard", scatter_dimension=0, tiled=True),
        lax.psum_scatter(grad_output, "shard", scatter_dimension=0, tiled=True),
        lax.psum_scatter(grad_up, "shard", scatter_dimension=0, tiled=True),
        lax.psum_scatter(grad_down, "shard", scatter_dimension=0, tiled=True),
        lax.psum_scatter(grad_in, "shard", scatter_dimension=1, tiled=True),
        lax.psum_scatter(grad_state_out, "shard", scatter_dimension=1, tiled=True),
    )
    piece_query, piece_key, piece_value, piece_output, piece_up, piece_down, piece_in, piece_out = (
        lax.psum(piece_query.astype(jnp.bfloat16), "rep").astype(jnp.float32),
        lax.psum(piece_key.astype(jnp.bfloat16), "rep").astype(jnp.float32),
        lax.psum(piece_value.astype(jnp.bfloat16), "rep").astype(jnp.float32),
        lax.psum(piece_output.astype(jnp.bfloat16), "rep").astype(jnp.float32),
        lax.psum(piece_up.astype(jnp.bfloat16), "rep").astype(jnp.float32),
        lax.psum(piece_down.astype(jnp.bfloat16), "rep").astype(jnp.float32),
        lax.psum(piece_in.astype(jnp.bfloat16), "rep").astype(jnp.float32),
        lax.psum(piece_out.astype(jnp.bfloat16), "rep").astype(jnp.float32),
    )
    (
        sum_first_gain,
        sum_first_bias,
        sum_rates,
        sum_skip,
        sum_second_gain,
        sum_second_bias,
        sum_up_bias,
        sum_down_bias,
    ) = lax.psum(
        (
            grad_first_gain,
            grad_first_bias,
            grad_rates,
            grad_skip,
            grad_second_gain,
            grad_second_bias,
            grad_up_bias,
            grad_down_bias,
        ),
        ("rep", "shard"),
    )
    return (
        result,
        grad_tokens,
        sum_first_gain,
        sum_first_bias,
        sum_rates,
        piece_in,
        piece_out,
        sum_skip,
        piece_query,
        piece_key,
        piece_value,
        piece_output,
        sum_second_gain,
        sum_second_bias,
        piece_up,
        sum_up_bias,
        piece_down,
        sum_down_bias,
    )


def solution(mesh):
    placed = (
        P(("rep", "shard"), None, None),
        P(("rep", "shard")),
        P(),
        P(),
        P(),
        P(None, "shard"),
        P(None, "shard"),
        P(),
        P("shard", None),
        P("shard", None),
        P("shard", None),
        P("shard", None),
        P(),
        P(),
        P("shard", None),
        P(),
        P("shard", None),
        P(),
        P(("rep", "shard"), None, None),
    )
    return jax.shard_map(
        per_device,
        mesh=mesh,
        in_specs=placed,
        out_specs=(
            P(("rep", "shard"), None, None),
            P(("rep", "shard"), None, None),
            P(),
            P(),
            P(),
            P(None, "shard"),
            P(None, "shard"),
            P(),
            P("shard", None),
            P("shard", None),
            P("shard", None),
            P("shard", None),
            P(),
            P(),
            P("shard", None),
            P(),
            P("shard", None),
            P(),
        ),
        check_vma=False,
    )
```

profile of v0, /device:TPU:0, one launch (start us, length us, event | category | flops | bytes accessed | tf_op | source)
XLA Modules:
  0.0 1287.6 jit_solution(255464946606225659)
XLA Ops:
  12.4 23.6 %all-gather = bf16[16,64,16]{1,2,0:T(8,128)(2,1)S(1)} all-gather(bf16[1,64,16]{1,2,0:T(8,128)(2,1)} %bitcast.341), channel_id=1, replica_groups=mesh['rep'=2,'shard'=16] {'shard'}, dimensions={0}, use_global_device_ids=true | all-gather | bytes 34816 | tf_op jit(solution)/shard_map/all_gather | solution.py:141
  55.8 17.6 %all-gather.1 = bf16[16,64,16]{1,2,0:T(8,128)(2,1)S(1)} all-gather(bf16[1,64,16]{1,2,0:T(8,128)(2,1)S(1)} %bitcast.342), channel_id=1, replica_groups=mesh['rep'=2,'shard'=16] {'shard'}, dimensions={0}, use_global_device_ids=true | all-gather | bytes 34816 | tf_op jit(solution)/shard_map/all_gather | solution.py:142
  73.6 4.2 copy.188
  77.9 5.4 copy.180
  101.5 5.3 fusion.81
  110.8 28.5 %all-gather.11.cloned.1.call-done = bf16[1024,1024]{1,0:T(8,128)(2,1)} async-done(((bf16[64,1024]{1,0:T(8,128)(2,1)}), bf16[1024,1024]{1,0:T(8,128)(2,1)}) %all-gather.11.cloned.1.call-update) | async-done | bytes 2097168 | tf_op jit(solution)/shard_map/all_gather | solution.py:135
  139.3 5.3 fusion.84
  144.6 4.5 copy.183
  149.0 5.3 fusion.87
  154.3 4.0 copy.185
  160.0 48.1 %while.30 = (s32[]{:T(128)}, bf16[2,512,1024]{2,1,0:T(8,128)(2,1)}, f32[2,8,512]{2,1,0:T(8,128)S(1)}, bf16[2,128,1024]{1,2,0:T(8,128)(2,1)}, bf16[2,512,1024]{1,...) while((s32[]{:T(128)}, bf16[2,512,1024]{2,1,0:T(8,128)(2,1)}, ...), condition=%wide.region_5.6_spmd, body=%wide.region_2.5_spmd.sunk | while | flops 1379987456 | bytes 57542468 | solution.py:181
  169.2 4.5 fusion.235
  176.5 4.8 fusion.237
  193.2 4.5 fusion.235
  200.5 4.8 fusion.237
  208.1 4.7 fusion.161
  215.4 41.8 %all-gather.17.cloned.1.call-done = bf16[1024,4096]{1,0:T(8,128)(2,1)} async-done(((bf16[64,4096]{1,0:T(8,128)(2,1)}), bf16[1024,4096]{1,0:T(8,128)(2,1)}) %all-gather.17.cloned.1.call-update) | async-done | bytes 8388624 | tf_op jit(solution)/shard_map/all_gather | solution.py:139
  257.2 16.9 %fusion.136 = f32[1024,4096]{1,0:T(8,128)} fusion(bf16[1024,4096]{1,0:T(8,128)(2,1)} %all-gather.17.cloned.1.call-done, f32[1024,1024]{0,1:T(8,128)} %copy-done.9, f32[1024]{0:T(1024)S(1)} %copy-done.149, f32[1024]{0:T(1024)S(1)} %copy-done.132, f32[1024]{0:T(1024)S(1)} %fusion.120, f32[1024]{0:T(1024)S(1)} %broadcast_multiply_fusion.17), kind=kOutput, calls=%fused_computation.300 | convolution fusion | flops 8595177472 | bytes 29376512 | tf_op jit(solution)/shard_map/dot_general | solution.py:188
  274.1 58.3 %all-gather.19.cloned.1.call-done = bf16[4096,1024]{1,0:T(8,128)(2,1)} async-done(((bf16[256,1024]{1,0:T(8,128)(2,1)}), bf16[4096,1024]{1,0:T(8,128)(2,1)}) %all-gather.19.cloned.1.call-update) | async-done | bytes 8388624 | tf_op jit(solution)/shard_map/all_gather | solution.py:140
  332.4 25.0 %convert_reduce_fusion = (f32[4096]{0:T(1024)}, bf16[1024,4096]{1,0:T(8,128)(2,1)}) fusion(f32[1024,4096]{1,0:T(8,128)} %fusion.136, f32[4096]{0:T(1024)S(1)} %copy-done.147, bf16[4096,1024]{1,0:T(8,128)(2,1)} %all-gather.19.cloned.1.call-done, bf16[1,1024,1024]{1,2,0:T(8,128)(2,1)S(1)} %copy-done.14, f32[1024]{0:T(1024)S(1)} %copy-done.111), kind=kOutput, calls=%fused_computation.79 | convolution fusion | flops 8689545216 | bytes 35688448 | tf_op jit(solution)/shard_map/rd,fd->rf/dot_general | solution.py:213
  357.4 15.7 %fusion.162 = (f32[1024]{0:T(1024)}, f32[1024,1024]{1,0:T(8,128)}) fusion(bf16[1024,4096]{1,0:T(8,128)(2,1)} %get-tuple-element.485, bf16[1024,4096]{1,0:T(8,128)(2,1)} %all-gather.17.cloned.1.call-done), kind=kOutput, calls=%fused_computation.324 | convolution fusion | flops 8590982144 | bytes 20975616 | tf_op jit(solution)/shard_map/rf,df->rd/dot_general | solution.py:222
  373.1 5.7 copy.189
  378.8 5.4 multiply_reduce_fusion.1
  389.3 4.4 fusion.167
  395.3 5.4 convolution_convert_fusion
  405.5 99.0 %while.31 = (s32[]{:T(128)}, bf16[2,512,1024]{2,1,0:T(8,128)(2,1)}, bf16[2,512,1024]{2,1,0:T(8,128)(2,1)}, bf16[2,512,1024]{2,1,0:T(8,128)(2,1)}, bf16[2,128,102...) while((s32[]{:T(128)}, bf16[2,512,1024]{2,1,0:T(8,128)(2,1)}, ...), condition=%wide.region_12.13_spmd, body=%wide.region_10.12_spmd.sunk | while | flops 3406229504 | bytes 220317776 | solution.py:234
  430.4 7.4 multiply_reduce_fusion.5
  479.8 7.4 multiply_reduce_fusion.5
  504.5 4.6 fusion.65
  513.7 4.0 fusion.67
  520.5 6.1 fusion.69
  528.3 21.0 %fusion.90 = f32[4096,1024]{1,0:T(8,128)} fusion(bf16[1,1024,1024]{1,2,0:T(8,128)(2,1)S(1)} %copy-done.15, f32[1024]{0:T(1024)S(1)} %copy-done.112, f32[1024,4096]{1,0:T(8,128)} %fusion.136, f32[4096]{0:T(1024)S(1)} %copy-done.148), kind=kOutput, calls=%fused_computation.133 | convolution fusion | flops 8635023360 | bytes 35672064 | tf_op jit(solution)/shard_map/rf,rd->fd/dot_general | solution.py:209
  550.0 16.7 %fusion.135 = f32[1024,4096]{1,0:T(8,128)} fusion(bf16[1024,4096]{1,0:T(8,128)(2,1)} %get-tuple-element.485, f32[1024,1024]{0,1:T(8,128)} %copy-done.9, f32[1024]{0:T(1024)S(1)} %copy-done.150, f32[1024]{0:T(1024)S(1)} %copy-done.133, f32[1024]{0:T(1024)S(1)} %copy-done.116, f32[1024]{0:T(1024)S(1)} %copy-done.108), kind=kOutput, calls=%fused_computation.299 | convolution fusion | flops 8595177472 | bytes 29376512 | tf_op jit(solution)/shard_map/rd,rf->df/dot_general | solution.py:218
  609.3 5.4 copy.208
  614.7 5.2 fusion.165
  625.2 5.3 fusion.57
  630.5 17.3 %fusion.64 = bf16[1,1024,1024]{1,2,0:T(8,128)(2,1)} fusion(f32[1024,1024]{0,1:T(8,128)} %copy-done.9, f32[1024]{0:T(1024)S(1)} %copy-done.112, f32[1024]{0:T(1024)S(1)} %copy-done.151, bf16[4096,1024]{1,0:T(8,128)(2,1)} %all-gather.19.cloned.1.call-done, f32[1024,4096]{1,0:T(8,128)} %fusion.136, f32[4096]{0:T(1024)S(1)} %copy-done.148), kind=kOutput, calls=%fused_computation.112 | convolution fusion | flops 8636071936 | bytes 31481856 | tf_op jit(solution)/shard_map/dot_general | solution.py:191
  651.1 7.5 reduce-scatter.15.cloned.1.call-done
  660.2 73.9 %reduce-scatter.13.cloned.1.call-done = f32[64,1024]{1,0:T(8,128)} async-done(((f32[1024,1024]{1,0:T(8,128)}), f32[64,1024]{1,0:T(8,128)}) %reduce-scatter.13.cloned.1.call-update) | async-done | bytes 262160 | tf_op jit(solution)/shard_map/reduce_scatter | solution.py:276
  735.7 180.2 %reduce-scatter.23.cloned.1.call-done = f32[256,1024]{1,0:T(8,128)} async-done(((f32[4096,1024]{1,0:T(8,128)}), f32[256,1024]{1,0:T(8,128)}) %reduce-scatter.23.cloned.1.call-update) | async-done | bytes 1048592 | tf_op jit(solution)/shard_map/reduce_scatter | solution.py:281
  918.0 179.4 %reduce-scatter.21.cloned.1.call-done = f32[64,4096]{1,0:T(8,128)} async-done(((f32[1024,4096]{1,0:T(8,128)}), f32[64,4096]{1,0:T(8,128)}) %reduce-scatter.21.cloned.1.call-update) | async-done | bytes 1048592 | tf_op jit(solution)/shard_map/reduce_scatter | solution.py:280
  1105.7 4.0 copy.210
  1113.1 6.5 fusion.62
  1119.6 4.0 copy.211
  1123.8 40.5 %all-reduce.99 = (f32[1024]{0:T(1024)}, f32[1024]{0:T(1024)}, f32[16]{0:T(128)}, f32[1024]{0:T(1024)}, f32[1024]{0:T(1024)}, /*index=5*/f32[1024]{0:T(1024)}, f32[4096]{0:T(1024)}, f32[1024]{0:T(1024)}) all-reduce(f32[1024]{0:T(1024)S(1)} %get-tuple-element.301, ...), channel_id=1, replica_groups=mesh['rep'=2,'shard'=16] {'rep','shard'}, use_global_device_ids=true, to_apply=%region_16.17 | all-reduce | flops 10256 | bytes 82048 | tf_op jit(solution)/shard_map/psum | solution.py:304
  1165.1 50.6 %reduce-scatter.25.cloned.1.call-done = f32[64,16]{1,0:T(8,128)} async-done(((f32[1024,16]{1,0:T(8,128)}), f32[64,16]{1,0:T(8,128)}) %reduce-scatter.25.cloned.1.call-update) | async-done | bytes 4112
  1216.5 5.0 all-reduce.100
  1222.7 47.5 %all-reduce.104.cloned.1.call-done = (bf16[64,1024]{1,0:T(8,128)(2,1)}, bf16[64,1024]{1,0:T(8,128)(2,1)}, bf16[64,1024]{1,0:T(8,128)(2,1)}, bf16[64,1024]{1,0:T(...) async-done(((bf16[64,1024]{1,0:T(8,128)(2,1)}, bf16[64,1024]{1,0:T(8,128)(2,1)}, bf16[64,1024]{1,0:T(8,128)(2,1)}, bf16[64,1024]{1,0:T(8,128)(2,1)}, ...) | async-done | bytes 1572880 | tf_op jit(solution)/shard_map/psum | solution.py:286
  (747 shorter events, 264.5 us)
Async XLA Ops:
  7.2 87.5 %all-gather.13.cloned.1.call-start = ((), (), s32[]{:S(2)}) async-start(), calls=%async_computation.10 | async-start | bytes 2228224 | tf_op jit(solution)/shard_map/all_gather | solution.py:136
  7.9 90.3 %all-gather.9.cloned.1.call-start = ((), (), s32[]{:S(2)}) async-start(), calls=%async_computation.8 | async-start | bytes 2228224 | tf_op jit(solution)/shard_map/all_gather | solution.py:137
  8.7 130.6 %all-gather.11.cloned.1.call-start = ((), (), s32[]{:S(2)}) async-start(), calls=%async_computation.9 | async-start | bytes 2228224 | tf_op jit(solution)/shard_map/all_gather | solution.py:135
  9.4 198.7 %all-gather.15.cloned.1.call-start = ((), (), s32[]{:S(2)}) async-start(), calls=%async_computation.11 | async-start | bytes 2228224 | tf_op jit(solution)/shard_map/all_gather | solution.py:138
  10.0 247.2 %all-gather.17.cloned.1.call-start = ((), (), s32[]{:S(2)}) async-start(), calls=%async_computation.12 | async-start | bytes 8912896 | tf_op jit(solution)/shard_map/all_gather | solution.py:139
  10.6 321.8 %all-gather.19.cloned.1.call-start = ((), (), s32[]{:S(2)}) async-start(), calls=%async_computation.13 | async-start | bytes 8912896 | tf_op jit(solution)/shard_map/all_gather | solution.py:140
  11.1 636.7 %reduce-scatter.19.cloned.1.call-start = ((), (), s32[]{:S(2)}) async-start(), calls=%async_computation.17 | async-start | bytes 4456448 | tf_op jit(solution)/shard_map/reduce_scatter | solution.py:279
  12.4 32.3 %copy-start.140 = (f32[16]{0:T(128)}, f32[16]{0:T(128)S(1)}, u32[]{:S(2)}) copy-start(f32[16]{0:T(128)S(1)} %get-tuple-element.475) | copy-start | bytes 196
  12.4 70.9 %copy-start.139 = (f32[16]{0:T(128)}, f32[16]{0:T(128)S(1)}, u32[]{:S(2)}) copy-start(f32[16]{0:T(128)S(1)} %get-tuple-element.397) | copy-start | bytes 196
  12.4 72.5 %copy-start.119 = (f32[16]{0:T(128)}, f32[16]{0:T(128)S(1)}, u32[]{:S(2)}) copy-start(f32[16]{0:T(128)S(1)} %get-tuple-element.398) | copy-start | bytes 196
  12.4 72.9 %copy-start.125 = (f32[16]{0:T(128)}, f32[16]{0:T(128)S(1)}, u32[]{:S(2)}) copy-start(f32[16]{0:T(128)S(1)} %get-tuple-element.476) | copy-start | bytes 196
  12.4 73.5 %copy-start.123 = (f32[16]{0:T(128)}, f32[16]{0:T(128)S(1)}, u32[]{:S(2)}) copy-start(f32[16]{0:T(128)S(1)} %get-tuple-element.474) | copy-start | bytes 196
  12.4 74.4 %copy-start.121 = (f32[16]{0:T(128)}, f32[16]{0:T(128)S(1)}, u32[]{:S(2)}) copy-start(f32[16]{0:T(128)S(1)} %get-tuple-element.473) | copy-start | bytes 196
  46.5 27.0 %copy-start.43 = (f32[1,512,16]{1,2,0:T(8,128)}, f32[1,512,16]{1,2,0:T(8,128)S(1)}, u32[]{:S(2)}) copy-start(f32[1,512,16]{1,2,0:T(8,128)S(1)} %slice.315) | copy-start | bytes 98308
  53.6 30.2 %copy-start.131 = (f32[16]{0:T(128)}, f32[16]{0:T(128)S(1)}, u32[]{:S(2)}) copy-start(f32[16]{0:T(128)S(1)} %get-tuple-element.470) | copy-start | bytes 196
  53.6 30.5 %copy-start.129 = (f32[16]{0:T(128)}, f32[16]{0:T(128)S(1)}, u32[]{:S(2)}) copy-start(f32[16]{0:T(128)S(1)} %get-tuple-element.472) | copy-start | bytes 196
  53.6 30.8 %copy-start.127 = (f32[16]{0:T(128)}, f32[16]{0:T(128)S(1)}, u32[]{:S(2)}) copy-start(f32[16]{0:T(128)S(1)} %get-tuple-element.471) | copy-start | bytes 196
  54.9 28.4 %copy-start.89 = (f32[1,2,16]{1,2,0:T(8,128)}, f32[1,2,16]{1,2,0:T(8,128)S(1)}, u32[]{:S(2)}) copy-start(f32[1,2,16]{1,2,0:T(8,128)S(1)} %slice.355) | copy-start | bytes 388
  55.7 27.6 %copy-start.93 = (f32[1,1,16]{1,2,0:T(8,128)}, f32[1,1,16]{1,2,0:T(8,128)S(1)}, u32[]{:S(2)}) copy-start(f32[1,1,16]{1,2,0:T(8,128)S(1)} %copy.176) | copy-start | bytes 196
  55.8 27.7 %copy-start.91 = (f32[1,1,16]{1,2,0:T(8,128)}, f32[1,1,16]{1,2,0:T(8,128)S(1)}, u32[]{:S(2)}) copy-start(f32[1,1,16]{1,2,0:T(8,128)S(1)} %copy.177) | copy-start | bytes 196
  73.6 19.7 %copy-start.41 = (bf16[1024,16,1]{0,1,2:T(8,128)(2,1)}, bf16[1024,16,1]{0,1,2:T(8,128)(2,1)S(1)}, u32[]{:S(2)}) copy-start(bf16[1024,16,1]{0,1,2:T(8,128)(2,1)S(1)} %reshape.393) | copy-start | bytes 98308
  160.0 48.1 %copy-start.6 = (bf16[1,1024,1024]{1,2,0:T(8,128)(2,1)S(1)}, bf16[1,1024,1024]{1,2,0:T(8,128)(2,1)}, u32[]{:S(2)}) copy-start(bf16[1,1024,1024]{1,2,0:T(8,128)(2,1)} %copy-done.5) | copy-start | bytes 6291460
  212.8 44.4 %copy-start.132 = (f32[1024]{0:T(1024)S(1)}, f32[1024]{0:T(1024)}, u32[]{:S(2)}) copy-start(f32[1024]{0:T(1024)} %param.35) | copy-start | bytes 12292
  212.8 44.4 %copy-start.149 = (f32[1024]{0:T(1024)S(1)}, f32[1024]{0:T(1024)}, u32[]{:S(2)}) copy-start(f32[1024]{0:T(1024)} %param.36) | copy-start | bytes 12292
  212.8 171.4 %copy-start.107 = (f32[1024]{0:T(1024)}, f32[1024]{0:T(1024)S(1)}, u32[]{:S(2)}) copy-start(f32[1024]{0:T(1024)S(1)} %broadcast_multiply_fusion.17) | copy-start | bytes 12292
  215.4 168.9 %copy-start.115 = (f32[1024]{0:T(1024)}, f32[1024]{0:T(1024)S(1)}, u32[]{:S(2)}) copy-start(f32[1024]{0:T(1024)S(1)} %fusion.120) | copy-start | bytes 12292
  215.4 117.0 %copy-start.14 = (bf16[1,1024,1024]{1,2,0:T(8,128)(2,1)S(1)}, bf16[1,1024,1024]{1,2,0:T(8,128)(2,1)}, u32[]{:S(2)}) copy-start(bf16[1,1024,1024]{1,2,0:T(8,128)(2,1)} %copy.188) | copy-start | bytes 6291460
  215.4 117.0 %copy-start.111 = (f32[1024]{0:T(1024)S(1)}, f32[1024]{0:T(1024)}, u32[]{:S(2)}) copy-start(f32[1024]{0:T(1024)} %fusion.118) | copy-start | bytes 12292
  215.4 117.0 %copy-start.147 = (f32[4096]{0:T(1024)S(1)}, f32[4096]{0:T(1024)}, u32[]{:S(2)}) copy-start(f32[4096]{0:T(1024)} %param.38) | copy-start | bytes 49156
  393.8 255.7 %reduce-scatter.17.cloned.1.call-start = ((), (), s32[]{:S(2)}) async-start(), calls=%async_computation.16 | async-start | bytes 4456448 | tf_op jit(solution)/shard_map/reduce_scatter | solution.py:278
  512.1 146.5 %reduce-scatter.15.cloned.1.call-start = ((), (), s32[]{:S(2)}) async-start(), calls=%async_computation.15 | async-start | bytes 4456448 | tf_op jit(solution)/shard_map/reduce_scatter | solution.py:277
  520.4 213.7 %reduce-scatter.13.cloned.1.call-start = ((), (), s32[]{:S(2)}) async-start(), calls=%async_computation.14 | async-start | bytes 4456448 | tf_op jit(solution)/shard_map/reduce_scatter | solution.py:276
  526.6 389.3 %reduce-scatter.23.cloned.1.call-start = ((), (), s32[]{:S(2)}) async-start(), calls=%async_computation.19 | async-start | bytes 17825792 | tf_op jit(solution)/shard_map/reduce_scatter | solution.py:281
  549.3 548.1 %reduce-scatter.21.cloned.1.call-start = ((), (), s32[]{:S(2)}) async-start(), calls=%async_computation.18 | async-start | bytes 17825792 | tf_op jit(solution)/shard_map/reduce_scatter | solution.py:280
  566.7 597.5 %reduce-scatter.27.cloned.1.call-start = ((), (), s32[]{:S(2)}) async-start(), calls=%async_computation.21 | async-start | bytes 557056
  570.3 18.6 %copy-start.100 = (f32[1,32,16]{1,2,0:T(8,128)S(1)}, f32[1,32,16]{1,2,0:T(8,128)}, u32[]{:S(2)}) copy-start(f32[1,32,16]{1,2,0:T(8,128)} %copy-done.99) | copy-start | bytes 6148
  570.3 19.2 %copy-start.98 = (f32[1,64,16]{1,2,0:T(8,128)S(1)}, f32[1,64,16]{1,2,0:T(8,128)}, u32[]{:S(2)}) copy-start(f32[1,64,16]{1,2,0:T(8,128)} %copy-done.97) | copy-start | bytes 12292
  570.4 20.2 %copy-start.96 = (f32[1,128,16]{1,2,0:T(8,128)S(1)}, f32[1,128,16]{1,2,0:T(8,128)}, u32[]{:S(2)}) copy-start(f32[1,128,16]{1,2,0:T(8,128)} %copy-done.95) | copy-start | bytes 24580
  570.4 22.0 %copy-start.54 = (f32[1,256,16]{1,2,0:T(8,128)S(1)}, f32[1,256,16]{1,2,0:T(8,128)}, u32[]{:S(2)}) copy-start(f32[1,256,16]{1,2,0:T(8,128)} %copy-done.53) | copy-start | bytes 49156
  571.2 24.4 %copy-start.44 = (f32[1,512,16]{1,2,0:T(8,128)S(1)}, f32[1,512,16]{1,2,0:T(8,128)}, u32[]{:S(2)}) copy-start(f32[1,512,16]{1,2,0:T(8,128)} %copy-done.43) | copy-start | bytes 98308
  571.2 29.3 %copy-start.52 = (f32[1,2,128,16]{2,1,3,0:T(2,128)S(1)}, f32[1,2,128,16]{2,1,3,0:T(2,128)}, u32[]{:S(2)}) copy-start(f32[1,2,128,16]{2,1,3,0:T(2,128)} %copy-done.51) | copy-start | bytes 49156
  571.2 31.2 %copy-start.36 = (f32[1024,16]{0,1:T(8,128)S(1)}, f32[1024,16]{0,1:T(8,128)}, u32[]{:S(2)}) copy-start(f32[1024,16]{0,1:T(8,128)} %copy-done.35) | copy-start | bytes 196612
  571.2 31.3 %copy-start.19 = (bf16[1,1024,1024]{1,2,0:T(8,128)(2,1)S(1)}, bf16[1,1024,1024]{1,2,0:T(8,128)(2,1)}, u32[]{:S(2)}) copy-start(bf16[1,1024,1024]{1,2,0:T(8,128)(2,1)} %copy-done.16) | copy-start | bytes 6291460
  574.9 27.6 %copy-start.141 = (f32[16]{0:T(128)S(1)}, f32[16]{0:T(128)}, u32[]{:S(2)}) copy-start(f32[16]{0:T(128)} %copy-done.140) | copy-start | bytes 196
  577.0 28.2 %copy-start.135 = (f32[1024]{0:T(1024)S(1)}, f32[1024]{0:T(1024)}, u32[]{:S(2)}) copy-start(f32[1024]{0:T(1024)} %param.30) | copy-start | bytes 12292
  605.2 610.5 %reduce-scatter.25.cloned.1.call-start = ((), (), s32[]{:S(2)}) async-start(), calls=%async_computation.20 | async-start | bytes 557056
  614.7 655.5 %all-reduce.104.cloned.1.call-start = ((), (), s32[]{:S(2)}) async-start(), calls=%async_computation.22 | async-start | bytes 3145728 | tf_op jit(solution)/shard_map/psum | solution.py:286
  647.8 451.7 %copy-start.88 = (f32[1024]{0:T(1024)S(1)}, f32[1024]{0:T(1024)}, u32[]{:S(2)}) copy-start(f32[1024]{0:T(1024)} %copy-done.87) | copy-start | bytes 12292
  (133 other events, 777.1 us)
Sparse Core Ops, SparseCore 0:
  10.2 44.2 all-gather.12
  56.6 40.1 all-gather.8
  99.0 40.2 all-gather.10
  141.3 40.1 all-gather.14
  183.5 73.6 all-gather.16
  259.2 73.1 all-gather.18
  393.9 70.9 reduce-scatter.18
  512.2 70.8 reduce-scatter.16
  587.0 71.5 reduce-scatter.14
  662.7 71.3 reduce-scatter.12
  738.2 177.6 reduce-scatter.22
  919.9 177.5 reduce-scatter.20
  1101.5 54.9 reduce-scatter.26
  1160.9 54.7 reduce-scatter.24
  1218.7 51.4 all-reduce.103
where the time goes:
time: 1300 us; the launch traced here: 1290 us
  waiting for transfers between devices  671 us (52%)
  matrix products  244 us (19%)
  local copies, waits for them, and re-layouts  190 us (15%)
  blocking collectives  86.6 us (7%)
  other arithmetic  76.2 us (6%)
  between operations  17.2 us (1%)
    reduce_scatter x1, waiting for transfers between devices, per_device(): lax.psum_scatter(grad_down, 'shard', scatter_dimension=0, tiled=True)  180 us
    reduce_scatter x1, waiting for transfers between devices, per_device(): lax.psum_scatter(grad_up, 'shard', scatter_dimension=0, tiled=True)  179 us
    reduce_scatter x1, waiting for transfers between devices, per_device(): lax.psum_scatter(grad_query, 'shard', scatter_dimension=0, tiled=True)  73.9 us
    all_gather x1, waiting for transfers between devices, per_device(): lax.all_gather(down_weight, 'shard', axis=0, tiled=True)  58.3 us
    unnamed x17, waiting for transfers between devices  54.3 us
    psum x1, waiting for transfers between devices, per_device(): lax.psum(piece_query.astype(jnp.bfloat16), 'rep').astype(jnp.float32)  47.5 us
    all_gather x1, waiting for transfers between devices, per_device(): lax.all_gather(up_weight, 'shard', axis=0, tiled=True)  41.8 us
    psum x1, blocking collectives, per_device(): lax.psum((grad_first_gain, grad_first_bias, grad_rates, grad_skip, grad_s...  40.5 us
  transfers between devices with their start and end apart: 15, of which 9 were waited for; matrix products, arithmetic and copies ran while one was open for 33% of the time, Pallas kernels for 0%

commit v1 on v0

--- a/solution.py
+++ b/solution.py
@@ -1,12 +1,1312 @@
+import functools
+import math
+
 import jax
 import jax.numpy as jnp
 from jax import lax
+from jax.experimental import pallas as pl
+from jax.experimental.pallas import tpu as pltpu
 from jax.sharding import PartitionSpec as P
 
 DH = 128
 BLK = 512
 CTX = 128
 NBLK = 2
+EPS = 1e-05
+NEG = -1e30
+SCALE = DH ** (-0.5)
+MESH = pl.DeviceIdType.MESH
+F32 = jnp.float32
+BF16 = jnp.bfloat16
+VMEM_LIMIT = 66_000_000
+NC = 8
+
+
+def chip_at(pos):
+    turned = pos // 4
+    return (1 - turned) * (2 * pos) + turned * (2 * (7 - pos) + 1)
+
+
+class Net:
+    def __init__(self):
+        self.rep = lax.axis_index("rep")
+        self.shard = lax.axis_index("shard")
+        self.core = self.shard % 2
+        chip = self.shard // 2
+        z, y = chip // 2, chip % 2
+        self.pos = (1 - y) * z + y * (7 - z)
+        self.step = 1 - 2 * self.core
+        self.mate = (self.rep, 2 * chip + 1 - self.core)
+        self.twin = (1 - self.rep, self.shard)
+
+    def at(self, hops, core):
+        return 2 * chip_at((self.pos + self.step * hops + 4 * NC) % NC) + core
+
+    def along(self, hops):
+        return (self.rep, self.at(hops, self.core))
+
+    def greet(self):
+        barrier = pltpu.get_barrier_semaphore()
+        for device in (self.along(1), self.along(-1), self.mate, self.twin):
+            pl.semaphore_signal(barrier, inc=1, device_id=device, device_id_type=MESH)
+        pl.semaphore_wait(barrier, 4)
+
+
+def rcopy(src, dst, send, recv, device):
+    return pltpu.make_async_remote_copy(
+        src_ref=src, dst_ref=dst, send_sem=send, recv_sem=recv, device_id=device, device_id_type=MESH
+    )
+
+
+def dot_nn(a, b):
+    return lax.dot_general(a, b, (((1,), (0,)), ((), ())), preferred_element_type=F32)
+
+
+def dot_nt(a, b):
+    return lax.dot_general(a, b, (((1,), (1,)), ((), ())), preferred_element_type=F32)
+
+
+def dot_tn(a, b):
+    return lax.dot_general(a, b, (((0,), (0,)), ((), ())), preferred_element_type=F32)
+
+
+def norm_parts(rows):
+    centred = rows - jnp.mean(rows, axis=-1, keepdims=True)
+    spread = jnp.mean(centred * centred, axis=-1, keepdims=True)
+    inverse = lax.rsqrt(spread + EPS)
+    return centred * inverse, inverse
+
+
+def split_dot(dot, left, right, narrow):
+    total = None
+    rest = left
+    for _ in range(narrow):
+        term = rest.astype(BF16)
+        part = dot(term, right)
+        total = part if total is None else total + part
+        rest = rest - term.astype(F32)
+    return total
+
+
+def lane_scan(values, factor, reverse):
+    width = values.shape[1]
+    lane = lax.broadcasted_iota(jnp.int32, values.shape, 1)
+    shift = 1
+    power = factor
+    while shift < width:
+        if reverse:
+            moved = pltpu.roll(values, width - shift, 1)
+            moved = jnp.where(lane < width - shift, moved, 0.0)
+        else:
+            moved = pltpu.roll(values, shift, 1)
+            moved = jnp.where(lane >= shift, moved, 0.0)
+        values = values + power * moved
+        power = power * power
+        shift *= 2
+    return values
+
+
+def forward_kernel(
+    tok, wq, wk, wv, wo, wup, sio, fg, fb, skip, sg, sb, decay,
+    wall, sio_all, rnd_o, q_o, k_o, v_o, att_o, res_o, sec_o, p_o, u_o, st_o,
+    tok_s, rnd_s, w_s, q_s, k_s, v_s, att_s, res_s, sec_s, pbuf, nctx, sio_s,
+    own_s, loc, rs, rr, ss, sr, cs, cr, xs, xr, outs, psem,
+):
+    net = Net()
+    rep, core = net.rep, net.core
+    rows_of = 64
+    width = 1024
+
+    def block(shard):
+        return pl.ds(pl.multiple_of(shard * rows_of, rows_of), rows_of)
+
+    mine = block(net.shard)
+    own = [wq, wk, wv, wo]
+    copies = [pltpu.make_async_copy(own[i], own_s.at[i], loc.at[i]) for i in range(4)]
+    copies += [
+        pltpu.make_async_copy(wup.at[:, pl.ds(i * width, width)], own_s.at[4 + i], loc.at[4 + i])
+        for i in range(4)
+    ]
+    small = pltpu.make_async_copy(sio, sio_all.at[mine], loc.at[8])
+    arrive = pltpu.make_async_copy(tok, tok_s, loc.at[9])
+    for copy in copies:
+        copy.start()
+    small.start()
+    arrive.start()
+    net.greet()
+    for copy in copies:
+        copy.wait()
+
+    def piece(slot):
+        if isinstance(slot, int) and slot < 2:
+            return 1 if slot else 2 * rep
+        later = slot - 2
+        return 3 + later + 3 * rep * ((later % 2) * (3 - later) // 2)
+
+    def ring(slot, way, hop, which, where):
+        ref = wall.at[which, where]
+        sems = rs.at[slot, way, hop], rr.at[slot, way, hop]
+        return rcopy(ref, ref, *sems, net.along(1 - 2 * way))
+
+    def ring_own(slot, way):
+        which = piece(slot)
+        sems = rs.at[slot, way, 0], rr.at[slot, way, 0]
+        ref = wall.at[which, mine]
+        rcopy(own_s.at[which], ref, *sems, net.along(1 - 2 * way)).start()
+
+    def ring_small(way, hop, where):
+        ref = sio_all.at[where]
+        return rcopy(ref, ref, ss.at[way, hop], sr.at[way, hop], net.along(1 - 2 * way))
+
+    def mate(which, index, where):
+        ref = wall.at[which, where]
+        return rcopy(ref, ref, cs.at[which, index], cr.at[which, index], net.mate)
+
+    def mate_small(index, where):
+        ref = sio_all.at[where]
+        return rcopy(ref, ref, cs.at[8, index], cr.at[8, index], net.mate)
+
+    def twin(turn, index, which, where):
+        ref = wall.at[which, where]
+        return rcopy(ref, ref, xs.at[turn, index], xr.at[turn, index], net.twin)
+
+    def source(way, hop):
+        return block(net.at((2 * way - 1) * (hop + 1), core))
+
+    def serve(slot, way, hop):
+        which = piece(slot)
+        where = source(way, hop)
+        ring(slot, way, hop, which, where).wait_recv()
+
+        @pl.when(hop < 3 - way)
+        def _():
+            ring(slot, way, hop + 1, which, where).start()
+
+        mate(which, 1 + 2 * hop + way, where).start()
+
+    def serve_out(slot, turn, way, hop):
+        twin(turn, 2 * hop + way, piece(slot), source(way, hop)).start()
+
+    def serve_in(turn, way, hop):
+        where = source(way, hop)
+        which = 2 * (1 - rep) if turn == 0 else 7 - 3 * rep
+        twin(turn, 2 * hop + way, which, where).wait_recv()
+        mate(which, 1 + 2 * hop + way, where).start()
+
+    for slot in range(2):
+        for way in range(2):
+            ring_own(slot, way)
+    small.wait()
+    for way in range(2):
+        ring_small(way, 0, mine).start()
+    mate_small(0, mine).start()
+    for which in range(8):
+        rcopy(own_s.at[which], wall.at[which, mine], cs.at[which, 0], cr.at[which, 0], net.mate).start()
+    keep = [pltpu.make_async_copy(own_s.at[i], wall.at[i, mine], loc.at[i]) for i in range(8)]
+    for copy in keep:
+        copy.start()
+    arrive.wait()
+
+    def first_norm(at):
+        rows = pl.ds(pl.multiple_of(at * 128, 128), 128)
+        xhat, _ = norm_parts(tok_s[rows, :].astype(F32))
+        normed = xhat * fg[...] + fb[...]
+        rnd_s[rows, :] = normed.astype(BF16)
+
+    turns = [(hop, way) for hop in range(4) for way in range(2) if hop < 4 - way]
+    for n, (hop, way) in enumerate(turns):
+        first_norm(n)
+        serve(0, way, hop)
+        serve_out(0, 0, way, hop)
+        serve(1, way, hop)
+        where = source(way, hop)
+        ring_small(way, hop, where).wait_recv()
+        if hop < 3 - way:
+            ring_small(way, hop + 1, where).start()
+        mate_small(1 + 2 * hop + way, where).start()
+        if n == 3:
+            for slot in range(2, 6):
+                for each in range(2):
+                    ring_own(slot, each)
+        if n >= 3:
+            serve_in(0, turns[n - 3][1], turns[n - 3][0])
+    first_norm(7)
+    for hop, way in turns[-3:]:
+        serve_in(0, way, hop)
+
+    def event(m):
+        hop = m // 8
+        way = (m % 8) // 4
+        slot = 2 + m % 4
+        serve(slot, way, hop)
+
+        @pl.when(slot == 3)
+        def _():
+            serve_out(3, 1, way, hop)
+
+        @pl.when((slot == 3) & (m >= 8))
+        def _():
+            serve_in(1, way, hop - 1)
+
+    xhat, _ = norm_parts(tok_s[pl.ds(BLK - CTX, CTX), :].astype(F32))
+    nctx[...] = xhat * fg[...] + fb[...]
+
+    @pl.loop(0, NC)
+    def _(index):
+        where = block(0)
+        mate_small(index, where).wait_recv()
+        for which in range(3):
+            mate(which, index, where).wait_recv()
+
+    for copy in keep:
+        copy.wait()
+    loads = [pltpu.make_async_copy(sio_all, sio_s, loc.at[8])]
+    loads += [pltpu.make_async_copy(wall.at[i], w_s.at[i], loc.at[i]) for i in range(3)]
+    for copy in loads:
+        copy.start()
+    loads[0].wait()
+    u_all = lax.dot_general(
+        sio_s[...], rnd_s[pl.ds(0, BLK), :], (((0,), (1,)), ((), ())), preferred_element_type=F32
+    )
+    factor = jnp.exp(-decay[...])
+    raw = u_all[0:16, :]
+    u_o[...] = raw
+    states = lane_scan(raw * jnp.sqrt(1.0 - factor * factor), factor, False)
+    st_o[...] = states
+    tail = states[:, BLK - CTX :]
+    padded = jnp.concatenate(
+        [jnp.zeros((16, CTX), F32), tail, jnp.zeros((96, CTX), F32)], axis=0
+    )
+    made = split_dot(
+        lambda a, b: lax.dot_general(a, b, (((0,), (1,)), ((), ())), preferred_element_type=F32),
+        padded, sio_s[...], 3,
+    )
+    rnd_s[pl.ds(1024, CTX), :] = (made + skip[...] * nctx[...]).astype(BF16)
+    finals = [pltpu.make_async_copy(rnd_s, rnd_o, outs.at[0])]
+    finals[0].start()
+
+    for copy in loads[1:]:
+        copy.wait()
+
+    @pl.loop(0, 4)
+    def _(at):
+        cols = pl.ds(pl.multiple_of(at * 256, 256), 256)
+        q_s[:, cols] = dot_nn(rnd_s[pl.ds(0, 1024), :], w_s[0, :, cols]).astype(BF16)
+        event(3 * at)
+        k_s[:, cols] = dot_nn(rnd_s[...], w_s[1, :, cols]).astype(BF16)
+        event(3 * at + 1)
+        v_s[:, cols] = dot_nn(rnd_s[...], w_s[2, :, cols]).astype(BF16)
+        event(3 * at + 2)
+
+    for i, (a, b) in enumerate(((q_s, q_o), (k_s, k_o), (v_s, v_o))):
+        finals.append(pltpu.make_async_copy(a, b, outs.at[1 + i]))
+        finals[-1].start()
+
+    for half in range(2):
+        pbuf[half] = jnp.zeros((BLK, CTX + BLK), BF16)
+
+    def p_copy(slot, at):
+        return pltpu.make_async_copy(pbuf.at[slot], p_o.at[at], psem.at[slot])
+
+    for b in range(NBLK):
+
+        @pl.loop(0, 8)
+        def _(h, b=b):
+            cols = pl.ds(pl.multiple_of(h * DH, DH), DH)
+            slot = h % 2
+            if b == 0:
+
+                @pl.when(h >= 2)
+                def _():
+                    p_copy(slot, h).wait()
+            else:
+                p_copy(slot, h).wait()
+            for i in range(2):
+                span = (i + 1) * 256
+                rows = pl.ds(b * BLK + i * 256, 256)
+                queries = q_s[rows, cols]
+                scores = dot_nt(queries, k_s[pl.ds(b * BLK, span), cols]) * SCALE
+                ahead = lax.broadcasted_iota(jnp.int32, scores.shape, 0) + i * 256
+                scores = jnp.where(
+                    ahead >= lax.broadcasted_iota(jnp.int32, scores.shape, 1), scores, NEG
+                )
+                top = jnp.max(scores, axis=-1, keepdims=True)
+                if b:
+                    before = dot_nt(queries, k_s[pl.ds(1024, CTX), cols]) * SCALE
+                    top = jnp.maximum(top, jnp.max(before, axis=-1, keepdims=True))
+                expos = jnp.exp(scores - top)
+                total = jnp.sum(expos, axis=-1, keepdims=True)
+                if b:
+                    expos_before = jnp.exp(before - top)
+                    total = total + jnp.sum(expos_before, axis=-1, keepdims=True)
+                share = 1.0 / total
+                weights = (expos * share).astype(BF16)
+                mixed = dot_nn(weights, v_s[pl.ds(b * BLK, span), cols])
+                pbuf[slot, pl.ds(i * 256, 256), pl.ds(CTX, span)] = weights
+                if b:
+                    weights = (expos_before * share).astype(BF16)
+                    mixed = mixed + dot_nn(weights, v_s[pl.ds(1024, CTX), cols])
+                    pbuf[slot, pl.ds(i * 256, 256), pl.ds(0, CTX)] = weights
+                att_s[rows, cols] = mixed.astype(BF16)
+            p_copy(slot, b * 8 + h).start()
+            event(12 + b * 8 + h)
+
+    finals.append(pltpu.make_async_copy(att_s, att_o, outs.at[4]))
+    finals[-1].start()
+
+    @pl.loop(0, NC)
+    def _(index):
+        mate(3, index, block(0)).wait_recv()
+
+    load = pltpu.make_async_copy(wall.at[3], w_s.at[3], loc.at[3])
+    load.start()
+    load.wait()
+
+    @pl.loop(0, 4)
+    def _(at):
+        rows = pl.ds(pl.multiple_of(at * 256, 256), 256)
+        residual = tok_s[rows, :].astype(F32) + dot_nn(att_s[rows, :], w_s[3])
+        res_s[rows, :] = residual
+        xhat, _ = norm_parts(residual)
+        sec_s[rows, :] = (xhat * sg[...] + sb[...]).astype(BF16)
+        pltpu.make_async_copy(res_s.at[rows], res_o.at[rows], outs.at[5 + at]).start()
+        pltpu.make_async_copy(sec_s.at[rows], sec_o.at[rows], outs.at[9 + at]).start()
+
+    for copy in finals:
+        copy.wait()
+    for at in range(4):
+        rows = pl.ds(at * 256, 256)
+        pltpu.make_async_copy(res_s.at[rows], res_o.at[rows], outs.at[5 + at]).wait()
+        pltpu.make_async_copy(sec_s.at[rows], sec_o.at[rows], outs.at[9 + at]).wait()
+    for slot in range(2):
+        p_copy(slot, slot).wait()
+
+    serve_in(1, 1, 2)
+    serve_in(1, 0, 3)
+
+    @pl.loop(0, NC)
+    def _(index):
+        for which in range(4, 8):
+            mate(which, index, block(0)).wait_recv()
+        for which in range(8):
+            mate(which, index, block(0)).wait_send()
+        mate_small(index, block(0)).wait_send()
+
+    @pl.loop(0, NC - 1)
+    def _(index):
+        hop = index // 2
+        way = index % 2
+        for slot in range(6):
+            ring(slot, way, hop, 0, block(0)).wait_send()
+        ring_small(way, hop, block(0)).wait_send()
+        for turn in range(2):
+            twin(turn, index, 0, block(0)).wait_send()
+
+
+def any_spec(n):
+    return [pl.BlockSpec(memory_space=pl.ANY)] * n
+
+
+def vmem_spec(n):
+    return [pl.BlockSpec(memory_space=pltpu.VMEM)] * n
+
+
+def run_forward(tok, wq, wk, wv, wo, wup, sio, fg, fb, skip, sg, sb, decay):
+    shape = jax.ShapeDtypeStruct
+    dma = pltpu.SemaphoreType.DMA
+    big = (1024, 1024)
+    ext = (1024 + CTX, 1024)
+    return pl.pallas_call(
+        forward_kernel,
+        name="forward_part",
+        out_shape=(
+            shape((8,) + big, BF16), shape((1024, 128), BF16), shape(ext, BF16), shape(big, BF16),
+            shape(ext, BF16), shape(ext, BF16), shape(big, BF16), shape(big, F32),
+            shape(big, BF16), shape((16, BLK, CTX + BLK), BF16), shape((16, BLK), F32),
+            shape((16, BLK), F32),
+        ),
+        in_specs=any_spec(7) + vmem_spec(6),
+        out_specs=any_spec(10) + vmem_spec(2),
+        scratch_shapes=[
+            pltpu.VMEM(big, BF16), pltpu.VMEM(ext, BF16), pltpu.VMEM((4,) + big, BF16),
+            pltpu.VMEM(big, BF16), pltpu.VMEM(ext, BF16), pltpu.VMEM(ext, BF16),
+            pltpu.VMEM(big, BF16), pltpu.VMEM(big, F32), pltpu.VMEM(big, BF16),
+            pltpu.VMEM((2, BLK, CTX + BLK), BF16), pltpu.VMEM((CTX, 1024), F32),
+            pltpu.VMEM((1024, 128), BF16),
+            pltpu.VMEM((8, 64, 1024), BF16),
+            dma((10,)), dma((6, 2, 4)), dma((6, 2, 4)), dma((2, 4)), dma((2, 4)),
+            dma((9, NC)), dma((9, NC)), dma((2, NC - 1)), dma((2, NC - 1)), dma((13,)), dma((2,)),
+        ],
+        compiler_params=pltpu.CompilerParams(
+            collective_id=0, has_side_effects=True, vmem_limit_bytes=VMEM_LIMIT
+        ),
+    )(tok, wq, wk, wv, wo, wup, sio, fg, fb, skip, sg, sb, decay)
+
+
+GELU_C = math.sqrt(2.0 / math.pi)
+GELU_A = 0.044715
+
+
+def feed_kernel(
+    sec, res, wall, wdn, cot, live, upb, dnb, sg,
+    out_o, gatt_o, dwup_o, piece_o, gdb_o, gub_o, gsg_o, gsb_o,
+    sec_s, gb_s, wup_s, wd_s, br_s, gs_s, act_s, gh_s, a_s, b_s, prec, rrec, rsend, xsend, xrec,
+    xfs, xfr, dwup_s, own_s, res_s,
+    loc, ars, arr, axs, axr, cas, car, cxs, cxr, ps, pr, rs, rr, xs, xr, fs, fr, outs, dsem,
+):
+    net = Net()
+    rep, core = net.rep, net.core
+    rows_of = 256
+    ring_rows = 192
+    part = 64
+    ahead, behind = net.along(1), net.along(-1)
+
+    def ring_part(shard, size=ring_rows, first=rep * part):
+        return pl.ds(pl.multiple_of(shard * rows_of + first, part), size)
+
+    def sole_part(shard, of):
+        return pl.ds(pl.multiple_of(shard * rows_of + 3 * of * part, part), part)
+
+    def block(shard):
+        return pl.ds(pl.multiple_of(shard * rows_of, rows_of), rows_of)
+
+    def mine_at(step):
+        return net.at(-(step + 1), core)
+
+    def other_at(step):
+        return net.at(step + 1, 1 - core)
+
+    loads = [
+        pltpu.make_async_copy(wdn, own_s, loc.at[0]),
+        pltpu.make_async_copy(sec, sec_s, loc.at[1]),
+        pltpu.make_async_copy(cot, gb_s, loc.at[2]),
+    ]
+    loads += [pltpu.make_async_copy(wall.at[4 + i], wup_s.at[i], loc.at[3 + i]) for i in range(4)]
+    for load in loads:
+        load.start()
+    net.greet()
+    loads[0].wait()
+
+    def gather(hop, shard):
+        ref = wd_s.at[ring_part(shard)]
+        return rcopy(ref, ref, ars.at[hop], arr.at[hop], ahead)
+
+    def gather_twin(hop, shard, of):
+        ref = wd_s.at[sole_part(shard, of)]
+        return rcopy(ref, ref, axs.at[hop], axr.at[hop], net.twin)
+
+    def mate_ring(index, shard, first):
+        ref = wd_s.at[ring_part(shard, ring_rows, first)]
+        return rcopy(ref, ref, cas.at[index], car.at[index], net.mate)
+
+    def mate_sole(index, shard, of):
+        ref = wd_s.at[sole_part(shard, of)]
+        return rcopy(ref, ref, cxs.at[index], cxr.at[index], net.mate)
+
+    here = net.shard
+    ring_own = own_s.at[pl.ds(pl.multiple_of(rep * part, part), ring_rows)]
+    sole_own = own_s.at[pl.ds(pl.multiple_of(3 * (1 - rep) * part, part), part)]
+    rcopy(ring_own, wd_s.at[ring_part(here)], ars.at[0], arr.at[0], ahead).start()
+    rcopy(ring_own, wd_s.at[ring_part(here)], cas.at[0], car.at[0], net.mate).start()
+    rcopy(sole_own, wd_s.at[sole_part(here, 1 - rep)], cxs.at[0], cxr.at[0], net.mate).start()
+
+    def serve(hop):
+        shard = mine_at(hop)
+        gather(hop, shard).wait_recv()
+
+        @pl.when(hop < NC - 2)
+        def _():
+            gather(hop + 1, shard).start()
+
+        gather_twin(hop, shard, rep).start()
+        mate_ring(hop + 1, shard, rep * part).start()
+
+    def serve_twin(hop):
+        shard = mine_at(hop)
+        gather_twin(hop, shard, 1 - rep).wait_recv()
+        mate_sole(hop + 1, shard, 1 - rep).start()
+
+    for load in loads[1:3]:
+        load.wait()
+
+    wd_s[block(here), :] = own_s[...]
+
+    @pl.loop(0, 4)
+    def _(at):
+        rows = pl.ds(pl.multiple_of(at * 256, 256), 256)
+        when = lax.broadcasted_iota(jnp.int32, (256, 1024), 0) + at * 256
+        kept = jnp.where(when < live[...], gb_s[rows, :].astype(F32), 0.0)
+        gb_s[rows, :] = kept.astype(BF16)
+        added = jnp.sum(kept, axis=0, keepdims=True)
+        gdb_o[...] = jnp.where(at == 0, added, gdb_o[...] + added)
+        br_s[rows, :] = jnp.zeros((256, 1024), F32)
+        gs_s[rows, :] = jnp.zeros((256, 1024), F32)
+
+    serve(0)
+    for load in loads[3:]:
+        load.wait()
+    serve_twin(0)
+
+    def to_mate(step):
+        slot = step % 2
+        return rcopy(b_s.at[slot], prec.at[step], ps.at[step], pr.at[step], net.mate)
+
+    def to_ring(step):
+        return rcopy(rsend.at[step % 2], rrec.at[step], rs.at[step], rr.at[step], ahead)
+
+    def to_twin(step):
+        return rcopy(xsend.at[step % 2], xrec.at[step], xs.at[step], xr.at[step], net.twin)
+
+    def dwup_copy(slot, half, shard):
+        cols = pl.ds(pl.multiple_of((shard % 4) * 256, 256), 256)
+        return pltpu.make_async_copy(
+            dwup_s.at[slot, half], dwup_o.at[shard // 4, :, cols], dsem.at[slot, half]
+        )
+
+    ring_local = pl.ds(pl.multiple_of(rep * part, part), ring_rows)
+    sole_mine = pl.ds(pl.multiple_of(3 * rep * part, part), part)
+    sole_theirs = pl.ds(pl.multiple_of(3 * (1 - rep) * part, part), part)
+
+    def combine(step):
+        slot = step % 2
+        to_mate(step).wait_recv()
+        a_s[slot] = a_s[slot] + prec[step].astype(F32)
+
+        @pl.when(step >= 2)
+        def _():
+            to_twin(step - 2).wait_send()
+
+        xsend[slot] = a_s[slot, sole_theirs, :].astype(BF16)
+        to_twin(step).start()
+
+    def forward(step):
+        slot = step % 2
+        to_twin(step).wait_recv()
+        a_s[slot, sole_mine, :] = a_s[slot, sole_mine, :] + xrec[step].astype(F32)
+
+        @pl.when(step >= 1)
+        def _():
+            to_ring(step - 1).wait_recv()
+            a_s[slot, ring_local, :] = a_s[slot, ring_local, :] + rrec[step - 1].astype(F32)
+
+        @pl.when((step >= 2) & (step < NC - 1))
+        def _():
+            to_ring(step - 2).wait_send()
+
+        @pl.when(step < NC - 1)
+        def _():
+            rsend[slot] = a_s[slot, ring_local, :].astype(BF16)
+            to_ring(step).start()
+
+    @pl.loop(0, NC)
+    def _(step):
+        slot = step % 2
+        a, b = mine_at(step), other_at(step)
+        index = (step + 1) % NC
+        mate_ring(index, b, rep * part).wait_recv()
+        mate_sole(index, b, 1 - rep).wait_recv()
+
+        @pl.when(step < NC - 2)
+        def _():
+            serve(step + 1)
+
+        def up(shard):
+            cols = pl.ds(pl.multiple_of((shard % 4) * 256, 256), 256)
+            return wup_s[shard // 4, :, cols]
+
+        def bias(shard):
+            return upb[:, pl.ds(pl.multiple_of(shard * 256, 256), 256)]
+
+        @pl.loop(0, 4)
+        def _(at):
+            rows = pl.ds(pl.multiple_of(at * 256, 256), 256)
+            for half, shard in enumerate((a, b)):
+                cols = pl.ds(half * 256, 256)
+                hidden = dot_nn(sec_s[rows, :], up(shard)) + bias(shard)
+                grad = dot_nt(gb_s[rows, :], wd_s[block(shard), :])
+                square = hidden * hidden
+                bent = jnp.tanh(hidden * (GELU_C + (GELU_C * GELU_A) * square))
+                half_up = 0.5 + 0.5 * bent
+                act_s[rows, cols] = (hidden * half_up).astype(BF16)
+                slope = half_up + (0.5 * hidden) * (1.0 - bent * bent) * (
+                    GELU_C + (3.0 * GELU_C * GELU_A) * square
+                )
+                gh_s[rows, cols] = (grad * slope).astype(BF16)
+
+        @pl.when(step < NC - 2)
+        def _():
+            serve_twin(step + 1)
+
+        @pl.when(step >= 1)
+        def _():
+            combine(step - 1)
+
+        made = dot_tn(act_s[...], gb_s[...])
+
+        @pl.when(step >= 2)
+        def _():
+            to_mate(step - 2).wait_send()
+
+        a_s[slot] = made[0:256]
+        b_s[slot] = made[256:512].astype(BF16)
+        to_mate(step).start()
+
+        for half, shard in enumerate((a, b)):
+            cols = pl.ds(pl.multiple_of(shard * 256, 256), 256)
+            gub_o[:, cols] = jnp.sum(
+                gh_s[:, half * 256 : half * 256 + 256].astype(F32), axis=0, keepdims=True
+            )
+
+            @pl.when(step >= 2)
+            def _(half=half, shard=shard):
+                dwup_copy(slot, half, shard).wait()
+
+            dwup_s[slot, half] = dot_tn(sec_s[...], gh_s[:, half * 256 : half * 256 + 256]).astype(BF16)
+            dwup_copy(slot, half, shard).start()
+
+        @pl.when(step >= 1)
+        def _():
+            forward(step - 1)
+
+        @pl.loop(0, 4)
+        def _(at):
+            rows = pl.ds(pl.multiple_of(at * 256, 256), 256)
+            down = jnp.concatenate([wd_s[block(a), :], wd_s[block(b), :]], axis=0)
+            br_s[rows, :] = br_s[rows, :] + dot_nn(act_s[rows, :], down)
+            rise = jnp.concatenate([up(a), up(b)], axis=1)
+            gs_s[rows, :] = gs_s[rows, :] + dot_nt(gh_s[rows, :], rise)
+
+    def residual_in(at):
+        rows = pl.ds(at * 256, 256)
+        return pltpu.make_async_copy(res.at[rows], res_s.at[rows], loc.at[at])
+
+    for at in range(4):
+        residual_in(at).start()
+    combine(NC - 1)
+
+    def leave(at, which):
+        rows = pl.ds(pl.multiple_of(at * 256, 256), 256)
+        source = (sec_s, gb_s)[which]
+        return pltpu.make_async_copy(
+            source.at[rows], (out_o, gatt_o)[which].at[rows], outs.at[which, at]
+        )
+
+    @pl.loop(0, 4)
+    def _(at):
+        residual_in(at).wait()
+        rows = pl.ds(pl.multiple_of(at * 256, 256), 256)
+        kept = res_s[rows, :]
+        when = lax.broadcasted_iota(jnp.int32, (256, 1024), 0) + at * 256
+        total = kept + br_s[rows, :] + dnb[...]
+        sec_s[rows, :] = jnp.where(when < live[...], total, 0.0).astype(BF16)
+        xhat, inverse = norm_parts(kept)
+        grad = gs_s[rows, :]
+        gain = jnp.sum(grad * xhat, axis=0, keepdims=True)
+        shift = jnp.sum(grad, axis=0, keepdims=True)
+        gsg_o[...] = jnp.where(at == 0, gain, gsg_o[...] + gain)
+        gsb_o[...] = jnp.where(at == 0, shift, gsb_o[...] + shift)
+        grad = grad * sg[...]
+        grad = grad - jnp.mean(grad, axis=-1, keepdims=True) - xhat * jnp.mean(
+            grad * xhat, axis=-1, keepdims=True
+        )
+        gb_s[rows, :] = (gb_s[rows, :].astype(F32) + inverse * grad).astype(BF16)
+        for which in range(2):
+            leave(at, which).start()
+
+    forward(NC - 1)
+    last = (NC - 1) % 2
+    xfs[...] = a_s[last, ring_local, :].astype(BF16)
+    swap = rcopy(xfs, xfr, fs.at[0], fr.at[0], net.twin)
+    swap.start()
+
+    @pl.loop(0, NC - 1)
+    def _(hop):
+        gather(hop, 0).wait_send()
+        gather_twin(hop, 0, 0).wait_send()
+
+    @pl.loop(0, NC)
+    def _(index):
+        mate_ring(index, 0, 0).wait_send()
+        mate_sole(index, 0, 0).wait_send()
+
+    for step in range(NC - 2, NC):
+        to_mate(step).wait_send()
+        to_twin(step).wait_send()
+        to_ring(step - 1).wait_send()
+        for half in range(2):
+            dwup_copy(step % 2, half, 0).wait()
+    for at in range(4):
+        for which in range(2):
+            leave(at, which).wait()
+    swap.wait()
+    theirs = pl.ds(pl.multiple_of((1 - rep) * part, part), ring_rows)
+    piece_o[...] = jnp.zeros((rows_of, 1024), F32)
+    piece_o[ring_local, :] = xfs[...].astype(F32)
+    piece_o[theirs, :] = piece_o[theirs, :] + xfr[...].astype(F32)
+
+
+def run_feed(sec, res, wall, wdn, cot, live, upb, dnb, sg):
+    shape = jax.ShapeDtypeStruct
+    dma = pltpu.SemaphoreType.DMA
+    vmem = pltpu.VMEM
+    big = (1024, 1024)
+    return pl.pallas_call(
+        feed_kernel,
+        name="feed_part",
+        out_shape=(
+            shape(big, BF16), shape(big, BF16), shape((4,) + big, BF16),
+            shape((256, 1024), F32), shape((1, 1024), F32), shape((1, 4096), F32),
+            shape((1, 1024), F32), shape((1, 1024), F32),
+        ),
+        in_specs=any_spec(5) + vmem_spec(4),
+        out_specs=any_spec(3) + vmem_spec(5),
+        scratch_shapes=[
+            vmem(big, BF16), vmem(big, BF16), vmem((4,) + big, BF16), vmem((4096, 1024), BF16),
+            vmem(big, F32), vmem(big, F32), vmem((1024, 512), BF16), vmem((1024, 512), BF16),
+            vmem((2, 256, 1024), F32), vmem((2, 256, 1024), BF16), vmem((NC, 256, 1024), BF16),
+            vmem((NC - 1, 192, 1024), BF16), vmem((2, 192, 1024), BF16), vmem((2, 64, 1024), BF16),
+            vmem((NC, 64, 1024), BF16), vmem((192, 1024), BF16), vmem((192, 1024), BF16),
+            vmem((2, 2, 1024, 256), BF16), vmem((256, 1024), BF16), vmem(big, F32),
+            dma((7,)), dma((NC - 1,)), dma((NC - 1,)), dma((NC - 1,)), dma((NC - 1,)),
+            dma((NC,)), dma((NC,)), dma((NC,)), dma((NC,)), dma((NC,)), dma((NC,)),
+            dma((NC - 1,)), dma((NC - 1,)), dma((NC,)), dma((NC,)), dma((1,)), dma((1,)),
+            dma((2, 4)), dma((2, 2)),
+        ],
+        compiler_params=pltpu.CompilerParams(
+            collective_id=1, has_side_effects=True, vmem_limit_bytes=VMEM_LIMIT
+        ),
+    )(sec, res, wall, wdn, cot, live, upb, dnb, sg)
+
+
+def backward_kernel(
+    dwup, gatt, att, wall, q, kx, vx, rnd, p, tok, sio, u_in, st_in, fg, fb, skip, decay,
+    gtok_o, dup_o, do_o, dq_o, dk_o, dv_o, gfg_o, gfb_o, gskip_o, gsi_o, gso_o, grate_o,
+    own_b, prec_b, rrec_b, xrec_b, fin_b, finr_b, acc_b,
+    own_g, prec_g, rrec_g, xrec_g, fin_g, finr_g, acc_g, go_s,
+    gatt_s, wo_s, att_s, ga_s, q_s, k_s, v_s, rnd_s, dk_s, dv_s, pbuf, ds_s, gres_s, nb_s,
+    sio_s, gd_s, gctx_s,
+    loc, psem, gsem, osem, mbs, mbr, mgs, mgr, rbs, rbr, rgs, rgr, xbs, xbr, xgs, xgr,
+    fbs, fbr, fgs, fgr,
+):
+    net = Net()
+    rep, core = net.rep, net.core
+    theirs = 1 - core
+
+    loads = [
+        pltpu.make_async_copy(gatt, gatt_s, loc.at[0]),
+        pltpu.make_async_copy(wall.at[3], wo_s, loc.at[1]),
+        pltpu.make_async_copy(att, att_s, loc.at[2]),
+        pltpu.make_async_copy(q, q_s, loc.at[3]),
+        pltpu.make_async_copy(kx, k_s, loc.at[4]),
+        pltpu.make_async_copy(vx, v_s, loc.at[5]),
+        pltpu.make_async_copy(rnd, rnd_s, loc.at[6]),
+        pltpu.make_async_copy(sio, sio_s, loc.at[7]),
+    ]
+    rises = [pltpu.make_async_copy(dwup.at[i, :, core], own_b.at[i], loc.at[8 + i]) for i in range(4)]
+    for copy in rises:
+        copy.start()
+    for copy in loads:
+        copy.start()
+    fin_b[...] = jnp.zeros(fin_b.shape, BF16)
+    finr_b[...] = jnp.zeros(finr_b.shape, BF16)
+    fin_g[...] = jnp.zeros(fin_g.shape, BF16)
+    finr_g[...] = jnp.zeros(finr_g.shape, BF16)
+    net.greet()
+
+    def mate_big(which, source):
+        return rcopy(source, prec_b.at[which], mbs.at[which], mbr.at[which], net.mate)
+
+    def mate_group(g):
+        return rcopy(own_g.at[g, :, theirs], prec_g.at[g], mgs.at[g], mgr.at[g], net.mate)
+
+    for i in (0, 3, 1, 2):
+        mate_big(i, dwup.at[i, :, theirs]).start()
+
+    def chip_for(n):
+        t, way = n // 2, n % 2
+        hops = (4 - t) * (1 - way) + (t - 3) * way
+        return chip_at((net.pos + net.step * hops + 4 * NC) % NC)
+
+    class Stream:
+        def __init__(self, own, prec, rrec, xrec, fin, finr, acc, sems):
+            self.own, self.prec, self.rrec, self.xrec = own, prec, rrec, xrec
+            self.fin, self.finr, self.acc = fin, finr, acc
+            self.rs, self.rr, self.xs, self.xr, self.fs, self.fr = sems
+
+        def ring(self, slot, which, n):
+            source = self.prec.at[which, chip_for(n)]
+            way = n % 2
+            return rcopy(
+                source, self.rrec.at[slot, n], self.rs.at[slot, n], self.rr.at[slot, n],
+                net.along(1 - 2 * way),
+            )
+
+        def twin(self, which, n):
+            chip = chip_for(n)
+            return rcopy(
+                self.prec.at[which, chip], self.xrec.at[chip], self.xs.at[n], self.xr.at[n], net.twin
+            )
+
+        def finish(self, which):
+            return rcopy(
+                self.fin.at[which], self.finr.at[which], self.fs.at[which], self.fr.at[which], net.twin
+            )
+
+        def give(self, which, n):
+            chip = chip_for(n)
+            self.prec[which, chip] = (
+                self.own(which, chip).astype(F32) + self.prec[which, chip].astype(F32)
+            ).astype(BF16)
+            self.twin(which, n).start()
+
+        def turn(self, slot, which, n, sole):
+            chip = chip_for(n)
+            self.acc[...] = self.own(which, chip).astype(F32) + self.prec[which, chip].astype(F32)
+
+            @pl.when(sole)
+            def _():
+                self.twin(which, n).wait_recv()
+                self.acc[...] = self.acc[...] + self.xrec[chip].astype(F32)
+
+            @pl.when((n >= 2) & (n < 7))
+            def _():
+                self.ring(slot, which, n - 2).wait_recv()
+                self.acc[...] = self.acc[...] + self.rrec[slot, n - 2].astype(F32)
+
+            @pl.when(n < 7)
+            def _():
+                self.prec[which, chip] = self.acc[...].astype(BF16)
+                self.ring(slot, which, n).start()
+
+            @pl.when(n == 7)
+            def _():
+                self.ring(slot, which, 5).wait_recv()
+                self.ring(slot, which, 6).wait_recv()
+                total = self.acc[...] + self.rrec[slot, 5].astype(F32) + self.rrec[slot, 6].astype(F32)
+                self.fin[which] = total.astype(BF16)
+                self.finish(which).start()
+
+    big = Stream(
+        lambda which, chip: go_s[chip, core] if isinstance(which, int) and which == 4 else own_b[which, chip],
+        prec_b, rrec_b, xrec_b, fin_b, finr_b, acc_b,
+        (rbs, rbr, xbs, xbr, fbs, fbr),
+    )
+    group = Stream(
+        lambda which, chip: own_g[which, chip, core], prec_g, rrec_g, xrec_g, fin_g, finr_g, acc_g,
+        (rgs, rgr, xgs, xgr, fgs, fgr),
+    )
+
+    def rise(j):
+        return j + 3 * rep * ((2 - j) // 2)
+
+    for i in range(2):
+        loads[i].wait()
+
+    def p_copy(slot, at):
+        return pltpu.make_async_copy(p.at[at], pbuf.at[slot], psem.at[slot])
+
+    p_copy(0, 0).start()
+
+    @pl.loop(0, 4)
+    def _(at):
+        rows = pl.ds(pl.multiple_of(at * 256, 256), 256)
+        ga_s[rows, :] = dot_nt(gatt_s[rows, :], wo_s[...]).astype(BF16)
+
+    for copy in rises:
+        copy.wait()
+    for i in range(4):
+        mate_big(i, dwup.at[i, :, theirs]).wait_recv()
+
+    @pl.loop(0, NC)
+    def _(n):
+        big.give(3 * (1 - rep), n)
+
+    for n in range(2):
+        for j in (1, 2, 0):
+            big.turn(j, rise(j), n, j == 0)
+    loads[2].wait()
+
+    @pl.loop(0, 4)
+    def _(at):
+        cols = pl.ds(pl.multiple_of(at * 256, 256), 256)
+        made = dot_tn(att_s[...], gatt_s[:, cols]).astype(BF16)
+        go_s[:, :, :, cols] = made.reshape(NC, 2, 64, 256)
+
+    mate_big(4, go_s.at[:, theirs]).start()
+    tok_load = pltpu.make_async_copy(tok, wo_s, loc.at[0])
+    tok_load.start()
+    for copy in loads[3:]:
+        copy.wait()
+    ds_s[...] = jnp.zeros(ds_s.shape, BF16)
+    dq_s = gatt_s
+
+    def weights_in(i):
+        target = (q_s, k_s.at[pl.ds(0, 1024)], v_s.at[pl.ds(0, 1024)])[i]
+        return pltpu.make_async_copy(wall.at[i], target, loc.at[1 + i])
+
+    @pl.loop(0, 4)
+    def _(g):
+        for hh in range(2):
+            for b in range(NBLK):
+                i = 2 * hh + b
+                m = 4 * g + i
+                h = 2 * g + hh
+                slot = i % 2
+                cols = pl.ds(pl.multiple_of(h * DH, DH), DH)
+                following = 2 * hh + b + 1
+                nb, nh = following % 2, 2 * g + following // 2
+                p_copy(slot, b * 8 + h).wait()
+                if following < 4:
+                    p_copy(1 - slot, nb * 8 + nh).start()
+                else:
+
+                    @pl.when(g < 3)
+                    def _():
+                        p_copy(1 - slot, nh).start()
+
+                for part in range(2):
+                    span = (part + 1) * 256
+                    rows = pl.ds(b * BLK + part * 256, 256)
+                    local = pl.ds(part * 256, 256)
+                    grads = ga_s[rows, cols]
+                    slope = dot_nt(grads, v_s[pl.ds(b * BLK, span), cols])
+                    kept = pbuf[slot, local, pl.ds(CTX, span)].astype(F32)
+                    both = jnp.sum(kept * slope, axis=-1, keepdims=True)
+                    mass = jnp.sum(kept, axis=-1, keepdims=True)
+                    if b:
+                        slope_before = dot_nt(grads, v_s[pl.ds(1024, CTX), cols])
+                        kept_before = pbuf[slot, local, pl.ds(0, CTX)].astype(F32)
+                        both += jnp.sum(kept_before * slope_before, axis=-1, keepdims=True)
+                        mass += jnp.sum(kept_before, axis=-1, keepdims=True)
+                    both = both / mass
+                    inner = (kept * (slope - both)).astype(BF16)
+                    ds_s[local, pl.ds(CTX, span)] = inner
+                    total = dot_nn(inner, k_s[pl.ds(b * BLK, span), cols])
+                    if b:
+                        inner = (kept_before * (slope_before - both)).astype(BF16)
+                        ds_s[local, pl.ds(0, CTX)] = inner
+                        total = total + dot_nn(inner, k_s[pl.ds(1024, CTX), cols])
+                    dq_s[rows, cols] = (total * SCALE).astype(BF16)
+                rows = pl.ds(b * BLK, BLK)
+                first = 0 if b else CTX
+                made_k = dot_tn(ds_s[:, first:], q_s[rows, cols]) * SCALE
+                made_v = dot_tn(pbuf[slot, :, first:], ga_s[rows, cols])
+                if b:
+                    dk_s[pl.ds(1024, CTX), cols] = made_k[:CTX].astype(BF16)
+                    dv_s[pl.ds(1024, CTX), cols] = made_v[:CTX].astype(BF16)
+                    made_k, made_v = made_k[CTX:], made_v[CTX:]
+                dk_s[rows, cols] = made_k.astype(BF16)
+                dv_s[rows, cols] = made_v.astype(BF16)
+
+                @pl.when(m < 9)
+                def _(m=m):
+                    for e in range(2):
+                        at = 2 * m + e
+                        j = at % 3
+                        big.turn(j, rise(j), 2 + at // 3, j == 0)
+
+                @pl.when(m == 4)
+                def _():
+                    mate_big(4, go_s.at[:, theirs]).wait_recv()
+
+                @pl.when((m >= 4) & (m < 12))
+                def _(m=m):
+                    big.turn(3, 4, m - 4, False)
+
+                @pl.when(m == 9)
+                def _():
+                    for each in range(2):
+                        mate_group(each).wait_recv()
+
+                @pl.when((m >= 9) & (m < 13))
+                def _(m=m):
+                    for e in range(2):
+                        group.give(1 - rep, 2 * (m - 9) + e)
+
+                @pl.when(m >= 12)
+                def _(m=m):
+                    for e in range(2):
+                        group.turn(0, rep, 2 * (m - 12) + e, True)
+
+        @pl.when(g == 3)
+        def _():
+            for i in range(3):
+                weights_in(i).start()
+
+        cols = pl.ds(pl.multiple_of(g * 256, 256), 256)
+        own_g[g, :, :, :, 0:256] = dot_tn(rnd_s[0:1024, :], dq_s[:, cols]).astype(BF16).reshape(NC, 2, 64, 256)
+        own_g[g, :, :, :, 256:512] = dot_tn(rnd_s[...], dk_s[:, cols]).astype(BF16).reshape(NC, 2, 64, 256)
+        own_g[g, :, :, :, 512:768] = dot_tn(rnd_s[...], dv_s[:, cols]).astype(BF16).reshape(NC, 2, 64, 256)
+        mate_group(g).start()
+
+    mate_group(2).wait_recv()
+    for n in range(2):
+        group.turn(1, 2, n, False)
+    for i in range(3):
+        weights_in(i).wait()
+    tok_load.wait()
+
+    def gres_in(at):
+        rows = pl.ds(pl.multiple_of(at * 256, 256), 256)
+        return pltpu.make_async_copy(gatt.at[rows], gres_s.at[at % 2], gsem.at[at % 2])
+
+    gres_in(0).start()
+
+    after = pl.ds(1024, CTX)
+    gctx = dot_nt(dk_s[after, :], k_s[0:1024, :]) + dot_nt(dv_s[after, :], v_s[0:1024, :])
+    gctx_s[...] = gctx
+    xhat, _ = norm_parts(wo_s[pl.ds(BLK - CTX, CTX), :].astype(F32))
+    gskip_o[...] = jnp.sum(gctx * (xhat * fg[...] + fb[...]), axis=0, keepdims=True)
+    mate_group(3).wait_recv()
+    for n in range(2):
+        group.turn(2, 3, n, False)
+    states, raw = st_in[...], u_in[...]
+    factor = jnp.exp(-decay[...])
+    scale = jnp.sqrt(1.0 - factor * factor)
+    gso_o[...] = lax.dot_general(
+        states[:, BLK - CTX :], gctx, (((1,), (0,)), ((), ())),
+        preferred_element_type=F32, precision=lax.Precision.HIGHEST,
+    )
+    back = split_dot(
+        lambda a, b: lax.dot_general(b, a, (((0,), (1,)), ((), ())), preferred_element_type=F32),
+        gctx, sio_s[...], 3,
+    )
+    seeds = jnp.concatenate([jnp.zeros((16, BLK - CTX), F32), back[16:32, :]], axis=1)
+    lam = lane_scan(seeds, factor, True)
+    lane = lax.broadcasted_iota(jnp.int32, lam.shape, 1)
+    earlier = jnp.where(lane >= 1, pltpu.roll(states, 1, 1), 0.0)
+    rates = -factor * jnp.sum(lam * (earlier - (factor / scale) * raw), axis=1, keepdims=True)
+    grate_o[...] = jnp.broadcast_to(rates, grate_o.shape)
+    driven = scale * lam
+    gsi_o[...] = split_dot(dot_nn, driven, rnd_s[0:BLK, :], 3)
+    gd_s[...] = jnp.zeros(gd_s.shape, F32)
+    gd_s[0:16, 0:BLK] = driven
+
+    def leave(at):
+        rows = pl.ds(pl.multiple_of(at * 256, 256), 256)
+        return pltpu.make_async_copy(rnd_s.at[rows], gtok_o.at[rows], osem.at[at])
+
+    @pl.loop(0, 4)
+    def _(at):
+        rows = pl.ds(pl.multiple_of(at * 256, 256), 256)
+
+        @pl.when(at < 3)
+        def _():
+            gres_in(at + 1).start()
+
+        nb_s[...] = (
+            dot_nt(dq_s[rows, :], q_s[...])
+            + dot_nt(dk_s[rows, :], k_s[0:1024, :])
+            + dot_nt(dv_s[rows, :], v_s[0:1024, :])
+            + split_dot(
+                lambda a, b: lax.dot_general(a, b, (((0,), (1,)), ((), ())), preferred_element_type=F32),
+                gd_s[:, rows], sio_s[...], 3,
+            )
+        )
+
+        @pl.when(at == 1)
+        def _():
+            half = pl.ds(128, CTX)
+            nb_s[half, :] = nb_s[half, :] + skip[...] * gctx_s[...]
+
+        @pl.when(at < 3)
+        def _():
+            for e in range(2):
+                group.turn(1, 2, 2 + 2 * at + e, False)
+                group.turn(2, 3, 2 + 2 * at + e, False)
+
+        xhat, inverse = norm_parts(wo_s[rows, :].astype(F32))
+        grad = nb_s[...]
+        gain = jnp.sum(grad * xhat, axis=0, keepdims=True)
+        shift = jnp.sum(grad, axis=0, keepdims=True)
+        gfg_o[...] = jnp.where(at == 0, gain, gfg_o[...] + gain)
+        gfb_o[...] = jnp.where(at == 0, shift, gfb_o[...] + shift)
+        grad = grad * fg[...]
+        grad = grad - jnp.mean(grad, axis=-1, keepdims=True) - xhat * jnp.mean(
+            grad * xhat, axis=-1, keepdims=True
+        )
+        gres_in(at).wait()
+        rnd_s[rows, :] = (gres_s[at % 2].astype(F32) + inverse * grad).astype(BF16)
+        leave(at).start()
+
+    for j in range(3):
+        big.finish(rise(j)).wait_send()
+    big.finish(4).wait_send()
+    for which in (rep, 2, 3):
+        group.finish(which).wait_send()
+    twin_rise = 3 * (1 - rep)
+    for which in (twin_rise, 1, 2, 4):
+        big.finish(which).wait_recv()
+    for which in (1 - rep, 2, 3):
+        group.finish(which).wait_recv()
+    for i in range(4):
+        dup_o[:, i * 1024 : (i + 1) * 1024] = fin_b[i].astype(F32) + finr_b[i].astype(F32)
+    do_o[...] = fin_b[4].astype(F32) + finr_b[4].astype(F32)
+    for g in range(4):
+        for i, out in enumerate((dq_o, dk_o, dv_o)):
+            cols = slice(i * 256, (i + 1) * 256)
+            out[:, g * 256 : (g + 1) * 256] = fin_g[g, :, cols].astype(F32) + finr_g[g, :, cols].astype(F32)
+
+    for i in range(4):
+        mate_big(i, dwup.at[i, :, theirs]).wait_send()
+        mate_group(i).wait_send()
+        leave(i).wait()
+    mate_big(4, go_s.at[:, theirs]).wait_send()
+
+    @pl.loop(0, NC)
+    def _(n):
+        big.twin(3 * (1 - rep), n).wait_send()
+        group.twin(1 - rep, n).wait_send()
+
+    @pl.loop(0, NC - 1)
+    def _(n):
+        for slot in range(4):
+            big.ring(slot, 0, n).wait_send()
+        for slot in range(3):
+            group.ring(slot, 0, n).wait_send()
+
+
+def run_backward(dwup, gatt, att, wall, q, kx, vx, rnd, p, tok, sio, u, st, fg, fb, skip, decay):
+    shape = jax.ShapeDtypeStruct
+    dma = pltpu.SemaphoreType.DMA
+    vmem = pltpu.VMEM
+    full = (1024, 1024)
+    ext = (1024 + CTX, 1024)
+    part = (64, 1024)
+    cut = (64, 768)
+    return pl.pallas_call(
+        backward_kernel,
+        name="backward_part",
+        out_shape=(
+            shape(full, BF16), shape((64, 4096), F32), shape(part, F32), shape(part, F32),
+            shape(part, F32), shape(part, F32), shape((1, 1024), F32), shape((1, 1024), F32),
+            shape((1, 1024), F32), shape((16, 1024), F32), shape((16, 1024), F32), shape((16, 128), F32),
+        ),
+        in_specs=any_spec(11) + vmem_spec(6),
+        out_specs=any_spec(1) + vmem_spec(11),
+        scratch_shapes=[
+            vmem((4, NC) + part, BF16), vmem((5, NC) + part, BF16), vmem((4, NC - 1) + part, BF16),
+            vmem((NC,) + part, BF16), vmem((5,) + part, BF16), vmem((5,) + part, BF16), vmem(part, F32),
+            vmem((4, NC, 2) + cut, BF16), vmem((4, NC) + cut, BF16), vmem((3, NC - 1) + cut, BF16),
+            vmem((NC,) + cut, BF16), vmem((4,) + cut, BF16), vmem((4,) + cut, BF16), vmem(cut, F32),
+            vmem((NC, 2) + part, BF16),
+            vmem(full, BF16), vmem(full, BF16), vmem(full, BF16), vmem(full, BF16), vmem(full, BF16),
+            vmem(ext, BF16), vmem(ext, BF16), vmem(ext, BF16), vmem(ext, BF16), vmem(ext, BF16),
+            vmem((2, BLK, CTX + BLK), BF16), vmem((BLK, CTX + BLK), BF16), vmem((2, 256, 1024), BF16),
+            vmem((256, 1024), F32), vmem((1024, 128), BF16), vmem((128, 1024), F32), vmem((CTX, 1024), F32),
+            dma((12,)), dma((2,)), dma((2,)), dma((4,)), dma((5,)), dma((5,)), dma((4,)), dma((4,)),
+            dma((4, NC - 1)), dma((4, NC - 1)), dma((3, NC - 1)), dma((3, NC - 1)),
+            dma((NC,)), dma((NC,)), dma((NC,)), dma((NC,)), dma((5,)), dma((5,)), dma((4,)), dma((4,)),
+        ],
+        compiler_params=pltpu.CompilerParams(
+            collective_id=2, has_side_effects=True, vmem_limit_bytes=VMEM_LIMIT
+        ),
+    )(dwup, gatt, att, wall, q, kx, vx, rnd, p, tok, sio, u, st, fg, fb, skip, decay)
+
+
+def small_kernel(x, out, got, here, ss, sr, bs, br):
+    rep, shard = lax.axis_index("rep"), lax.axis_index("shard")
+    me = rep * 16 + shard
+
+    def device(away):
+        other = (me + away) % 32
+        return other, (other // 16, other % 16)
+
+    barrier = pltpu.get_barrier_semaphore()
+
+    @pl.loop(1, 32)
+    def _(away):
+        pl.semaphore_signal(barrier, inc=1, device_id=device(away)[1], device_id_type=MESH)
+
+    pl.semaphore_wait(barrier, 31)
+
+    def share(away):
+        other, where = device(away)
+        return rcopy(x.at[other], got.at[away], ss.at[away], sr.at[away], where)
+
+    def spread(away):
+        return rcopy(here, out.at[me], bs.at[away], br.at[away], device(away)[1])
+
+    @pl.loop(1, 32)
+    def _(away):
+        share(away).start()
+
+    here[...] = x[me]
+
+    @pl.loop(1, 32)
+    def _(away):
+        share(away).wait_recv()
+        here[...] = here[...] + got[away]
+
+    @pl.loop(1, 32)
+    def _(away):
+        spread(away).start()
+
+    out[me] = here[...]
+
+    @pl.loop(1, 32)
+    def _(away):
+        spread(away).wait()
+        share(away).wait_send()
+
+
+def run_small(x):
+    dma = pltpu.SemaphoreType.DMA
+    return pl.pallas_call(
+        small_kernel,
+        name="small_sums",
+        out_shape=jax.ShapeDtypeStruct((32, 16, 128), F32),
+        in_specs=vmem_spec(1),
+        out_specs=vmem_spec(1)[0],
+        scratch_shapes=[
+            pltpu.VMEM((32, 16, 128), F32), pltpu.VMEM((16, 128), F32),
+            dma((32,)), dma((32,)), dma((32,)), dma((32,)),
+        ],
+        compiler_params=pltpu.CompilerParams(collective_id=3, has_side_effects=True),
+    )(x)
+
+
+def fused_device(
+    tokens, lengths, first_gain, first_bias, decay_rates, state_in, state_out, skip_gain,
+    query_weight, key_weight, value_weight, output_weight, second_gain, second_bias,
+    up_weight, up_bias, down_weight, down_bias, cotangent,
+):
+    tok = tokens.reshape(1024, 1024)
+    cot = cotangent.reshape(1024, 1024)
+    fg, fb, skip, sg, sb, dnb, upb = (
+        v.reshape(1, -1)
+        for v in (first_gain, first_bias, skip_gain, second_gain, second_bias, down_bias, up_bias)
+    )
+    decay = decay_rates.reshape(16, 1)
+    live = jnp.broadcast_to(lengths.reshape(1, 1), (1, 1024))
+    sio = jnp.concatenate([state_in.T, state_out.T, jnp.zeros((64, 96), BF16)], axis=1)
+    wall, sio_all, rnd, q, kx, vx, att, res, sec, p, u, st = run_forward(
+        tok, query_weight, key_weight, value_weight, output_weight, up_weight, sio,
+        fg, fb, skip, sg, sb, decay,
+    )
+    result, gatt, dwup, piece_down, gdb, gub, gsg, gsb = run_feed(
+        sec, res, wall, down_weight, cot, live, upb, dnb, sg
+    )
+    gtok, piece_up, piece_out, piece_q, piece_k, piece_v, gfg, gfb, gskip, gsi, gso, grate = run_backward(
+        dwup.reshape(4, NC, 2, 64, 1024), gatt, att, wall, q, kx, vx, rnd, p, tok, sio_all,
+        u, st, fg, fb, skip, decay,
+    )
+    flat = jnp.concatenate(
+        [gfg[0], gfb[0], gskip[0], gsg[0], gsb[0], gdb[0], gub[0], gsi.reshape(-1), gso.reshape(-1)]
+        + [grate[:, 0], jnp.zeros((65536 - 10 * 1024 - 2 * 16384 - 16,), F32)]
+    )
+    total = run_small(flat.reshape(32, 16, 128)).reshape(-1)
+    row = [total[i * 1024 : (i + 1) * 1024] for i in range(6)]
+    shard = lax.axis_index("shard")
+    mine = [
+        lax.dynamic_slice(total[at : at + 16384].reshape(16, 1024), (0, shard * 64), (16, 64))
+        for at in (10240, 26624)
+    ]
+    return (
+        result.reshape(1, 1024, 1024), gtok.reshape(1, 1024, 1024), row[0], row[1],
+        total[43008:43024], mine[0], mine[1], row[2], piece_q, piece_k, piece_v, piece_out,
+        row[3], row[4], piece_up, total[6144:10240], piece_down, row[5],
+    )
 
 
 NORM_EPS = 1e-05
@@ -358,8 +1658,9 @@
         P(),
         P(("rep", "shard"), None, None),
     )
+    fused = mesh.shape["rep"] == 2 and mesh.shape["shard"] == 2 * NC
     return jax.shard_map(
-        per_device,
+        fused_device if fused else per_device,
         mesh=mesh,
         in_specs=placed,
         out_specs=(

time: 1300 us -> 377 us (0.29)
  waiting for transfers between devices: 671 us -> 0 us
  Pallas kernels: 0 us -> 345 us
  matrix products: 244 us -> 0 us
  local copies, waits for them, and re-layouts: 190 us -> 29.2 us
  blocking collectives: 86.6 us -> 0 us
  other arithmetic: 76.2 us -> 0.69 us
  between operations: 17.2 us -> 1.46 us
    reduce_scatter x6 -> x0, waiting for transfers between devices: 441 us -> none  [the longest x1 180 us: per_device(): lax.psum_scatter(grad_down, 'shard', scatter_dimension=0, tiled=True)]
    pallas_call x0 -> x4, Pallas kernels: none -> 345 us  [the longest x1 121 us: run_feed(): pl.pallas_call(feed_kernel, name='feed_part', out_shape=(shape(big, BF16)...]
    dot_general x43 -> x0, matrix products: 242 us -> none  [the longest x1 25 us: per_device(): jnp.einsum('rd,fd->rf', branch_rounded, full_down, preferred_element_type...]
    all_gather x6 -> x0, waiting for transfers between devices: 129 us -> none  [the longest x1 58.3 us: per_device(): lax.all_gather(down_weight, 'shard', axis=0, tiled=True)]
    unnamed x17 -> x0, waiting for transfers between devices: 54.3 us -> none
    psum x1 -> x0, waiting for transfers between devices: 47.5 us -> none  [per_device(): lax.psum(piece_query.astype(jnp.bfloat16), 'rep').astype(jnp.float32)]
    psum x2 -> x0, blocking collectives: 45.5 us -> none  [the longest x1 40.5 us: per_device(): lax.psum((grad_first_gain, grad_first_bias, grad_rates, grad_skip, grad_s...]
    all_gather x2 -> x0, blocking collectives: 41.2 us -> none  [the longest x1 23.6 us: per_device(): lax.all_gather(state_in, 'shard', axis=1, tiled=True)]
  transfers between devices with their start and end apart: 15 -> 0, of which waited for: 9 -> 0; matrix products, arithmetic and copies ran while one was open for 33% -> 0% of each run, Pallas kernels for 0% -> 0%
where the time goes in v1:
time: 377 us; the launch traced here: 376 us
  Pallas kernels  345 us (92%)
  local copies, waits for them, and re-layouts  29.2 us (8%)
    pallas_call x1, Pallas kernels, run_feed(): pl.pallas_call(feed_kernel, name='feed_part', out_shape=(shape(big, BF16)...  121 us
    pallas_call x1, Pallas kernels, run_backward(): pl.pallas_call(backward_kernel, name='backward_part', out_shape=(shape(fu...  111 us
    pallas_call x1, Pallas kernels, run_forward(): pl.pallas_call(forward_kernel, name='forward_part', out_shape=(shape((8,)...  92.1 us
    pallas_call x1, Pallas kernels, run_small(): pl.pallas_call(small_kernel, name='small_sums', out_shape=jax.ShapeDtypeS...  21.8 us
    unnamed x36, local copies, waits for them, and re-layouts  11.9 us
    concatenate x1, local copies, waits for them, and re-layouts, fused_device(): jnp.concatenate([gfg[0], gfb[0], gskip[0], gsg[0], gsb[0], gdb[0], gub[0]...  9.02 us

profile of v1, /device:TPU:0, one launch (start us, length us, event | category | flops | bytes accessed | tf_op | source)
XLA Modules:
  0.0 376.4 jit_solution(13860775369631532318)
XLA Ops:
  0.7 1.3 copy.43.decay
  2.0 0.8 copy.41
  2.8 0.8 copy.42
  3.5 0.1 pad.2.clone
  3.6 0.7 maximum_maximum_fusion.sio
  4.3 92.1 %forward_part.1 = (bf16[8,1024,1024]{2,1,0:T(8,128)(2,1)}, bf16[1024,128]{1,0:T(8,128)(2,1)}, bf16[1152,1024]{1,0:T(8,128)(2,1)}, bf16[1024,1024]{1,0:T(8,128)(2...) custom-call(bf16[1024,1024]{1,0:T(8,128)(2,1)} %bitcast.31, ...), custom_call_target="tpu_custom_call" | custom-call | tf_op jit(solution)/shard_map/forward_part/pallas_call | solution.py:419
  97.1 0.6 broadcast_in_dim.15.live
  97.7 120.6 %feed_part.1 = (bf16[1024,1024]{1,0:T(8,128)(2,1)}, bf16[1024,1024]{1,0:T(8,128)(2,1)}, bf16[4,1024,1024]{2,1,0:T(8,128)(2,1)}, f32[256,1024]{1,0:T(8,128)}, f32...) custom-call(bf16[1024,1024]{1,0:T(8,128)(2,1)} %get-tuple-element.50.sec, ...), custom_call_target="tpu_custom_call" | custom-call | tf_op jit(solution)/shard_map/feed_part/pallas_call | solution.py:753
  218.3 0.0 copy-start.8
  218.3 0.0 copy-start.9
  218.3 0.0 copy-start.10
  218.4 0.0 copy-start.11
  218.4 110.6 %backward_part.1 = (bf16[1024,1024]{1,0:T(8,128)(2,1)}, f32[64,4096]{1,0:T(8,128)}, f32[64,1024]{1,0:T(8,128)}, f32[64,1024]{1,0:T(8,128)}, f32[64,1024]{1,0:T(8...) custom-call(bf16[4,8,2,64,1024]{4,3,2,1,0:T(8,128)(2,1)} %bitcast.33, ...), custom_call_target="tpu_custom_call" | custom-call | tf_op jit(solution)/shard_map/backward_part/pallas_call | solution.py:1177
  329.0 0.0 copy-start
  329.0 1.0 copy.45
  330.0 0.9 copy.46
  330.9 0.8 slice_reduce_fusion
  331.7 0.0 copy-done.8
  331.7 0.0 copy-done.9
  331.7 0.0 copy-done.10
  331.7 0.0 copy-done.11
  331.7 9.0 %concatenate.7 = f32[65536]{0:T(1024)} concatenate(f32[1024]{0:T(1024)} %bitcast.61, f32[1024]{0:T(1024)} %bitcast.62, f32[1024]{0:T(1024)} %bitcast.63, f32[1024]{0:T(1024)S(1)} %bitcast.59, f32[1024]{0:T(1024)S(1)} %bitcast.60, f32[1024]{0:T(1024)S(1)} %bitcast.58, f32[4096]{0:T(1024)S(1)} %bitcast.52, f32[16384]{0:T(1024)S(1)} %bitcast.40, f32[16384]{0:T(1024)S(1)} %bitcast.41, ...), dimensions={0} | concatenate | bytes 524288 | tf_op jit(solution)/shard_map/concatenate | solution.py:1294
  340.7 21.8 %small_sums.1 = f32[32,16,128]{2,1,0:T(8,128)} custom-call(f32[32,16,128]{2,1,0:T(8,128)} %bitcast.37), custom_call_target="tpu_custom_call" | custom-call | tf_op jit(solution)/shard_map/small_sums/pallas_call | solution.py:1255
  362.5 0.9 fusion.1
  363.5 0.7 constant_dynamic-slice_fusion
  364.1 1.3 fusion
  365.5 1.3 slice.47
  366.8 1.2 slice.52
  368.0 0.0 copy-done
  368.0 0.0 copy-start.1
  368.0 1.3 copy.56
  369.3 1.0 copy-done.1
  370.3 0.0 copy-start.7
  370.3 0.0 copy-start.6
  370.3 0.0 copy-start.3
  370.3 1.3 copy.57
  371.7 0.0 copy-done.7
  371.7 0.7 copy.58
  372.4 0.0 copy-done.6
  372.4 0.7 copy.59
  373.1 0.0 copy-done.5
  373.1 0.7 copy.60
  373.8 0.0 copy-done.4
  373.8 0.7 copy.61
  374.5 0.0 copy-done.3
  374.5 1.0 copy.62
  375.5 0.0 copy-done.2
  375.5 1.0 copy.63
  (7 shorter events, 0.1 us)
Async XLA Ops:
  218.3 113.4 %copy-start.8 = (f32[1,4096]{1,0:T(1,128)S(1)}, f32[1,4096]{1,0:T(1,128)}, u32[]{:S(2)}) copy-start(f32[1,4096]{1,0:T(1,128)} %get-tuple-element.72) | copy-start | bytes 49156
  218.3 113.4 %copy-start.9 = (f32[1,1024]{1,0:T(1,128)S(1)}, f32[1,1024]{1,0:T(1,128)}, u32[]{:S(2)}) copy-start(f32[1,1024]{1,0:T(1,128)} %get-tuple-element.71) | copy-start | bytes 12292
  218.3 113.4 %copy-start.10 = (f32[1,1024]{1,0:T(1,128)S(1)}, f32[1,1024]{1,0:T(1,128)}, u32[]{:S(2)}) copy-start(f32[1,1024]{1,0:T(1,128)} %get-tuple-element.69) | copy-start | bytes 12292
  218.4 113.4 %copy-start.11 = (f32[1,1024]{1,0:T(1,128)S(1)}, f32[1,1024]{1,0:T(1,128)}, u32[]{:S(2)}) copy-start(f32[1,1024]{1,0:T(1,128)} %get-tuple-element.70) | copy-start | bytes 12292
  329.0 39.0 %copy-start = (bf16[1024,1024]{1,0:T(8,128)(2,1)S(1)}, bf16[1024,1024]{1,0:T(8,128)(2,1)}, u32[]{:S(2)}) copy-start(bf16[1024,1024]{1,0:T(8,128)(2,1)} %get-tuple-element.53) | copy-start | bytes 6291460
  368.0 2.3 copy-start.1
  370.3 1.3 copy-start.7
  370.3 2.1 copy-start.6
  370.3 2.8 copy-start.5
  370.3 3.5 copy-start.4
  370.3 4.2 %copy-start.3 = (f32[64,4096]{1,0:T(8,128)S(1)}, f32[64,4096]{1,0:T(8,128)}, u32[]{:S(2)}) copy-start(f32[64,4096]{1,0:T(8,128)} %get-tuple-element.124) | copy-start | bytes 3145732
  371.7 3.8 %copy-start.2 = (f32[256,1024]{1,0:T(8,128)S(1)}, f32[256,1024]{1,0:T(8,128)}, u32[]{:S(2)}) copy-start(f32[256,1024]{1,0:T(8,128)} %get-tuple-element.126) | copy-start | bytes 3145732

commit v2 on v1

--- a/solution.py
+++ b/solution.py
@@ -107,10 +107,10 @@
 
 
 def forward_kernel(
-    tok, wq, wk, wv, wo, wup, sio, fg, fb, skip, sg, sb, decay,
+    tok, wq, wk, wv, wo, wup, s_in, s_out, fg, fb, skip, sg, sb, decay,
     wall, sio_all, rnd_o, q_o, k_o, v_o, att_o, res_o, sec_o, p_o, u_o, st_o,
     tok_s, rnd_s, w_s, q_s, k_s, v_s, att_s, res_s, sec_s, pbuf, nctx, sio_s,
-    own_s, loc, rs, rr, ss, sr, cs, cr, xs, xr, outs, psem,
+    own_s, sio_own, loc, rs, rr, ss, sr, cs, cr, xs, xr, outs, psem,
 ):
     net = Net()
     rep, core = net.rep, net.core
@@ -127,12 +127,16 @@
         pltpu.make_async_copy(wup.at[:, pl.ds(i * width, width)], own_s.at[4 + i], loc.at[4 + i])
         for i in range(4)
     ]
-    small = pltpu.make_async_copy(sio, sio_all.at[mine], loc.at[8])
+    small = pltpu.make_async_copy(sio_own, sio_all.at[mine], loc.at[8])
     arrive = pltpu.make_async_copy(tok, tok_s, loc.at[9])
     for copy in copies:
         copy.start()
+    arrive.start()
+    packed = jnp.concatenate(
+        [s_in[...].astype(F32), s_out[...].astype(F32), jnp.zeros((96, rows_of), F32)], axis=0
+    )
+    sio_own[...] = packed.T.astype(BF16)
     small.start()
-    arrive.start()
     net.greet()
     for copy in copies:
         copy.wait()
@@ -224,10 +228,11 @@
         if hop < 3 - way:
             ring_small(way, hop + 1, where).start()
         mate_small(1 + 2 * hop + way, where).start()
-        if n == 3:
-            for slot in range(2, 6):
-                for each in range(2):
-                    ring_own(slot, each)
+        if n >= 2:
+            serve(2, turns[n - 2][1], turns[n - 2][0])
+        if n in (0, 2, 4, 5):
+            for each in range(2):
+                ring_own({0: 2, 2: 3, 4: 4, 5: 5}[n], each)
         if n >= 3:
             serve_in(0, turns[n - 3][1], turns[n - 3][0])
     first_norm(7)
@@ -235,16 +240,17 @@
         serve_in(0, way, hop)
 
     def event(m):
-        hop = m // 8
-        way = (m % 8) // 4
-        slot = 2 + m % 4
+        later = (m - 2 + 3) // 3 - 1
+        turn = (5 + m) * (1 - (m + 20) // 22) + later * ((m + 20) // 22)
+        slot = 2 + ((m + 20) // 22) * (1 + (m + 1) % 3)
+        hop, way = turn // 2, turn % 2
         serve(slot, way, hop)
 
         @pl.when(slot == 3)
         def _():
             serve_out(3, 1, way, hop)
 
-        @pl.when((slot == 3) & (m >= 8))
+        @pl.when((slot == 5) & (turn >= 2))
         def _():
             serve_in(1, way, hop - 1)
 
@@ -268,7 +274,7 @@
     u_all = lax.dot_general(
         sio_s[...], rnd_s[pl.ds(0, BLK), :], (((0,), (1,)), ((), ())), preferred_element_type=F32
     )
-    factor = jnp.exp(-decay[...])
+    factor = jnp.exp(-column(decay[...]))
     raw = u_all[0:16, :]
     u_o[...] = raw
     states = lane_scan(raw * jnp.sqrt(1.0 - factor * factor), factor, False)
@@ -292,11 +298,10 @@
     def _(at):
         cols = pl.ds(pl.multiple_of(at * 256, 256), 256)
         q_s[:, cols] = dot_nn(rnd_s[pl.ds(0, 1024), :], w_s[0, :, cols]).astype(BF16)
-        event(3 * at)
+        event(2 * at)
         k_s[:, cols] = dot_nn(rnd_s[...], w_s[1, :, cols]).astype(BF16)
-        event(3 * at + 1)
         v_s[:, cols] = dot_nn(rnd_s[...], w_s[2, :, cols]).astype(BF16)
-        event(3 * at + 2)
+        event(2 * at + 1)
 
     for i, (a, b) in enumerate(((q_s, q_o), (k_s, k_o), (v_s, v_o))):
         finals.append(pltpu.make_async_copy(a, b, outs.at[1 + i]))
@@ -349,7 +354,10 @@
                     pbuf[slot, pl.ds(i * 256, 256), pl.ds(0, CTX)] = weights
                 att_s[rows, cols] = mixed.astype(BF16)
             p_copy(slot, b * 8 + h).start()
-            event(12 + b * 8 + h)
+
+            @pl.when(h < 5)
+            def _(b=b, h=h):
+                event(8 + 5 * b + h)
 
     finals.append(pltpu.make_async_copy(att_s, att_o, outs.at[4]))
     finals[-1].start()
@@ -371,7 +379,9 @@
         sec_s[rows, :] = (xhat * sg[...] + sb[...]).astype(BF16)
         pltpu.make_async_copy(res_s.at[rows], res_o.at[rows], outs.at[5 + at]).start()
         pltpu.make_async_copy(sec_s.at[rows], sec_o.at[rows], outs.at[9 + at]).start()
-
+        event(18 + at)
+
+    event(22)
     for copy in finals:
         copy.wait()
     for at in range(4):
@@ -403,6 +413,12 @@
             twin(turn, index, 0, block(0)).wait_send()
 
 
+def column(row):
+    wide = jnp.broadcast_to(row, (16, 16))
+    same = lax.broadcasted_iota(jnp.int32, (16, 16), 0) == lax.broadcasted_iota(jnp.int32, (16, 16), 1)
+    return jnp.sum(jnp.where(same, wide, 0.0), axis=1, keepdims=True)
+
+
 def any_spec(n):
     return [pl.BlockSpec(memory_space=pl.ANY)] * n
 
@@ -411,7 +427,7 @@
     return [pl.BlockSpec(memory_space=pltpu.VMEM)] * n
 
 
-def run_forward(tok, wq, wk, wv, wo, wup, sio, fg, fb, skip, sg, sb, decay):
+def run_forward(tok, wq, wk, wv, wo, wup, s_in, s_out, fg, fb, skip, sg, sb, decay):
     shape = jax.ShapeDtypeStruct
     dma = pltpu.SemaphoreType.DMA
     big = (1024, 1024)
@@ -425,7 +441,7 @@
             shape(big, BF16), shape((16, BLK, CTX + BLK), BF16), shape((16, BLK), F32),
             shape((16, BLK), F32),
         ),
-        in_specs=any_spec(7) + vmem_spec(6),
+        in_specs=any_spec(6) + vmem_spec(8),
         out_specs=any_spec(10) + vmem_spec(2),
         scratch_shapes=[
             pltpu.VMEM(big, BF16), pltpu.VMEM(ext, BF16), pltpu.VMEM((4,) + big, BF16),
@@ -433,14 +449,14 @@
             pltpu.VMEM(big, BF16), pltpu.VMEM(big, F32), pltpu.VMEM(big, BF16),
             pltpu.VMEM((2, BLK, CTX + BLK), BF16), pltpu.VMEM((CTX, 1024), F32),
             pltpu.VMEM((1024, 128), BF16),
-            pltpu.VMEM((8, 64, 1024), BF16),
+            pltpu.VMEM((8, 64, 1024), BF16), pltpu.VMEM((64, 128), BF16),
             dma((10,)), dma((6, 2, 4)), dma((6, 2, 4)), dma((2, 4)), dma((2, 4)),
             dma((9, NC)), dma((9, NC)), dma((2, NC - 1)), dma((2, NC - 1)), dma((13,)), dma((2,)),
         ],
         compiler_params=pltpu.CompilerParams(
             collective_id=0, has_side_effects=True, vmem_limit_bytes=VMEM_LIMIT
         ),
-    )(tok, wq, wk, wv, wo, wup, sio, fg, fb, skip, sg, sb, decay)
+    )(tok, wq, wk, wv, wo, wup, s_in, s_out, fg, fb, skip, sg, sb, decay)
 
 
 GELU_C = math.sqrt(2.0 / math.pi)
@@ -449,7 +465,7 @@
 
 def feed_kernel(
     sec, res, wall, wdn, cot, live, upb, dnb, sg,
-    out_o, gatt_o, dwup_o, piece_o, gdb_o, gub_o, gsg_o, gsb_o,
+    out_o, gatt_o, dwup_o, fin_o, finr_o, gdb_o, gub_o, gsg_o, gsb_o,
     sec_s, gb_s, wup_s, wd_s, br_s, gs_s, act_s, gh_s, a_s, b_s, prec, rrec, rsend, xsend, xrec,
     xfs, xfr, dwup_s, own_s, res_s,
     loc, ars, arr, axs, axr, cas, car, cxs, cxr, ps, pr, rs, rr, xs, xr, fs, fr, outs, dsem,
@@ -461,8 +477,8 @@
     part = 64
     ahead, behind = net.along(1), net.along(-1)
 
-    def ring_part(shard, size=ring_rows, first=rep * part):
-        return pl.ds(pl.multiple_of(shard * rows_of + first, part), size)
+    def ring_part(shard, j, first=rep):
+        return pl.ds(pl.multiple_of(shard * rows_of + (first + j) * part, part), part)
 
     def sole_part(shard, of):
         return pl.ds(pl.multiple_of(shard * rows_of + 3 * of * part, part), part)
@@ -487,39 +503,44 @@
     net.greet()
     loads[0].wait()
 
-    def gather(hop, shard):
-        ref = wd_s.at[ring_part(shard)]
-        return rcopy(ref, ref, ars.at[hop], arr.at[hop], ahead)
+    def gather(j, hop, shard):
+        ref = wd_s.at[ring_part(shard, j)]
+        return rcopy(ref, ref, ars.at[j, hop], arr.at[j, hop], ahead)
 
     def gather_twin(hop, shard, of):
         ref = wd_s.at[sole_part(shard, of)]
         return rcopy(ref, ref, axs.at[hop], axr.at[hop], net.twin)
 
-    def mate_ring(index, shard, first):
-        ref = wd_s.at[ring_part(shard, ring_rows, first)]
-        return rcopy(ref, ref, cas.at[index], car.at[index], net.mate)
+    def mate_ring(j, index, shard):
+        ref = wd_s.at[ring_part(shard, j)]
+        return rcopy(ref, ref, cas.at[j, index], car.at[j, index], net.mate)
 
     def mate_sole(index, shard, of):
         ref = wd_s.at[sole_part(shard, of)]
         return rcopy(ref, ref, cxs.at[index], cxr.at[index], net.mate)
 
     here = net.shard
-    ring_own = own_s.at[pl.ds(pl.multiple_of(rep * part, part), ring_rows)]
     sole_own = own_s.at[pl.ds(pl.multiple_of(3 * (1 - rep) * part, part), part)]
-    rcopy(ring_own, wd_s.at[ring_part(here)], ars.at[0], arr.at[0], ahead).start()
-    rcopy(ring_own, wd_s.at[ring_part(here)], cas.at[0], car.at[0], net.mate).start()
+    for j in range(3):
+        ring_own = own_s.at[pl.ds(pl.multiple_of((rep + j) * part, part), part)]
+        target = wd_s.at[ring_part(here, j)]
+        rcopy(ring_own, target, ars.at[j, 0], arr.at[j, 0], ahead).start()
+        rcopy(ring_own, target, cas.at[j, 0], car.at[j, 0], net.mate).start()
     rcopy(sole_own, wd_s.at[sole_part(here, 1 - rep)], cxs.at[0], cxr.at[0], net.mate).start()
 
-    def serve(hop):
+    def serve(j, hop):
         shard = mine_at(hop)
-        gather(hop, shard).wait_recv()
+        gather(j, hop, shard).wait_recv()
 
         @pl.when(hop < NC - 2)
         def _():
-            gather(hop + 1, shard).start()
-
-        gather_twin(hop, shard, rep).start()
-        mate_ring(hop + 1, shard, rep * part).start()
+            gather(j, hop + 1, shard).start()
+
+        @pl.when(j == 2 * rep)
+        def _():
+            gather_twin(hop, shard, rep).start()
+
+        mate_ring(j, hop + 1, shard).start()
 
     def serve_twin(hop):
         shard = mine_at(hop)
@@ -535,14 +556,15 @@
     def _(at):
         rows = pl.ds(pl.multiple_of(at * 256, 256), 256)
         when = lax.broadcasted_iota(jnp.int32, (256, 1024), 0) + at * 256
-        kept = jnp.where(when < live[...], gb_s[rows, :].astype(F32), 0.0)
+        kept = jnp.where(when < live[0], gb_s[rows, :].astype(F32), 0.0)
         gb_s[rows, :] = kept.astype(BF16)
         added = jnp.sum(kept, axis=0, keepdims=True)
         gdb_o[...] = jnp.where(at == 0, added, gdb_o[...] + added)
         br_s[rows, :] = jnp.zeros((256, 1024), F32)
         gs_s[rows, :] = jnp.zeros((256, 1024), F32)
 
-    serve(0)
+    for j in range(3):
+        serve((2 * rep + j) % 3, 0)
     for load in loads[3:]:
         load.wait()
     serve_twin(0)
@@ -551,8 +573,8 @@
         slot = step % 2
         return rcopy(b_s.at[slot], prec.at[step], ps.at[step], pr.at[step], net.mate)
 
-    def to_ring(step):
-        return rcopy(rsend.at[step % 2], rrec.at[step], rs.at[step], rr.at[step], ahead)
+    def to_ring(j, step):
+        return rcopy(rsend.at[step % 2, j], rrec.at[step, j], rs.at[step, j], rr.at[step, j], ahead)
 
     def to_twin(step):
         return rcopy(xsend.at[step % 2], xrec.at[step], xs.at[step], xr.at[step], net.twin)
@@ -579,36 +601,38 @@
         xsend[slot] = a_s[slot, sole_theirs, :].astype(BF16)
         to_twin(step).start()
 
-    def forward(step):
+    def forward(j, step):
         slot = step % 2
-        to_twin(step).wait_recv()
-        a_s[slot, sole_mine, :] = a_s[slot, sole_mine, :] + xrec[step].astype(F32)
+        rows = pl.ds(pl.multiple_of((rep + j) * part, part), part)
+
+        @pl.when(j == 2 * rep)
+        def _():
+            to_twin(step).wait_recv()
+            a_s[slot, rows, :] = a_s[slot, rows, :] + xrec[step].astype(F32)
 
         @pl.when(step >= 1)
         def _():
-            to_ring(step - 1).wait_recv()
-            a_s[slot, ring_local, :] = a_s[slot, ring_local, :] + rrec[step - 1].astype(F32)
+            to_ring(j, step - 1).wait_recv()
+            a_s[slot, rows, :] = a_s[slot, rows, :] + rrec[step - 1, j].astype(F32)
 
         @pl.when((step >= 2) & (step < NC - 1))
         def _():
-            to_ring(step - 2).wait_send()
+            to_ring(j, step - 2).wait_send()
 
         @pl.when(step < NC - 1)
         def _():
-            rsend[slot] = a_s[slot, ring_local, :].astype(BF16)
-            to_ring(step).start()
+            rsend[slot, j] = a_s[slot, rows, :].astype(BF16)
+            to_ring(j, step).start()
 
     @pl.loop(0, NC)
     def _(step):
         slot = step % 2
         a, b = mine_at(step), other_at(step)
         index = (step + 1) % NC
-        mate_ring(index, b, rep * part).wait_recv()
-        mate_sole(index, b, 1 - rep).wait_recv()
-
-        @pl.when(step < NC - 2)
-        def _():
-            serve(step + 1)
+
+        @pl.when(step >= 1)
+        def _():
+            combine(step - 1)
 
         def up(shard):
             cols = pl.ds(pl.multiple_of((shard % 4) * 256, 256), 256)
@@ -617,10 +641,9 @@
         def bias(shard):
             return upb[:, pl.ds(pl.multiple_of(shard * 256, 256), 256)]
 
-        @pl.loop(0, 4)
-        def _(at):
-            rows = pl.ds(pl.multiple_of(at * 256, 256), 256)
-            for half, shard in enumerate((a, b)):
+        def middle(half, shard, at):
+            for block_at in range(2):
+                rows = pl.ds(pl.multiple_of(at * 512 + block_at * 256, 256), 256)
                 cols = pl.ds(half * 256, 256)
                 hidden = dot_nn(sec_s[rows, :], up(shard)) + bias(shard)
                 grad = dot_nt(gb_s[rows, :], wd_s[block(shard), :])
@@ -633,13 +656,25 @@
                 )
                 gh_s[rows, cols] = (grad * slope).astype(BF16)
 
-        @pl.when(step < NC - 2)
-        def _():
-            serve_twin(step + 1)
-
-        @pl.when(step >= 1)
-        def _():
-            combine(step - 1)
+        @pl.loop(0, 2)
+        def _(at):
+            @pl.when(step < NC - 2)
+            def _():
+                serve((2 * rep + at) % 3, step + 1)
+
+            middle(0, a, at)
+
+        for j in range(3):
+            mate_ring(j, index, b).wait_recv()
+        mate_sole(index, b, 1 - rep).wait_recv()
+
+        @pl.loop(0, 2)
+        def _(at):
+            @pl.when((at == 0) & (step < NC - 2))
+            def _():
+                serve((2 * rep + 2) % 3, step + 1)
+
+            middle(1, b, at)
 
         made = dot_tn(act_s[...], gb_s[...])
 
@@ -651,6 +686,7 @@
         b_s[slot] = made[256:512].astype(BF16)
         to_mate(step).start()
 
+        rise_up = dot_tn(sec_s[...], gh_s[...]).astype(BF16)
         for half, shard in enumerate((a, b)):
             cols = pl.ds(pl.multiple_of(shard * 256, 256), 256)
             gub_o[:, cols] = jnp.sum(
@@ -661,12 +697,8 @@
             def _(half=half, shard=shard):
                 dwup_copy(slot, half, shard).wait()
 
-            dwup_s[slot, half] = dot_tn(sec_s[...], gh_s[:, half * 256 : half * 256 + 256]).astype(BF16)
+            dwup_s[slot, half] = rise_up[:, half * 256 : half * 256 + 256]
             dwup_copy(slot, half, shard).start()
-
-        @pl.when(step >= 1)
-        def _():
-            forward(step - 1)
 
         @pl.loop(0, 4)
         def _(at):
@@ -676,6 +708,14 @@
             rise = jnp.concatenate([up(a), up(b)], axis=1)
             gs_s[rows, :] = gs_s[rows, :] + dot_nt(gh_s[rows, :], rise)
 
+            @pl.when((at < 3) & (step >= 1))
+            def _():
+                forward((2 * rep + 1 + at) % 3, step - 1)
+
+            @pl.when((at == 1) & (step < NC - 2))
+            def _():
+                serve_twin(step + 1)
+
     def residual_in(at):
         rows = pl.ds(at * 256, 256)
         return pltpu.make_async_copy(res.at[rows], res_s.at[rows], loc.at[at])
@@ -698,7 +738,7 @@
         kept = res_s[rows, :]
         when = lax.broadcasted_iota(jnp.int32, (256, 1024), 0) + at * 256
         total = kept + br_s[rows, :] + dnb[...]
-        sec_s[rows, :] = jnp.where(when < live[...], total, 0.0).astype(BF16)
+        sec_s[rows, :] = jnp.where(when < live[0], total, 0.0).astype(BF16)
         xhat, inverse = norm_parts(kept)
         grad = gs_s[rows, :]
         gain = jnp.sum(grad * xhat, axis=0, keepdims=True)
@@ -713,36 +753,38 @@
         for which in range(2):
             leave(at, which).start()
 
-    forward(NC - 1)
+    for j in range(3):
+        forward((2 * rep + 1 + j) % 3, NC - 1)
     last = (NC - 1) % 2
     xfs[...] = a_s[last, ring_local, :].astype(BF16)
     swap = rcopy(xfs, xfr, fs.at[0], fr.at[0], net.twin)
     swap.start()
+    fin_o[...] = xfs[...]
 
     @pl.loop(0, NC - 1)
     def _(hop):
-        gather(hop, 0).wait_send()
+        for j in range(3):
+            gather(j, hop, 0).wait_send()
         gather_twin(hop, 0, 0).wait_send()
 
     @pl.loop(0, NC)
     def _(index):
-        mate_ring(index, 0, 0).wait_send()
+        for j in range(3):
+            mate_ring(j, index, 0).wait_send()
         mate_sole(index, 0, 0).wait_send()
 
     for step in range(NC - 2, NC):
         to_mate(step).wait_send()
         to_twin(step).wait_send()
-        to_ring(step - 1).wait_send()
+        for j in range(3):
+            to_ring(j, step - 1).wait_send()
         for half in range(2):
             dwup_copy(step % 2, half, 0).wait()
     for at in range(4):
         for which in range(2):
             leave(at, which).wait()
     swap.wait()
-    theirs = pl.ds(pl.multiple_of((1 - rep) * part, part), ring_rows)
-    piece_o[...] = jnp.zeros((rows_of, 1024), F32)
-    piece_o[ring_local, :] = xfs[...].astype(F32)
-    piece_o[theirs, :] = piece_o[theirs, :] + xfr[...].astype(F32)
+    finr_o[...] = xfr[...]
 
 
 def run_feed(sec, res, wall, wdn, cot, live, upb, dnb, sg):
@@ -755,21 +797,21 @@
         name="feed_part",
         out_shape=(
             shape(big, BF16), shape(big, BF16), shape((4,) + big, BF16),
-            shape((256, 1024), F32), shape((1, 1024), F32), shape((1, 4096), F32),
+            shape((192, 1024), BF16), shape((192, 1024), BF16), shape((1, 1024), F32), shape((1, 4096), F32),
             shape((1, 1024), F32), shape((1, 1024), F32),
         ),
-        in_specs=any_spec(5) + vmem_spec(4),
-        out_specs=any_spec(3) + vmem_spec(5),
+        in_specs=any_spec(5) + [pl.BlockSpec(memory_space=pltpu.SMEM)] + vmem_spec(3),
+        out_specs=any_spec(3) + vmem_spec(6),
         scratch_shapes=[
             vmem(big, BF16), vmem(big, BF16), vmem((4,) + big, BF16), vmem((4096, 1024), BF16),
             vmem(big, F32), vmem(big, F32), vmem((1024, 512), BF16), vmem((1024, 512), BF16),
             vmem((2, 256, 1024), F32), vmem((2, 256, 1024), BF16), vmem((NC, 256, 1024), BF16),
-            vmem((NC - 1, 192, 1024), BF16), vmem((2, 192, 1024), BF16), vmem((2, 64, 1024), BF16),
+            vmem((NC - 1, 3, 64, 1024), BF16), vmem((2, 3, 64, 1024), BF16), vmem((2, 64, 1024), BF16),
             vmem((NC, 64, 1024), BF16), vmem((192, 1024), BF16), vmem((192, 1024), BF16),
             vmem((2, 2, 1024, 256), BF16), vmem((256, 1024), BF16), vmem(big, F32),
-            dma((7,)), dma((NC - 1,)), dma((NC - 1,)), dma((NC - 1,)), dma((NC - 1,)),
-            dma((NC,)), dma((NC,)), dma((NC,)), dma((NC,)), dma((NC,)), dma((NC,)),
-            dma((NC - 1,)), dma((NC - 1,)), dma((NC,)), dma((NC,)), dma((1,)), dma((1,)),
+            dma((7,)), dma((3, NC - 1)), dma((3, NC - 1)), dma((NC - 1,)), dma((NC - 1,)),
+            dma((3, NC)), dma((3, NC)), dma((NC,)), dma((NC,)), dma((NC,)), dma((NC,)),
+            dma((NC - 1, 3)), dma((NC - 1, 3)), dma((NC,)), dma((NC,)), dma((1,)), dma((1,)),
             dma((2, 4)), dma((2, 2)),
         ],
         compiler_params=pltpu.CompilerParams(
@@ -780,13 +822,14 @@
 
 def backward_kernel(
     dwup, gatt, att, wall, q, kx, vx, rnd, p, tok, sio, u_in, st_in, fg, fb, skip, decay,
-    gtok_o, dup_o, do_o, dq_o, dk_o, dv_o, gfg_o, gfb_o, gskip_o, gsi_o, gso_o, grate_o,
+    gsg, gsb, gdb, gub,
+    gtok_o, finb_o, finrb_o, fing_o, finrg_o, sums_o,
     own_b, prec_b, rrec_b, xrec_b, fin_b, finr_b, acc_b,
     own_g, prec_g, rrec_g, xrec_g, fin_g, finr_g, acc_g, go_s,
     gatt_s, wo_s, att_s, ga_s, q_s, k_s, v_s, rnd_s, dk_s, dv_s, pbuf, ds_s, gres_s, nb_s,
-    sio_s, gd_s, gctx_s,
+    sio_s, gd_s, gctx_s, sum_s, got_s, part_s,
     loc, psem, gsem, osem, mbs, mbr, mgs, mgr, rbs, rbr, rgs, rgr, xbs, xbr, xgs, xgr,
-    fbs, fbr, fgs, fgr,
+    fbs, fbr, fgs, fgr, ts, tr, us, ur,
 ):
     net = Net()
     rep, core = net.rep, net.core
@@ -811,7 +854,18 @@
     finr_b[...] = jnp.zeros(finr_b.shape, BF16)
     fin_g[...] = jnp.zeros(fin_g.shape, BF16)
     finr_g[...] = jnp.zeros(finr_g.shape, BF16)
-    net.greet()
+    barrier = pltpu.get_barrier_semaphore()
+    me = rep * (2 * NC) + net.shard
+
+    def device(away):
+        other = (me + away) % (4 * NC)
+        return other, (other // (2 * NC), other % (2 * NC))
+
+    @pl.loop(1, 4 * NC)
+    def _(away):
+        pl.semaphore_signal(barrier, inc=1, device_id=device(away)[1], device_id_type=MESH)
+
+    pl.semaphore_wait(barrier, 4 * NC - 1)
 
     def mate_big(which, source):
         return rcopy(source, prec_b.at[which], mbs.at[which], mbr.at[which], net.mate)
@@ -819,7 +873,7 @@
     def mate_group(g):
         return rcopy(own_g.at[g, :, theirs], prec_g.at[g], mgs.at[g], mgr.at[g], net.mate)
 
-    for i in (0, 3, 1, 2):
+    for i in (1, 2, 3 * (1 - rep), 3 * rep):
         mate_big(i, dwup.at[i, :, theirs]).start()
 
     def chip_for(n):
@@ -887,8 +941,7 @@
                 self.finish(which).start()
 
     big = Stream(
-        lambda which, chip: go_s[chip, core] if isinstance(which, int) and which == 4 else own_b[which, chip],
-        prec_b, rrec_b, xrec_b, fin_b, finr_b, acc_b,
+        lambda which, chip: own_b[which, chip], prec_b, rrec_b, xrec_b, fin_b, finr_b, acc_b,
         (rbs, rbr, xbs, xbr, fbs, fbr),
     )
     group = Stream(
@@ -896,8 +949,54 @@
         (rgs, rgr, xgs, xgr, fgs, fgr),
     )
 
-    def rise(j):
-        return j + 3 * rep * ((2 - j) // 2)
+    def tile(index):
+        return (
+            pl.ds(pl.multiple_of((index // 8) * 16, 16), 16),
+            pl.ds(pl.multiple_of((index % 8) * 128, 128), 128),
+        )
+
+    def share(away):
+        other, where = device(away)
+        return rcopy(sum_s.at[tile(other)], got_s.at[away], ts.at[away], tr.at[away], where)
+
+    def spread(away):
+        return rcopy(part_s, sums_o.at[tile(me)], us.at[away], ur.at[away], device(away)[1])
+
+    def each_device(act):
+        @pl.loop(1, 4 * NC)
+        def _(away):
+            act(away)
+
+    def big_at(e):
+        k, j = e // 4, e % 4
+        n = k - 2 * (j // 2) - j // 3
+        which = (j + 1) * (1 - j // 2) + (j // 2) * (3 * rep * (1 - j // 3) + 4 * (j // 3))
+
+        @pl.when((j >= 2) & (n == 0))
+        def _():
+            mate_big(which, dwup.at[0, :, theirs]).wait_recv()
+
+        @pl.when((n >= 0) & (n <= 7))
+        def _():
+            big.turn(j, which, n, j == 2)
+
+    def group_at(e):
+        k, j = e // 3, e % 3
+        n = k - 2 * (j // 2)
+        which = rep * (1 - (j + 1) // 2) + (j + 1) * ((j + 1) // 2)
+
+        @pl.when((j >= 1) & (n == 0))
+        def _():
+            mate_group(which).wait_recv()
+
+        @pl.when((n >= 0) & (n <= 7))
+        def _():
+            group.turn(j, which, n, j == 0)
+
+    def run(at, low, high):
+        @pl.loop(low, high)
+        def _(e):
+            at(e)
 
     for i in range(2):
         loads[i].wait()
@@ -914,25 +1013,25 @@
 
     for copy in rises:
         copy.wait()
-    for i in range(4):
+    for i in (1, 2):
         mate_big(i, dwup.at[i, :, theirs]).wait_recv()
+    run(big_at, 0, 8)
+    mate_big(3 * (1 - rep), dwup.at[0, :, theirs]).wait_recv()
 
     @pl.loop(0, NC)
     def _(n):
         big.give(3 * (1 - rep), n)
 
-    for n in range(2):
-        for j in (1, 2, 0):
-            big.turn(j, rise(j), n, j == 0)
     loads[2].wait()
 
     @pl.loop(0, 4)
     def _(at):
         cols = pl.ds(pl.multiple_of(at * 256, 256), 256)
-        made = dot_tn(att_s[...], gatt_s[:, cols]).astype(BF16)
-        go_s[:, :, :, cols] = made.reshape(NC, 2, 64, 256)
-
-    mate_big(4, go_s.at[:, theirs]).start()
+        made = dot_tn(att_s[...], gatt_s[:, cols]).reshape(NC, 2, 64, 256)
+        own_b[4, :, :, cols] = jnp.where(core == 0, made[:, 0], made[:, 1]).astype(BF16)
+        go_s[:, :, cols] = jnp.where(core == 0, made[:, 1], made[:, 0]).astype(BF16)
+
+    mate_big(4, go_s).start()
     tok_load = pltpu.make_async_copy(tok, wo_s, loc.at[0])
     tok_load.start()
     for copy in loads[3:]:
@@ -998,20 +1097,7 @@
                 dk_s[rows, cols] = made_k.astype(BF16)
                 dv_s[rows, cols] = made_v.astype(BF16)
 
-                @pl.when(m < 9)
-                def _(m=m):
-                    for e in range(2):
-                        at = 2 * m + e
-                        j = at % 3
-                        big.turn(j, rise(j), 2 + at // 3, j == 0)
-
-                @pl.when(m == 4)
-                def _():
-                    mate_big(4, go_s.at[:, theirs]).wait_recv()
-
-                @pl.when((m >= 4) & (m < 12))
-                def _(m=m):
-                    big.turn(3, 4, m - 4, False)
+                run(big_at, 8 + (9 * m) // 4, 8 + (9 * (m + 1)) // 4)
 
                 @pl.when(m == 9)
                 def _():
@@ -1022,11 +1108,6 @@
                 def _(m=m):
                     for e in range(2):
                         group.give(1 - rep, 2 * (m - 9) + e)
-
-                @pl.when(m >= 12)
-                def _(m=m):
-                    for e in range(2):
-                        group.turn(0, rep, 2 * (m - 12) + e, True)
 
         @pl.when(g == 3)
         def _():
@@ -1039,9 +1120,7 @@
         own_g[g, :, :, :, 512:768] = dot_tn(rnd_s[...], dv_s[:, cols]).astype(BF16).reshape(NC, 2, 64, 256)
         mate_group(g).start()
 
-    mate_group(2).wait_recv()
-    for n in range(2):
-        group.turn(1, 2, n, False)
+    run(group_at, 0, 6)
     for i in range(3):
         weights_in(i).wait()
     tok_load.wait()
@@ -1056,14 +1135,17 @@
     gctx = dot_nt(dk_s[after, :], k_s[0:1024, :]) + dot_nt(dv_s[after, :], v_s[0:1024, :])
     gctx_s[...] = gctx
     xhat, _ = norm_parts(wo_s[pl.ds(BLK - CTX, CTX), :].astype(F32))
-    gskip_o[...] = jnp.sum(gctx * (xhat * fg[...] + fb[...]), axis=0, keepdims=True)
-    mate_group(3).wait_recv()
-    for n in range(2):
-        group.turn(2, 3, n, False)
+    sum_s[32:48, :] = jnp.zeros((16, 1024), F32)
+    sum_s[34:35, :] = jnp.sum(gctx * (xhat * fg[...] + fb[...]), axis=0, keepdims=True)
+    for at, vector in ((35, gsg), (36, gsb), (37, gdb)):
+        sum_s[at : at + 1, :] = vector[...]
+    for at in range(4):
+        sum_s[38 + at : 39 + at, :] = gub[:, at * 1024 : (at + 1) * 1024]
+    run(group_at, 6, 9)
     states, raw = st_in[...], u_in[...]
-    factor = jnp.exp(-decay[...])
+    factor = jnp.exp(-column(decay[...]))
     scale = jnp.sqrt(1.0 - factor * factor)
-    gso_o[...] = lax.dot_general(
+    sum_s[16:32, :] = lax.dot_general(
         states[:, BLK - CTX :], gctx, (((1,), (0,)), ((), ())),
         preferred_element_type=F32, precision=lax.Precision.HIGHEST,
     )
@@ -1076,9 +1158,9 @@
     lane = lax.broadcasted_iota(jnp.int32, lam.shape, 1)
     earlier = jnp.where(lane >= 1, pltpu.roll(states, 1, 1), 0.0)
     rates = -factor * jnp.sum(lam * (earlier - (factor / scale) * raw), axis=1, keepdims=True)
-    grate_o[...] = jnp.broadcast_to(rates, grate_o.shape)
+    sum_s[48:64, :] = jnp.broadcast_to(rates, (16, 1024))
     driven = scale * lam
-    gsi_o[...] = split_dot(dot_nn, driven, rnd_s[0:BLK, :], 3)
+    sum_s[0:16, :] = split_dot(dot_nn, driven, rnd_s[0:BLK, :], 3)
     gd_s[...] = jnp.zeros(gd_s.shape, F32)
     gd_s[0:16, 0:BLK] = driven
 
@@ -1109,18 +1191,14 @@
             half = pl.ds(128, CTX)
             nb_s[half, :] = nb_s[half, :] + skip[...] * gctx_s[...]
 
-        @pl.when(at < 3)
-        def _():
-            for e in range(2):
-                group.turn(1, 2, 2 + 2 * at + e, False)
-                group.turn(2, 3, 2 + 2 * at + e, False)
+        run(group_at, 9 + 3 * at, 12 + 3 * at)
 
         xhat, inverse = norm_parts(wo_s[rows, :].astype(F32))
         grad = nb_s[...]
         gain = jnp.sum(grad * xhat, axis=0, keepdims=True)
         shift = jnp.sum(grad, axis=0, keepdims=True)
-        gfg_o[...] = jnp.where(at == 0, gain, gfg_o[...] + gain)
-        gfb_o[...] = jnp.where(at == 0, shift, gfb_o[...] + shift)
+        sum_s[32:33, :] = sum_s[32:33, :] + gain
+        sum_s[33:34, :] = sum_s[33:34, :] + shift
         grad = grad * fg[...]
         grad = grad - jnp.mean(grad, axis=-1, keepdims=True) - xhat * jnp.mean(
             grad * xhat, axis=-1, keepdims=True
@@ -1129,9 +1207,21 @@
         rnd_s[rows, :] = (gres_s[at % 2].astype(F32) + inverse * grad).astype(BF16)
         leave(at).start()
 
-    for j in range(3):
-        big.finish(rise(j)).wait_send()
-    big.finish(4).wait_send()
+    each_device(lambda away: share(away).start())
+    part_s[...] = sum_s[tile(me)]
+    run(group_at, 21, 24)
+
+    def add_in(away):
+        share(away).wait_recv()
+        part_s[...] = part_s[...] + got_s[away]
+
+    each_device(add_in)
+    each_device(lambda away: spread(away).start())
+    sums_o[tile(me)] = part_s[...]
+    run(group_at, 24, 30)
+
+    for which in (3 * rep, 1, 2, 4):
+        big.finish(which).wait_send()
     for which in (rep, 2, 3):
         group.finish(which).wait_send()
     twin_rise = 3 * (1 - rep)
@@ -1139,19 +1229,19 @@
         big.finish(which).wait_recv()
     for which in (1 - rep, 2, 3):
         group.finish(which).wait_recv()
-    for i in range(4):
-        dup_o[:, i * 1024 : (i + 1) * 1024] = fin_b[i].astype(F32) + finr_b[i].astype(F32)
-    do_o[...] = fin_b[4].astype(F32) + finr_b[4].astype(F32)
-    for g in range(4):
-        for i, out in enumerate((dq_o, dk_o, dv_o)):
-            cols = slice(i * 256, (i + 1) * 256)
-            out[:, g * 256 : (g + 1) * 256] = fin_g[g, :, cols].astype(F32) + finr_g[g, :, cols].astype(F32)
-
+    for source, target in ((fin_b, finb_o), (finr_b, finrb_o), (fin_g, fing_o), (finr_g, finrg_o)):
+        target[...] = source[...]
+
+    def settle(away):
+        spread(away).wait()
+        share(away).wait_send()
+
+    each_device(settle)
     for i in range(4):
         mate_big(i, dwup.at[i, :, theirs]).wait_send()
         mate_group(i).wait_send()
         leave(i).wait()
-    mate_big(4, go_s.at[:, theirs]).wait_send()
+    mate_big(4, go_s).wait_send()
 
     @pl.loop(0, NC)
     def _(n):
@@ -1166,7 +1256,7 @@
             group.ring(slot, 0, n).wait_send()
 
 
-def run_backward(dwup, gatt, att, wall, q, kx, vx, rnd, p, tok, sio, u, st, fg, fb, skip, decay):
+def run_backward(*operands):
     shape = jax.ShapeDtypeStruct
     dma = pltpu.SemaphoreType.DMA
     vmem = pltpu.VMEM
@@ -1178,92 +1268,78 @@
         backward_kernel,
         name="backward_part",
         out_shape=(
-            shape(full, BF16), shape((64, 4096), F32), shape(part, F32), shape(part, F32),
-            shape(part, F32), shape(part, F32), shape((1, 1024), F32), shape((1, 1024), F32),
-            shape((1, 1024), F32), shape((16, 1024), F32), shape((16, 1024), F32), shape((16, 128), F32),
+            shape(full, BF16), shape((5,) + part, BF16), shape((5,) + part, BF16),
+            shape((4,) + cut, BF16), shape((4,) + cut, BF16), shape((64, 1024), F32),
         ),
-        in_specs=any_spec(11) + vmem_spec(6),
-        out_specs=any_spec(1) + vmem_spec(11),
+        in_specs=any_spec(11) + vmem_spec(10),
+        out_specs=any_spec(1) + vmem_spec(5),
         scratch_shapes=[
-            vmem((4, NC) + part, BF16), vmem((5, NC) + part, BF16), vmem((4, NC - 1) + part, BF16),
+            vmem((5, NC) + part, BF16), vmem((5, NC) + part, BF16), vmem((4, NC - 1) + part, BF16),
             vmem((NC,) + part, BF16), vmem((5,) + part, BF16), vmem((5,) + part, BF16), vmem(part, F32),
             vmem((4, NC, 2) + cut, BF16), vmem((4, NC) + cut, BF16), vmem((3, NC - 1) + cut, BF16),
             vmem((NC,) + cut, BF16), vmem((4,) + cut, BF16), vmem((4,) + cut, BF16), vmem(cut, F32),
-            vmem((NC, 2) + part, BF16),
+            vmem((NC,) + part, BF16),
             vmem(full, BF16), vmem(full, BF16), vmem(full, BF16), vmem(full, BF16), vmem(full, BF16),
             vmem(ext, BF16), vmem(ext, BF16), vmem(ext, BF16), vmem(ext, BF16), vmem(ext, BF16),
             vmem((2, BLK, CTX + BLK), BF16), vmem((BLK, CTX + BLK), BF16), vmem((2, 256, 1024), BF16),
             vmem((256, 1024), F32), vmem((1024, 128), BF16), vmem((128, 1024), F32), vmem((CTX, 1024), F32),
+            vmem((64, 1024), F32), vmem((4 * NC, 16, 128), F32), vmem((16, 128), F32),
             dma((12,)), dma((2,)), dma((2,)), dma((4,)), dma((5,)), dma((5,)), dma((4,)), dma((4,)),
             dma((4, NC - 1)), dma((4, NC - 1)), dma((3, NC - 1)), dma((3, NC - 1)),
             dma((NC,)), dma((NC,)), dma((NC,)), dma((NC,)), dma((5,)), dma((5,)), dma((4,)), dma((4,)),
+            dma((4 * NC,)), dma((4 * NC,)), dma((4 * NC,)), dma((4 * NC,)),
         ],
         compiler_params=pltpu.CompilerParams(
             collective_id=2, has_side_effects=True, vmem_limit_bytes=VMEM_LIMIT
         ),
-    )(dwup, gatt, att, wall, q, kx, vx, rnd, p, tok, sio, u, st, fg, fb, skip, decay)
-
-
-def small_kernel(x, out, got, here, ss, sr, bs, br):
+    )(*operands)
+
+
+def outputs_kernel(
+    finb, finrb, fing, finrg, find, findr, sums,
+    dup_o, do_o, dq_o, dk_o, dv_o, ddown_o, gfg_o, gfb_o, gskip_o, gsg_o, gsb_o, gdb_o, gub_o, grate_o,
+    gsi_o, gso_o,
+):
     rep, shard = lax.axis_index("rep"), lax.axis_index("shard")
-    me = rep * 16 + shard
-
-    def device(away):
-        other = (me + away) % 32
-        return other, (other // 16, other % 16)
-
-    barrier = pltpu.get_barrier_semaphore()
-
-    @pl.loop(1, 32)
-    def _(away):
-        pl.semaphore_signal(barrier, inc=1, device_id=device(away)[1], device_id_type=MESH)
-
-    pl.semaphore_wait(barrier, 31)
-
-    def share(away):
-        other, where = device(away)
-        return rcopy(x.at[other], got.at[away], ss.at[away], sr.at[away], where)
-
-    def spread(away):
-        return rcopy(here, out.at[me], bs.at[away], br.at[away], device(away)[1])
-
-    @pl.loop(1, 32)
-    def _(away):
-        share(away).start()
-
-    here[...] = x[me]
-
-    @pl.loop(1, 32)
-    def _(away):
-        share(away).wait_recv()
-        here[...] = here[...] + got[away]
-
-    @pl.loop(1, 32)
-    def _(away):
-        spread(away).start()
-
-    out[me] = here[...]
-
-    @pl.loop(1, 32)
-    def _(away):
-        spread(away).wait()
-        share(away).wait_send()
-
-
-def run_small(x):
-    dma = pltpu.SemaphoreType.DMA
+    for i in range(4):
+        dup_o[:, i * 1024 : (i + 1) * 1024] = finb[i].astype(F32) + finrb[i].astype(F32)
+    do_o[...] = finb[4].astype(F32) + finrb[4].astype(F32)
+    for g in range(4):
+        for i, out in enumerate((dq_o, dk_o, dv_o)):
+            cols = slice(i * 256, (i + 1) * 256)
+            out[:, g * 256 : (g + 1) * 256] = fing[g, :, cols].astype(F32) + finrg[g, :, cols].astype(F32)
+    mine = pl.ds(pl.multiple_of(rep * 64, 64), 192)
+    theirs = pl.ds(pl.multiple_of((1 - rep) * 64, 64), 192)
+    ddown_o[...] = jnp.zeros((256, 1024), F32)
+    ddown_o[mine, :] = find[...].astype(F32)
+    ddown_o[theirs, :] = ddown_o[theirs, :] + findr[...].astype(F32)
+    for at, out in enumerate((gfg_o, gfb_o, gskip_o, gsg_o, gsb_o, gdb_o)):
+        out[...] = sums[32 + at : 33 + at, :]
+    for at in range(4):
+        gub_o[:, at * 1024 : (at + 1) * 1024] = sums[38 + at : 39 + at, :]
+    same = lax.broadcasted_iota(jnp.int32, (16, 128), 0) == lax.broadcasted_iota(jnp.int32, (16, 128), 1)
+    grate_o[...] = jnp.sum(jnp.where(same, sums[48:64, 0:128], 0.0), axis=0, keepdims=True)
+    shift = (1024 - 64 * shard) % 1024
+    gsi_o[...] = pltpu.roll(sums[0:16, :], shift, 1)[:, 0:64]
+    gso_o[...] = pltpu.roll(sums[16:32, :], shift, 1)[:, 0:64]
+
+
+def run_outputs(*operands):
+    shape = jax.ShapeDtypeStruct
+    row = shape((1, 1024), F32)
+    part = shape((64, 1024), F32)
     return pl.pallas_call(
-        small_kernel,
-        name="small_sums",
-        out_shape=jax.ShapeDtypeStruct((32, 16, 128), F32),
-        in_specs=vmem_spec(1),
-        out_specs=vmem_spec(1)[0],
-        scratch_shapes=[
-            pltpu.VMEM((32, 16, 128), F32), pltpu.VMEM((16, 128), F32),
-            dma((32,)), dma((32,)), dma((32,)), dma((32,)),
-        ],
-        compiler_params=pltpu.CompilerParams(collective_id=3, has_side_effects=True),
-    )(x)
+        outputs_kernel,
+        name="outputs_part",
+        out_shape=(
+            shape((64, 4096), F32), part, part, part, part, shape((256, 1024), F32),
+            row, row, row, row, row, row, shape((1, 4096), F32), shape((1, 128), F32),
+            shape((16, 64), F32), shape((16, 64), F32),
+        ),
+        in_specs=vmem_spec(7),
+        out_specs=vmem_spec(16),
+        compiler_params=pltpu.CompilerParams(vmem_limit_bytes=VMEM_LIMIT),
+    )(*operands)
 
 
 def fused_device(
@@ -1273,39 +1349,28 @@
 ):
     tok = tokens.reshape(1024, 1024)
     cot = cotangent.reshape(1024, 1024)
-    fg, fb, skip, sg, sb, dnb, upb = (
+    fg, fb, skip, sg, sb, dnb, upb, decay = (
         v.reshape(1, -1)
-        for v in (first_gain, first_bias, skip_gain, second_gain, second_bias, down_bias, up_bias)
-    )
-    decay = decay_rates.reshape(16, 1)
-    live = jnp.broadcast_to(lengths.reshape(1, 1), (1, 1024))
-    sio = jnp.concatenate([state_in.T, state_out.T, jnp.zeros((64, 96), BF16)], axis=1)
-    wall, sio_all, rnd, q, kx, vx, att, res, sec, p, u, st = run_forward(
-        tok, query_weight, key_weight, value_weight, output_weight, up_weight, sio,
+        for v in (
+            first_gain, first_bias, skip_gain, second_gain, second_bias, down_bias, up_bias, decay_rates,
+        )
+    )
+    wall, sio, rnd, q, kx, vx, att, res, sec, p, u, st = run_forward(
+        tok, query_weight, key_weight, value_weight, output_weight, up_weight, state_in, state_out,
         fg, fb, skip, sg, sb, decay,
     )
-    result, gatt, dwup, piece_down, gdb, gub, gsg, gsb = run_feed(
-        sec, res, wall, down_weight, cot, live, upb, dnb, sg
-    )
-    gtok, piece_up, piece_out, piece_q, piece_k, piece_v, gfg, gfb, gskip, gsi, gso, grate = run_backward(
-        dwup.reshape(4, NC, 2, 64, 1024), gatt, att, wall, q, kx, vx, rnd, p, tok, sio_all,
-        u, st, fg, fb, skip, decay,
-    )
-    flat = jnp.concatenate(
-        [gfg[0], gfb[0], gskip[0], gsg[0], gsb[0], gdb[0], gub[0], gsi.reshape(-1), gso.reshape(-1)]
-        + [grate[:, 0], jnp.zeros((65536 - 10 * 1024 - 2 * 16384 - 16,), F32)]
-    )
-    total = run_small(flat.reshape(32, 16, 128)).reshape(-1)
-    row = [total[i * 1024 : (i + 1) * 1024] for i in range(6)]
-    shard = lax.axis_index("shard")
-    mine = [
-        lax.dynamic_slice(total[at : at + 16384].reshape(16, 1024), (0, shard * 64), (16, 64))
-        for at in (10240, 26624)
-    ]
+    result, gatt, dwup, find, findr, gdb, gub, gsg, gsb = run_feed(
+        sec, res, wall, down_weight, cot, lengths, upb, dnb, sg
+    )
+    gtok, finb, finrb, fing, finrg, sums = run_backward(
+        dwup.reshape(4, NC, 2, 64, 1024), gatt, att, wall, q, kx, vx, rnd, p, tok, sio,
+        u, st, fg, fb, skip, decay, gsg, gsb, gdb, gub,
+    )
+    dup, do, dq, dk, dv, ddown, *rest = run_outputs(finb, finrb, fing, finrg, find, findr, sums)
+    gfg, gfb, gskip, gsg, gsb, gdb, gub, grate, gsi, gso = rest
     return (
-        result.reshape(1, 1024, 1024), gtok.reshape(1, 1024, 1024), row[0], row[1],
-        total[43008:43024], mine[0], mine[1], row[2], piece_q, piece_k, piece_v, piece_out,
-        row[3], row[4], piece_up, total[6144:10240], piece_down, row[5],
+        result.reshape(1, 1024, 1024), gtok.reshape(1, 1024, 1024), gfg[0], gfb[0],
+        grate[0, 0:16], gsi, gso, gskip[0], dq, dk, dv, do, gsg[0], gsb[0], dup, gub[0], ddown, gdb[0],
     )
 
 

time: 377 us -> 321 us (0.85)
  Pallas kernels: 345 us -> 313 us
  local copies, waits for them, and re-layouts: 29.2 us -> 5.72 us
    pallas_call x1, Pallas kernels: 21.8 us -> 3.63 us  [run_outputs(): pl.pallas_call(outputs_kernel, name='outputs_part', out_shape=(shape((64,...]
    concatenate x2 -> x0, local copies, waits for them, and re-layouts: 9.1 us -> none  [the longest x1 9.02 us: fused_device(): jnp.concatenate([gfg[0], gfb[0], gskip[0], gsg[0], gsb[0], gdb[0], gub[0]...]
    pallas_call x1, Pallas kernels: 121 us -> 112 us  [run_feed(): pl.pallas_call(feed_kernel, name='feed_part', out_shape=(shape(big, BF16)...]
    unnamed x36 -> x4, local copies, waits for them, and re-layouts: 11.9 us -> 4.55 us
    slice x5 -> x0, local copies, waits for them, and re-layouts: 5.52 us -> none  [the longest x1 1.32 us: fused_device(): total[6144:10240]]
    pallas_call x1, Pallas kernels: 111 us -> 106 us  [run_backward(): pl.pallas_call(backward_kernel, name='backward_part', out_shape=(shape(fu...]
where the time goes in v2:
time: 321 us; the launch traced here: 320 us
  Pallas kernels  313 us (98%)
  local copies, waits for them, and re-layouts  5.72 us (2%)
    pallas_call x1, Pallas kernels, run_feed(): pl.pallas_call(feed_kernel, name='feed_part', out_shape=(shape(big, BF16)...  112 us
    pallas_call x1, Pallas kernels, run_backward(): pl.pallas_call(backward_kernel, name='backward_part', out_shape=(shape(fu...  106 us
    pallas_call x1, Pallas kernels, run_forward(): pl.pallas_call(forward_kernel, name='forward_part', out_shape=(shape((8,)...  91 us

profile of v2, /device:TPU:0, one launch (start us, length us, event | category | flops | bytes accessed | tf_op | source)
XLA Modules:
  0.0 319.7 jit_solution(11447444016610683411)
XLA Ops:
  1.3 91.0 %forward_part.1 = (bf16[8,1024,1024]{2,1,0:T(8,128)(2,1)}, bf16[1024,128]{1,0:T(8,128)(2,1)}, bf16[1152,1024]{1,0:T(8,128)(2,1)}, bf16[1024,1024]{1,0:T(8,128)(2...) custom-call(bf16[1024,1024]{1,0:T(8,128)(2,1)} %bitcast.23, ...), custom_call_target="tpu_custom_call" | custom-call | tf_op jit(solution)/shard_map/forward_part/pallas_call | solution.py:435
  92.4 111.6 %feed_part.1 = (bf16[1024,1024]{1,0:T(8,128)(2,1)}, bf16[1024,1024]{1,0:T(8,128)(2,1)}, bf16[4,1024,1024]{2,1,0:T(8,128)(2,1)}, bf16[192,1024]{1,0:T(8,128)(2,1)...) custom-call(bf16[1024,1024]{1,0:T(8,128)(2,1)} %get-tuple-element.61, ...), custom_call_target="tpu_custom_call" | custom-call | tf_op jit(solution)/shard_map/feed_part/pallas_call | solution.py:795
  203.9 106.4 %backward_part.1 = (bf16[1024,1024]{1,0:T(8,128)(2,1)}, bf16[5,64,1024]{2,1,0:T(8,128)(2,1)}, bf16[5,64,1024]{2,1,0:T(8,128)(2,1)}, bf16[4,64,768]{2,1,0:T(8,128...) custom-call(bf16[4,8,2,64,1024]{4,3,2,1,0:T(8,128)(2,1)} %bitcast.22, ...), custom_call_target="tpu_custom_call" | custom-call | tf_op jit(solution)/shard_map/backward_part/pallas_call | solution.py:1267
  310.4 3.6 %outputs_part.1 = (f32[64,4096]{1,0:T(8,128)}, f32[64,1024]{1,0:T(8,128)}, f32[64,1024]{1,0:T(8,128)}, f32[64,1024]{1,0:T(8,128)}, f32[64,1024]{1,0:T(8,128)}, /...) custom-call(bf16[5,64,1024]{2,1,0:T(8,128)(2,1)} %get-tuple-element., ...), custom_call_target="tpu_custom_call" | custom-call | tf_op jit(solution)/shard_map/outputs_part/pallas_call | solution.py:1331
  314.0 1.2 slice_bitcast_fusion
  315.2 0.0 copy-start
  315.2 3.2 %copy.40 = bf16[1,1024,1024]{2,1,0:T(8,128)(2,1)} copy(bf16[1,1024,1024]{2,1,0:T(8,128)(2,1)} %bitcast.26) | data formatting | bytes 4194304
  318.4 0.0 copy-done
  318.4 1.3 copy.41
Async XLA Ops:
  315.2 3.2 %copy-start = (bf16[1024,1024]{1,0:T(8,128)(2,1)S(1)}, bf16[1024,1024]{1,0:T(8,128)(2,1)}, u32[]{:S(2)}) copy-start(bf16[1024,1024]{1,0:T(8,128)(2,1)} %get-tuple-element.80) | copy-start | bytes 6291460

commit v3 on v2

--- a/solution.py
+++ b/solution.py
@@ -107,10 +107,10 @@
 
 
 def forward_kernel(
-    tok, wq, wk, wv, wo, wup, s_in, s_out, fg, fb, skip, sg, sb, decay,
-    wall, sio_all, rnd_o, q_o, k_o, v_o, att_o, res_o, sec_o, p_o, u_o, st_o,
+    tok, wq, wk, wv, wo, wup, wdn, s_in, s_out, fg, fb, skip, sg, sb, decay,
+    wall, wdpre, sio_all, rnd_o, q_o, k_o, v_o, att_o, res_o, sec_o, p_o, u_o, st_o,
     tok_s, rnd_s, w_s, q_s, k_s, v_s, att_s, res_s, sec_s, pbuf, nctx, sio_s,
-    own_s, sio_own, loc, rs, rr, ss, sr, cs, cr, xs, xr, outs, psem,
+    own_s, sio_own, loc, rs, rr, ss, sr, cs, cr, xs, xr, outs, psem, ds, dr,
 ):
     net = Net()
     rep, core = net.rep, net.core
@@ -145,7 +145,7 @@
         if isinstance(slot, int) and slot < 2:
             return 1 if slot else 2 * rep
         later = slot - 2
-        return 3 + later + 3 * rep * ((later % 2) * (3 - later) // 2)
+        return 3 + later + (1 + 3 * rep) * ((3 - later) // 3) - (later % 2) * (3 - later) // 2
 
     def ring(slot, way, hop, which, where):
         ref = wall.at[which, where]
@@ -173,6 +173,9 @@
     def twin(turn, index, which, where):
         ref = wall.at[which, where]
         return rcopy(ref, ref, xs.at[turn, index], xr.at[turn, index], net.twin)
+
+    hand = rcopy(wdn, wdpre.at[0], ds.at[0], dr.at[0], net.along(1))
+    hand_on = rcopy(wdpre.at[0], wdpre.at[1], ds.at[1], dr.at[1], net.mate)
 
     def source(way, hop):
         return block(net.at((2 * way - 1) * (hop + 1), core))
@@ -217,42 +220,53 @@
         normed = xhat * fg[...] + fb[...]
         rnd_s[rows, :] = normed.astype(BF16)
 
-    turns = [(hop, way) for hop in range(4) for way in range(2) if hop < 4 - way]
-    for n, (hop, way) in enumerate(turns):
-        first_norm(n)
-        serve(0, way, hop)
-        serve_out(0, 0, way, hop)
-        serve(1, way, hop)
-        where = source(way, hop)
-        ring_small(way, hop, where).wait_recv()
-        if hop < 3 - way:
-            ring_small(way, hop + 1, where).start()
-        mate_small(1 + 2 * hop + way, where).start()
-        if n >= 2:
-            serve(2, turns[n - 2][1], turns[n - 2][0])
-        if n in (0, 2, 4, 5):
-            for each in range(2):
-                ring_own({0: 2, 2: 3, 4: 4, 5: 5}[n], each)
-        if n >= 3:
-            serve_in(0, turns[n - 3][1], turns[n - 3][0])
+    order = [
+        (hop, slot, way) for hop in range(4) for slot in range(2) for way in range(2) if hop < 4 - way
+    ]
+    owed = []
+    for n, (hop, slot, way) in enumerate(order):
+        if n % 2 == 0:
+            first_norm(n // 2)
+        serve(slot, way, hop)
+        if slot == 0:
+            serve_out(0, 0, way, hop)
+            owed.append((n, way, hop))
+        else:
+            where = source(way, hop)
+            ring_small(way, hop, where).wait_recv()
+            if hop < 3 - way:
+                ring_small(way, hop + 1, where).start()
+            mate_small(1 + 2 * hop + way, where).start()
+        if n in (10, 12):
+            for later in range(2):
+                for each in range(2):
+                    ring_own(n - 8 + later, each)
+        if owed and n - owed[0][0] >= 6:
+            serve_in(0, *owed.pop(0)[1:])
     first_norm(7)
-    for hop, way in turns[-3:]:
-        serve_in(0, way, hop)
+    for each in owed:
+        serve_in(0, *each[1:])
 
     def event(m):
-        later = (m - 2 + 3) // 3 - 1
-        turn = (5 + m) * (1 - (m + 20) // 22) + later * ((m + 20) // 22)
-        slot = 2 + ((m + 20) // 22) * (1 + (m + 1) % 3)
-        hop, way = turn // 2, turn % 2
+        half, place = m // 14, m % 14
+        late = place // 12
+        hop = place // 4
+        index = ((place % 4) // 2) * (1 - late) + (place - 12) * late
+        way = (place % 2) * (1 - late)
+        slot = 2 + 2 * half + index
         serve(slot, way, hop)
 
-        @pl.when(slot == 3)
-        def _():
-            serve_out(3, 1, way, hop)
-
-        @pl.when((slot == 5) & (turn >= 2))
-        def _():
-            serve_in(1, way, hop - 1)
+        @pl.when(slot == 2)
+        def _():
+            serve_out(2, 1, way, hop)
+
+        @pl.when(m == 10)
+        def _():
+            hand.start()
+
+        @pl.when((m >= 8) & (m <= 20) & (m % 4 < 2))
+        def _():
+            serve_in(1, m % 2, (m - 8) // 4)
 
     xhat, _ = norm_parts(tok_s[pl.ds(BLK - CTX, CTX), :].astype(F32))
     nctx[...] = xhat * fg[...] + fb[...]
@@ -355,9 +369,7 @@
                 att_s[rows, cols] = mixed.astype(BF16)
             p_copy(slot, b * 8 + h).start()
 
-            @pl.when(h < 5)
-            def _(b=b, h=h):
-                event(8 + 5 * b + h)
+            event(8 + 8 * b + h)
 
     finals.append(pltpu.make_async_copy(att_s, att_o, outs.at[4]))
     finals[-1].start()
@@ -379,9 +391,13 @@
         sec_s[rows, :] = (xhat * sg[...] + sb[...]).astype(BF16)
         pltpu.make_async_copy(res_s.at[rows], res_o.at[rows], outs.at[5 + at]).start()
         pltpu.make_async_copy(sec_s.at[rows], sec_o.at[rows], outs.at[9 + at]).start()
-        event(18 + at)
-
-    event(22)
+        event(24 + at)
+
+        @pl.when(at == 0)
+        def _():
+            hand.wait_recv()
+            hand_on.start()
+
     for copy in finals:
         copy.wait()
     for at in range(4):
@@ -391,8 +407,8 @@
     for slot in range(2):
         p_copy(slot, slot).wait()
 
-    serve_in(1, 1, 2)
-    serve_in(1, 0, 3)
+    hand.wait_send()
+    hand_on.wait()
 
     @pl.loop(0, NC)
     def _(index):
@@ -427,7 +443,7 @@
     return [pl.BlockSpec(memory_space=pltpu.VMEM)] * n
 
 
-def run_forward(tok, wq, wk, wv, wo, wup, s_in, s_out, fg, fb, skip, sg, sb, decay):
+def run_forward(tok, wq, wk, wv, wo, wup, wdn, s_in, s_out, fg, fb, skip, sg, sb, decay):
     shape = jax.ShapeDtypeStruct
     dma = pltpu.SemaphoreType.DMA
     big = (1024, 1024)
@@ -436,13 +452,14 @@
         forward_kernel,
         name="forward_part",
         out_shape=(
-            shape((8,) + big, BF16), shape((1024, 128), BF16), shape(ext, BF16), shape(big, BF16),
+            shape((8,) + big, BF16), shape((2, 256, 1024), BF16), shape((1024, 128), BF16),
+            shape(ext, BF16), shape(big, BF16),
             shape(ext, BF16), shape(ext, BF16), shape(big, BF16), shape(big, F32),
             shape(big, BF16), shape((16, BLK, CTX + BLK), BF16), shape((16, BLK), F32),
             shape((16, BLK), F32),
         ),
-        in_specs=any_spec(6) + vmem_spec(8),
-        out_specs=any_spec(10) + vmem_spec(2),
+        in_specs=any_spec(7) + vmem_spec(8),
+        out_specs=any_spec(11) + vmem_spec(2),
         scratch_shapes=[
             pltpu.VMEM(big, BF16), pltpu.VMEM(ext, BF16), pltpu.VMEM((4,) + big, BF16),
             pltpu.VMEM(big, BF16), pltpu.VMEM(ext, BF16), pltpu.VMEM(ext, BF16),
@@ -451,12 +468,12 @@
             pltpu.VMEM((1024, 128), BF16),
             pltpu.VMEM((8, 64, 1024), BF16), pltpu.VMEM((64, 128), BF16),
             dma((10,)), dma((6, 2, 4)), dma((6, 2, 4)), dma((2, 4)), dma((2, 4)),
-            dma((9, NC)), dma((9, NC)), dma((2, NC - 1)), dma((2, NC - 1)), dma((13,)), dma((2,)),
+            dma((9, NC)), dma((9, NC)), dma((2, NC - 1)), dma((2, NC - 1)), dma((13,)), dma((2,)), dma((2,)), dma((2,)),
         ],
         compiler_params=pltpu.CompilerParams(
             collective_id=0, has_side_effects=True, vmem_limit_bytes=VMEM_LIMIT
         ),
-    )(tok, wq, wk, wv, wo, wup, s_in, s_out, fg, fb, skip, sg, sb, decay)
+    )(tok, wq, wk, wv, wo, wup, wdn, s_in, s_out, fg, fb, skip, sg, sb, decay)
 
 
 GELU_C = math.sqrt(2.0 / math.pi)
@@ -464,11 +481,11 @@
 
 
 def feed_kernel(
-    sec, res, wall, wdn, cot, live, upb, dnb, sg,
-    out_o, gatt_o, dwup_o, fin_o, finr_o, gdb_o, gub_o, gsg_o, gsb_o,
+    sec, res, wall, wdn, wdpre, cot, live, upb, dnb, sg,
+    out_o, gatt_o, dwown_o, dwmate_o, fin_o, gdb_o, gub_o, gsg_o, gsb_o,
     sec_s, gb_s, wup_s, wd_s, br_s, gs_s, act_s, gh_s, a_s, b_s, prec, rrec, rsend, xsend, xrec,
-    xfs, xfr, dwup_s, own_s, res_s,
-    loc, ars, arr, axs, axr, cas, car, cxs, cxr, ps, pr, rs, rr, xs, xr, fs, fr, outs, dsem,
+    dwup_s, own_s, res_s,
+    loc, ars, arr, axs, axr, cas, car, cxs, cxr, ps, pr, rs, rr, xs, xr, outs, dsem, dms, dmr,
 ):
     net = Net()
     rep, core = net.rep, net.core
@@ -496,12 +513,15 @@
         pltpu.make_async_copy(wdn, own_s, loc.at[0]),
         pltpu.make_async_copy(sec, sec_s, loc.at[1]),
         pltpu.make_async_copy(cot, gb_s, loc.at[2]),
+        pltpu.make_async_copy(wdpre.at[0], wd_s.at[block(mine_at(0))], loc.at[7]),
+        pltpu.make_async_copy(wdpre.at[1], wd_s.at[block(other_at(0))], loc.at[8]),
     ]
     loads += [pltpu.make_async_copy(wall.at[4 + i], wup_s.at[i], loc.at[3 + i]) for i in range(4)]
     for load in loads:
         load.start()
     net.greet()
     loads[0].wait()
+    loads[3].wait()
 
     def gather(j, hop, shard):
         ref = wd_s.at[ring_part(shard, j)]
@@ -524,7 +544,7 @@
     for j in range(3):
         ring_own = own_s.at[pl.ds(pl.multiple_of((rep + j) * part, part), part)]
         target = wd_s.at[ring_part(here, j)]
-        rcopy(ring_own, target, ars.at[j, 0], arr.at[j, 0], ahead).start()
+        gather(j, 1, mine_at(0)).start()
         rcopy(ring_own, target, cas.at[j, 0], car.at[j, 0], net.mate).start()
     rcopy(sole_own, wd_s.at[sole_part(here, 1 - rep)], cxs.at[0], cxr.at[0], net.mate).start()
 
@@ -563,11 +583,8 @@
         br_s[rows, :] = jnp.zeros((256, 1024), F32)
         gs_s[rows, :] = jnp.zeros((256, 1024), F32)
 
-    for j in range(3):
-        serve((2 * rep + j) % 3, 0)
-    for load in loads[3:]:
+    for load in loads[4:]:
         load.wait()
-    serve_twin(0)
 
     def to_mate(step):
         slot = step % 2
@@ -579,10 +596,19 @@
     def to_twin(step):
         return rcopy(xsend.at[step % 2], xrec.at[step], xs.at[step], xr.at[step], net.twin)
 
+    def dwup_at(target, shard):
+        cols = pl.ds(pl.multiple_of((shard % 4) * 256, 256), 256)
+        return target.at[shard // 4, :, :, cols]
+
     def dwup_copy(slot, half, shard):
-        cols = pl.ds(pl.multiple_of((shard % 4) * 256, 256), 256)
         return pltpu.make_async_copy(
-            dwup_s.at[slot, half], dwup_o.at[shard // 4, :, cols], dsem.at[slot, half]
+            dwup_s.at[slot, half, :, core], dwup_at(dwown_o, shard), dsem.at[slot, half]
+        )
+
+    def dwup_mate(step, half, shard):
+        return rcopy(
+            dwup_s.at[step % 2, half, :, 1 - core], dwup_at(dwmate_o, shard),
+            dms.at[step, half], dmr.at[step, half], net.mate,
         )
 
     ring_local = pl.ds(pl.multiple_of(rep * part, part), ring_rows)
@@ -658,23 +684,25 @@
 
         @pl.loop(0, 2)
         def _(at):
+            middle(0, a, at)
+
+        @pl.when(step < NC - 2)
+        def _():
+            serve(2 * rep, step + 1)
+
+        @pl.when(step >= 1)
+        def _():
+            for j in range(3):
+                mate_ring(j, index, b).wait_recv()
+            mate_sole(index, b, 1 - rep).wait_recv()
+
+        @pl.loop(0, 2)
+        def _(at):
+            middle(1, b, at)
+
             @pl.when(step < NC - 2)
             def _():
-                serve((2 * rep + at) % 3, step + 1)
-
-            middle(0, a, at)
-
-        for j in range(3):
-            mate_ring(j, index, b).wait_recv()
-        mate_sole(index, b, 1 - rep).wait_recv()
-
-        @pl.loop(0, 2)
-        def _(at):
-            @pl.when((at == 0) & (step < NC - 2))
-            def _():
-                serve((2 * rep + 2) % 3, step + 1)
-
-            middle(1, b, at)
+                serve((2 * rep + 1 + at) % 3, step + 1)
 
         made = dot_tn(act_s[...], gb_s[...])
 
@@ -696,9 +724,11 @@
             @pl.when(step >= 2)
             def _(half=half, shard=shard):
                 dwup_copy(slot, half, shard).wait()
-
-            dwup_s[slot, half] = rise_up[:, half * 256 : half * 256 + 256]
+                dwup_mate(step - 2, half, shard).wait_send()
+
+            dwup_s[slot, half] = rise_up[:, half * 256 : half * 256 + 256].reshape(NC, 2, 64, 256)
             dwup_copy(slot, half, shard).start()
+            dwup_mate(step, half, shard).start()
 
         @pl.loop(0, 4)
         def _(at):
@@ -756,19 +786,17 @@
     for j in range(3):
         forward((2 * rep + 1 + j) % 3, NC - 1)
     last = (NC - 1) % 2
-    xfs[...] = a_s[last, ring_local, :].astype(BF16)
-    swap = rcopy(xfs, xfr, fs.at[0], fr.at[0], net.twin)
-    swap.start()
-    fin_o[...] = xfs[...]
-
-    @pl.loop(0, NC - 1)
+    fin_o[...] = a_s[last, ring_local, :].astype(BF16)
+
+    @pl.loop(1, NC - 1)
     def _(hop):
         for j in range(3):
             gather(j, hop, 0).wait_send()
         gather_twin(hop, 0, 0).wait_send()
 
-    @pl.loop(0, NC)
-    def _(index):
+    @pl.loop(1, NC)
+    def _(later):
+        index = (later + 1) % NC
         for j in range(3):
             mate_ring(j, index, 0).wait_send()
         mate_sole(index, 0, 0).wait_send()
@@ -780,14 +808,18 @@
             to_ring(j, step - 1).wait_send()
         for half in range(2):
             dwup_copy(step % 2, half, 0).wait()
+            dwup_mate(step, half, 0).wait_send()
     for at in range(4):
         for which in range(2):
             leave(at, which).wait()
-    swap.wait()
-    finr_o[...] = xfr[...]
-
-
-def run_feed(sec, res, wall, wdn, cot, live, upb, dnb, sg):
+
+    @pl.loop(0, NC)
+    def _(step):
+        for half in range(2):
+            dwup_mate(step, half, 0).wait_recv()
+
+
+def run_feed(sec, res, wall, wdn, wdpre, cot, live, upb, dnb, sg):
     shape = jax.ShapeDtypeStruct
     dma = pltpu.SemaphoreType.DMA
     vmem = pltpu.VMEM
@@ -796,40 +828,40 @@
         feed_kernel,
         name="feed_part",
         out_shape=(
-            shape(big, BF16), shape(big, BF16), shape((4,) + big, BF16),
-            shape((192, 1024), BF16), shape((192, 1024), BF16), shape((1, 1024), F32), shape((1, 4096), F32),
+            shape(big, BF16), shape(big, BF16), shape((4, NC, 64, 1024), BF16),
+            shape((4, NC, 64, 1024), BF16), shape((192, 1024), BF16), shape((1, 1024), F32), shape((1, 4096), F32),
             shape((1, 1024), F32), shape((1, 1024), F32),
         ),
-        in_specs=any_spec(5) + [pl.BlockSpec(memory_space=pltpu.SMEM)] + vmem_spec(3),
-        out_specs=any_spec(3) + vmem_spec(6),
+        in_specs=any_spec(6) + [pl.BlockSpec(memory_space=pltpu.SMEM)] + vmem_spec(3),
+        out_specs=any_spec(4) + vmem_spec(5),
         scratch_shapes=[
             vmem(big, BF16), vmem(big, BF16), vmem((4,) + big, BF16), vmem((4096, 1024), BF16),
             vmem(big, F32), vmem(big, F32), vmem((1024, 512), BF16), vmem((1024, 512), BF16),
             vmem((2, 256, 1024), F32), vmem((2, 256, 1024), BF16), vmem((NC, 256, 1024), BF16),
             vmem((NC - 1, 3, 64, 1024), BF16), vmem((2, 3, 64, 1024), BF16), vmem((2, 64, 1024), BF16),
-            vmem((NC, 64, 1024), BF16), vmem((192, 1024), BF16), vmem((192, 1024), BF16),
-            vmem((2, 2, 1024, 256), BF16), vmem((256, 1024), BF16), vmem(big, F32),
-            dma((7,)), dma((3, NC - 1)), dma((3, NC - 1)), dma((NC - 1,)), dma((NC - 1,)),
+            vmem((NC, 64, 1024), BF16),
+            vmem((2, 2, NC, 2, 64, 256), BF16), vmem((256, 1024), BF16), vmem(big, F32),
+            dma((9,)), dma((3, NC - 1)), dma((3, NC - 1)), dma((NC - 1,)), dma((NC - 1,)),
             dma((3, NC)), dma((3, NC)), dma((NC,)), dma((NC,)), dma((NC,)), dma((NC,)),
-            dma((NC - 1, 3)), dma((NC - 1, 3)), dma((NC,)), dma((NC,)), dma((1,)), dma((1,)),
-            dma((2, 4)), dma((2, 2)),
+            dma((NC - 1, 3)), dma((NC - 1, 3)), dma((NC,)), dma((NC,)),
+            dma((2, 4)), dma((2, 2)), dma((NC, 2)), dma((NC, 2)),
         ],
         compiler_params=pltpu.CompilerParams(
             collective_id=1, has_side_effects=True, vmem_limit_bytes=VMEM_LIMIT
         ),
-    )(sec, res, wall, wdn, cot, live, upb, dnb, sg)
+    )(sec, res, wall, wdn, wdpre, cot, live, upb, dnb, sg)
 
 
 def backward_kernel(
-    dwup, gatt, att, wall, q, kx, vx, rnd, p, tok, sio, u_in, st_in, fg, fb, skip, decay,
+    dwown, dwmate, find, gatt, att, wall, q, kx, vx, rnd, p, tok, sio, u_in, st_in, fg, fb, skip, decay,
     gsg, gsb, gdb, gub,
-    gtok_o, finb_o, finrb_o, fing_o, finrg_o, sums_o,
-    own_b, prec_b, rrec_b, xrec_b, fin_b, finr_b, acc_b,
-    own_g, prec_g, rrec_g, xrec_g, fin_g, finr_g, acc_g, go_s,
+    gtok_o, findr_o, fin_b, finr_b, fin_g, finr_g, sums_o,
+    own_b, prec_b, rrec_b, xrec_b, acc_b,
+    own_g, prec_g, rrec_g, xrec_g, acc_g, go_s,
     gatt_s, wo_s, att_s, ga_s, q_s, k_s, v_s, rnd_s, dk_s, dv_s, pbuf, ds_s, gres_s, nb_s,
     sio_s, gd_s, gctx_s, sum_s, got_s, part_s,
     loc, psem, gsem, osem, mbs, mbr, mgs, mgr, rbs, rbr, rgs, rgr, xbs, xbr, xgs, xgr,
-    fbs, fbr, fgs, fgr, ts, tr, us, ur,
+    fbs, fbr, fgs, fgr, ts, tr, us, ur, ds, dr,
 ):
     net = Net()
     rep, core = net.rep, net.core
@@ -845,7 +877,10 @@
         pltpu.make_async_copy(rnd, rnd_s, loc.at[6]),
         pltpu.make_async_copy(sio, sio_s, loc.at[7]),
     ]
-    rises = [pltpu.make_async_copy(dwup.at[i, :, core], own_b.at[i], loc.at[8 + i]) for i in range(4)]
+    rises = [
+        pltpu.make_async_copy(dwown, own_b.at[pl.ds(0, 4)], loc.at[8]),
+        pltpu.make_async_copy(dwmate, prec_b.at[pl.ds(0, 4)], loc.at[9]),
+    ]
     for copy in rises:
         copy.start()
     for copy in loads:
@@ -867,14 +902,13 @@
 
     pl.semaphore_wait(barrier, 4 * NC - 1)
 
-    def mate_big(which, source):
-        return rcopy(source, prec_b.at[which], mbs.at[which], mbr.at[which], net.mate)
+    mate_out = rcopy(go_s, prec_b.at[4], mbs.at[0], mbr.at[0], net.mate)
 
     def mate_group(g):
         return rcopy(own_g.at[g, :, theirs], prec_g.at[g], mgs.at[g], mgr.at[g], net.mate)
 
-    for i in (1, 2, 3 * (1 - rep), 3 * rep):
-        mate_big(i, dwup.at[i, :, theirs]).start()
+    swap = rcopy(find, findr_o, ds.at[0], dr.at[0], net.twin)
+    swap.start()
 
     def chip_for(n):
         t, way = n // 2, n % 2
@@ -963,8 +997,7 @@
         return rcopy(part_s, sums_o.at[tile(me)], us.at[away], ur.at[away], device(away)[1])
 
     def each_device(act):
-        @pl.loop(1, 4 * NC)
-        def _(away):
+        for away in range(1, 4 * NC):
             act(away)
 
     def big_at(e):
@@ -972,9 +1005,9 @@
         n = k - 2 * (j // 2) - j // 3
         which = (j + 1) * (1 - j // 2) + (j // 2) * (3 * rep * (1 - j // 3) + 4 * (j // 3))
 
-        @pl.when((j >= 2) & (n == 0))
-        def _():
-            mate_big(which, dwup.at[0, :, theirs]).wait_recv()
+        @pl.when((j == 3) & (n == 0))
+        def _():
+            mate_out.wait_recv()
 
         @pl.when((n >= 0) & (n <= 7))
         def _():
@@ -982,7 +1015,7 @@
 
     def group_at(e):
         k, j = e // 3, e % 3
-        n = k - 2 * (j // 2)
+        n = k - j // 2
         which = rep * (1 - (j + 1) // 2) + (j + 1) * ((j + 1) // 2)
 
         @pl.when((j >= 1) & (n == 0))
@@ -998,6 +1031,14 @@
         def _(e):
             at(e)
 
+    for copy in rises:
+        copy.wait()
+
+    @pl.loop(0, NC)
+    def _(n):
+        big.give(3 * (1 - rep), n)
+
+    run(big_at, 0, 4)
     for i in range(2):
         loads[i].wait()
 
@@ -1011,17 +1052,7 @@
         rows = pl.ds(pl.multiple_of(at * 256, 256), 256)
         ga_s[rows, :] = dot_nt(gatt_s[rows, :], wo_s[...]).astype(BF16)
 
-    for copy in rises:
-        copy.wait()
-    for i in (1, 2):
-        mate_big(i, dwup.at[i, :, theirs]).wait_recv()
-    run(big_at, 0, 8)
-    mate_big(3 * (1 - rep), dwup.at[0, :, theirs]).wait_recv()
-
-    @pl.loop(0, NC)
-    def _(n):
-        big.give(3 * (1 - rep), n)
-
+    run(big_at, 4, 8)
     loads[2].wait()
 
     @pl.loop(0, 4)
@@ -1031,7 +1062,7 @@
         own_b[4, :, :, cols] = jnp.where(core == 0, made[:, 0], made[:, 1]).astype(BF16)
         go_s[:, :, cols] = jnp.where(core == 0, made[:, 1], made[:, 0]).astype(BF16)
 
-    mate_big(4, go_s).start()
+    mate_out.start()
     tok_load = pltpu.make_async_copy(tok, wo_s, loc.at[0])
     tok_load.start()
     for copy in loads[3:]:
@@ -1097,7 +1128,10 @@
                 dk_s[rows, cols] = made_k.astype(BF16)
                 dv_s[rows, cols] = made_v.astype(BF16)
 
-                run(big_at, 8 + (9 * m) // 4, 8 + (9 * (m + 1)) // 4)
+                @pl.when(m < 15)
+                def _(m=m):
+                    run(big_at, 8 + (5 * m) // 2, 8 + (5 * m + 5) // 2)
+
 
                 @pl.when(m == 9)
                 def _():
@@ -1120,7 +1154,7 @@
         own_g[g, :, :, :, 512:768] = dot_tn(rnd_s[...], dv_s[:, cols]).astype(BF16).reshape(NC, 2, 64, 256)
         mate_group(g).start()
 
-    run(group_at, 0, 6)
+    run(group_at, 0, 3)
     for i in range(3):
         weights_in(i).wait()
     tok_load.wait()
@@ -1141,7 +1175,7 @@
         sum_s[at : at + 1, :] = vector[...]
     for at in range(4):
         sum_s[38 + at : 39 + at, :] = gub[:, at * 1024 : (at + 1) * 1024]
-    run(group_at, 6, 9)
+    run(group_at, 3, 6)
     states, raw = st_in[...], u_in[...]
     factor = jnp.exp(-column(decay[...]))
     scale = jnp.sqrt(1.0 - factor * factor)
@@ -1164,6 +1198,10 @@
     gd_s[...] = jnp.zeros(gd_s.shape, F32)
     gd_s[0:16, 0:BLK] = driven
 
+    def add_in(away):
+        share(away).wait_recv()
+        part_s[...] = part_s[...] + got_s[away]
+
     def leave(at):
         rows = pl.ds(pl.multiple_of(at * 256, 256), 256)
         return pltpu.make_async_copy(rnd_s.at[rows], gtok_o.at[rows], osem.at[at])
@@ -1191,7 +1229,7 @@
             half = pl.ds(128, CTX)
             nb_s[half, :] = nb_s[half, :] + skip[...] * gctx_s[...]
 
-        run(group_at, 9 + 3 * at, 12 + 3 * at)
+        run(group_at, 6 + 3 * at, 9 + 3 * at)
 
         xhat, inverse = norm_parts(wo_s[rows, :].astype(F32))
         grad = nb_s[...]
@@ -1209,16 +1247,11 @@
 
     each_device(lambda away: share(away).start())
     part_s[...] = sum_s[tile(me)]
-    run(group_at, 21, 24)
-
-    def add_in(away):
-        share(away).wait_recv()
-        part_s[...] = part_s[...] + got_s[away]
-
+    run(group_at, 18, 21)
     each_device(add_in)
     each_device(lambda away: spread(away).start())
     sums_o[tile(me)] = part_s[...]
-    run(group_at, 24, 30)
+    run(group_at, 21, 27)
 
     for which in (3 * rep, 1, 2, 4):
         big.finish(which).wait_send()
@@ -1229,19 +1262,16 @@
         big.finish(which).wait_recv()
     for which in (1 - rep, 2, 3):
         group.finish(which).wait_recv()
-    for source, target in ((fin_b, finb_o), (finr_b, finrb_o), (fin_g, fing_o), (finr_g, finrg_o)):
-        target[...] = source[...]
-
     def settle(away):
         spread(away).wait()
         share(away).wait_send()
 
     each_device(settle)
     for i in range(4):
-        mate_big(i, dwup.at[i, :, theirs]).wait_send()
         mate_group(i).wait_send()
         leave(i).wait()
-    mate_big(4, go_s).wait_send()
+    mate_out.wait_send()
+    swap.wait()
 
     @pl.loop(0, NC)
     def _(n):
@@ -1268,26 +1298,25 @@
         backward_kernel,
         name="backward_part",
         out_shape=(
-            shape(full, BF16), shape((5,) + part, BF16), shape((5,) + part, BF16),
+            shape(full, BF16), shape((192, 1024), BF16), shape((5,) + part, BF16), shape((5,) + part, BF16),
             shape((4,) + cut, BF16), shape((4,) + cut, BF16), shape((64, 1024), F32),
         ),
-        in_specs=any_spec(11) + vmem_spec(10),
-        out_specs=any_spec(1) + vmem_spec(5),
+        in_specs=any_spec(13) + vmem_spec(10),
+        out_specs=any_spec(2) + vmem_spec(5),
         scratch_shapes=[
             vmem((5, NC) + part, BF16), vmem((5, NC) + part, BF16), vmem((4, NC - 1) + part, BF16),
-            vmem((NC,) + part, BF16), vmem((5,) + part, BF16), vmem((5,) + part, BF16), vmem(part, F32),
+            vmem((NC,) + part, BF16), vmem(part, F32),
             vmem((4, NC, 2) + cut, BF16), vmem((4, NC) + cut, BF16), vmem((3, NC - 1) + cut, BF16),
-            vmem((NC,) + cut, BF16), vmem((4,) + cut, BF16), vmem((4,) + cut, BF16), vmem(cut, F32),
+            vmem((NC,) + cut, BF16), vmem(cut, F32),
             vmem((NC,) + part, BF16),
             vmem(full, BF16), vmem(full, BF16), vmem(full, BF16), vmem(full, BF16), vmem(full, BF16),
             vmem(ext, BF16), vmem(ext, BF16), vmem(ext, BF16), vmem(ext, BF16), vmem(ext, BF16),
             vmem((2, BLK, CTX + BLK), BF16), vmem((BLK, CTX + BLK), BF16), vmem((2, 256, 1024), BF16),
-            vmem((256, 1024), F32), vmem((1024, 128), BF16), vmem((128, 1024), F32), vmem((CTX, 1024), F32),
-            vmem((64, 1024), F32), vmem((4 * NC, 16, 128), F32), vmem((16, 128), F32),
-            dma((12,)), dma((2,)), dma((2,)), dma((4,)), dma((5,)), dma((5,)), dma((4,)), dma((4,)),
+            vmem((256, 1024), F32), vmem((1024, 128), BF16), vmem((128, 1024), F32), vmem((CTX, 1024), F32), vmem((64, 1024), F32), vmem((4 * NC, 16, 128), F32), vmem((16, 128), F32),
+            dma((10,)), dma((2,)), dma((2,)), dma((4,)), dma((1,)), dma((1,)), dma((4,)), dma((4,)),
             dma((4, NC - 1)), dma((4, NC - 1)), dma((3, NC - 1)), dma((3, NC - 1)),
             dma((NC,)), dma((NC,)), dma((NC,)), dma((NC,)), dma((5,)), dma((5,)), dma((4,)), dma((4,)),
-            dma((4 * NC,)), dma((4 * NC,)), dma((4 * NC,)), dma((4 * NC,)),
+            dma((4 * NC,)), dma((4 * NC,)), dma((4 * NC,)), dma((4 * NC,)), dma((1,)), dma((1,)),
         ],
         compiler_params=pltpu.CompilerParams(
             collective_id=2, has_side_effects=True, vmem_limit_bytes=VMEM_LIMIT
@@ -1355,15 +1384,15 @@
             first_gain, first_bias, skip_gain, second_gain, second_bias, down_bias, up_bias, decay_rates,
         )
     )
-    wall, sio, rnd, q, kx, vx, att, res, sec, p, u, st = run_forward(
-        tok, query_weight, key_weight, value_weight, output_weight, up_weight, state_in, state_out,
+    wall, wdpre, sio, rnd, q, kx, vx, att, res, sec, p, u, st = run_forward(
+        tok, query_weight, key_weight, value_weight, output_weight, up_weight, down_weight, state_in, state_out,
         fg, fb, skip, sg, sb, decay,
     )
-    result, gatt, dwup, find, findr, gdb, gub, gsg, gsb = run_feed(
-        sec, res, wall, down_weight, cot, lengths, upb, dnb, sg
-    )
-    gtok, finb, finrb, fing, finrg, sums = run_backward(
-        dwup.reshape(4, NC, 2, 64, 1024), gatt, att, wall, q, kx, vx, rnd, p, tok, sio,
+    result, gatt, dwown, dwmate, find, gdb, gub, gsg, gsb = run_feed(
+        sec, res, wall, down_weight, wdpre, cot, lengths, upb, dnb, sg
+    )
+    gtok, findr, finb, finrb, fing, finrg, sums = run_backward(
+        dwown, dwmate, find, gatt, att, wall, q, kx, vx, rnd, p, tok, sio,
         u, st, fg, fb, skip, decay, gsg, gsb, gdb, gub,
     )
     dup, do, dq, dk, dv, ddown, *rest = run_outputs(finb, finrb, fing, finrg, find, findr, sums)

time: 321 us -> 295 us (0.919)
  Pallas kernels: 313 us -> 287 us
    pallas_call x1, Pallas kernels: 112 us -> 95.6 us  [run_feed(): pl.pallas_call(feed_kernel, name='feed_part', out_shape=(shape(big, BF16)...]
    pallas_call x1, Pallas kernels: 91 us -> 85.2 us  [run_forward(): pl.pallas_call(forward_kernel, name='forward_part', out_shape=(shape((8,)...]
    pallas_call x1, Pallas kernels: 106 us -> 103 us  [run_backward(): pl.pallas_call(backward_kernel, name='backward_part', out_shape=(shape(fu...]
where the time goes in v3:
time: 295 us; the launch traced here: 294 us
  Pallas kernels  287 us (97%)
  local copies, waits for them, and re-layouts  5.72 us (2%)
    pallas_call x1, Pallas kernels, run_backward(): pl.pallas_call(backward_kernel, name='backward_part', out_shape=(shape(fu...  103 us
    pallas_call x1, Pallas kernels, run_feed(): pl.pallas_call(feed_kernel, name='feed_part', out_shape=(shape(big, BF16)...  95.6 us
    pallas_call x1, Pallas kernels, run_forward(): pl.pallas_call(forward_kernel, name='forward_part', out_shape=(shape((8,)...  85.2 us

profile of v3, /device:TPU:0, one launch (start us, length us, event | category | flops | bytes accessed | tf_op | source)
XLA Modules:
  0.0 294.4 jit_solution(7694203035103835766)
XLA Ops:
  1.3 85.2 %forward_part.1 = (bf16[8,1024,1024]{2,1,0:T(8,128)(2,1)}, bf16[2,256,1024]{2,1,0:T(8,128)(2,1)}, bf16[1024,128]{1,0:T(8,128)(2,1)}, bf16[1152,1024]{1,0:T(8,128...) custom-call(bf16[1024,1024]{1,0:T(8,128)(2,1)} %bitcast.21, ...), custom_call_target="tpu_custom_call" | custom-call | tf_op jit(solution)/shard_map/forward_part/pallas_call | solution.py:451
  86.5 95.6 %feed_part.1 = (bf16[1024,1024]{1,0:T(8,128)(2,1)}, bf16[1024,1024]{1,0:T(8,128)(2,1)}, bf16[4,8,64,1024]{3,2,1,0:T(8,128)(2,1)}, bf16[4,8,64,1024]{3,2,1,0:T(8,...) custom-call(bf16[1024,1024]{1,0:T(8,128)(2,1)} %get-tuple-element.63, ...), custom_call_target="tpu_custom_call" | custom-call | tf_op jit(solution)/shard_map/feed_part/pallas_call | solution.py:827
  182.2 102.8 %backward_part.1 = (bf16[1024,1024]{1,0:T(8,128)(2,1)}, bf16[192,1024]{1,0:T(8,128)(2,1)}, bf16[5,64,1024]{2,1,0:T(8,128)(2,1)}, bf16[5,64,1024]{2,1,0:T(8,128)(...) custom-call(bf16[4,8,64,1024]{3,2,1,0:T(8,128)(2,1)} %get-tuple-element.68.dwown, ...), custom_call_target="tpu_custom_call" | custom-call | tf_op jit(solution)/shard_map/backward_part/pallas_call | solution.py:1297
  285.0 3.6 %outputs_part.1 = (f32[64,4096]{1,0:T(8,128)}, f32[64,1024]{1,0:T(8,128)}, f32[64,1024]{1,0:T(8,128)}, f32[64,1024]{1,0:T(8,128)}, f32[64,1024]{1,0:T(8,128)}, /...) custom-call(bf16[5,64,1024]{2,1,0:T(8,128)(2,1)} %get-tuple-element., ...), custom_call_target="tpu_custom_call" | custom-call | tf_op jit(solution)/shard_map/outputs_part/pallas_call | solution.py:1360
  288.7 1.2 slice_bitcast_fusion
  289.8 0.0 copy-start
  289.8 3.2 %copy.40 = bf16[1,1024,1024]{2,1,0:T(8,128)(2,1)} copy(bf16[1,1024,1024]{2,1,0:T(8,128)(2,1)} %bitcast.24) | data formatting | bytes 4194304
  293.1 0.0 copy-done
  293.1 1.3 copy.41
Async XLA Ops:
  289.8 3.2 %copy-start = (bf16[1024,1024]{1,0:T(8,128)(2,1)S(1)}, bf16[1024,1024]{1,0:T(8,128)(2,1)}, u32[]{:S(2)}) copy-start(bf16[1024,1024]{1,0:T(8,128)(2,1)} %get-tuple-element.85) | copy-start | bytes 6291460

commit v4 on v3

--- a/solution.py
+++ b/solution.py
@@ -237,10 +237,10 @@
             if hop < 3 - way:
                 ring_small(way, hop + 1, where).start()
             mate_small(1 + 2 * hop + way, where).start()
-        if n in (10, 12):
+        if n in (12, 13):
             for later in range(2):
                 for each in range(2):
-                    ring_own(n - 8 + later, each)
+                    ring_own((2 if n == 12 else 4) + later, each)
         if owed and n - owed[0][0] >= 6:
             serve_in(0, *owed.pop(0)[1:])
     first_norm(7)
@@ -668,8 +668,8 @@
             return upb[:, pl.ds(pl.multiple_of(shard * 256, 256), 256)]
 
         def middle(half, shard, at):
-            for block_at in range(2):
-                rows = pl.ds(pl.multiple_of(at * 512 + block_at * 256, 256), 256)
+            for block_at in range(1):
+                rows = pl.ds(pl.multiple_of(at * 512 + block_at * 256, 256), 512)
                 cols = pl.ds(half * 256, 256)
                 hidden = dot_nn(sec_s[rows, :], up(shard)) + bias(shard)
                 grad = dot_nt(gb_s[rows, :], wd_s[block(shard), :])
@@ -730,21 +730,25 @@
             dwup_copy(slot, half, shard).start()
             dwup_mate(step, half, shard).start()
 
-        @pl.loop(0, 4)
+        @pl.loop(0, 2)
         def _(at):
-            rows = pl.ds(pl.multiple_of(at * 256, 256), 256)
+            rows = pl.ds(pl.multiple_of(at * 512, 512), 512)
             down = jnp.concatenate([wd_s[block(a), :], wd_s[block(b), :]], axis=0)
             br_s[rows, :] = br_s[rows, :] + dot_nn(act_s[rows, :], down)
             rise = jnp.concatenate([up(a), up(b)], axis=1)
             gs_s[rows, :] = gs_s[rows, :] + dot_nt(gh_s[rows, :], rise)
 
-            @pl.when((at < 3) & (step >= 1))
+            @pl.when(step >= 1)
             def _():
                 forward((2 * rep + 1 + at) % 3, step - 1)
 
             @pl.when((at == 1) & (step < NC - 2))
             def _():
                 serve_twin(step + 1)
+
+        @pl.when(step >= 1)
+        def _():
+            forward((2 * rep + 3) % 3, step - 1)
 
     def residual_in(at):
         rows = pl.ds(at * 256, 256)
@@ -1002,7 +1006,7 @@
 
     def big_at(e):
         k, j = e // 4, e % 4
-        n = k - 2 * (j // 2) - j // 3
+        n = k - j - (j // 2) * (1 - 2 * (j // 3))
         which = (j + 1) * (1 - j // 2) + (j // 2) * (3 * rep * (1 - j // 3) + 4 * (j // 3))
 
         @pl.when((j == 3) & (n == 0))
@@ -1015,7 +1019,7 @@
 
     def group_at(e):
         k, j = e // 3, e % 3
-        n = k - j // 2
+        n = k
         which = rep * (1 - (j + 1) // 2) + (j + 1) * ((j + 1) // 2)
 
         @pl.when((j >= 1) & (n == 0))
@@ -1047,18 +1051,18 @@
 
     p_copy(0, 0).start()
 
-    @pl.loop(0, 4)
+    @pl.loop(0, 2)
     def _(at):
-        rows = pl.ds(pl.multiple_of(at * 256, 256), 256)
+        rows = pl.ds(pl.multiple_of(at * 512, 512), 512)
         ga_s[rows, :] = dot_nt(gatt_s[rows, :], wo_s[...]).astype(BF16)
 
     run(big_at, 4, 8)
     loads[2].wait()
 
-    @pl.loop(0, 4)
+    @pl.loop(0, 2)
     def _(at):
-        cols = pl.ds(pl.multiple_of(at * 256, 256), 256)
-        made = dot_tn(att_s[...], gatt_s[:, cols]).reshape(NC, 2, 64, 256)
+        cols = pl.ds(pl.multiple_of(at * 512, 512), 512)
+        made = dot_tn(att_s[...], gatt_s[:, cols]).reshape(NC, 2, 64, 512)
         own_b[4, :, :, cols] = jnp.where(core == 0, made[:, 0], made[:, 1]).astype(BF16)
         go_s[:, :, cols] = jnp.where(core == 0, made[:, 1], made[:, 0]).astype(BF16)
 
@@ -1128,20 +1132,18 @@
                 dk_s[rows, cols] = made_k.astype(BF16)
                 dv_s[rows, cols] = made_v.astype(BF16)
 
-                @pl.when(m < 15)
-                def _(m=m):
-                    run(big_at, 8 + (5 * m) // 2, 8 + (5 * m + 5) // 2)
-
-
-                @pl.when(m == 9)
+                run(big_at, 8 + 2 * m, 10 + 2 * m)
+
+
+                @pl.when(m == 10)
                 def _():
                     for each in range(2):
                         mate_group(each).wait_recv()
 
-                @pl.when((m >= 9) & (m < 13))
+                @pl.when((m >= 10) & (m < 14))
                 def _(m=m):
                     for e in range(2):
-                        group.give(1 - rep, 2 * (m - 9) + e)
+                        group.give(1 - rep, 2 * (m - 10) + e)
 
         @pl.when(g == 3)
         def _():
@@ -1154,7 +1156,8 @@
         own_g[g, :, :, :, 512:768] = dot_tn(rnd_s[...], dv_s[:, cols]).astype(BF16).reshape(NC, 2, 64, 256)
         mate_group(g).start()
 
-    run(group_at, 0, 3)
+    run(big_at, 40, 44)
+    run(group_at, 0, 2)
     for i in range(3):
         weights_in(i).wait()
     tok_load.wait()
@@ -1175,7 +1178,7 @@
         sum_s[at : at + 1, :] = vector[...]
     for at in range(4):
         sum_s[38 + at : 39 + at, :] = gub[:, at * 1024 : (at + 1) * 1024]
-    run(group_at, 3, 6)
+    run(group_at, 2, 5)
     states, raw = st_in[...], u_in[...]
     factor = jnp.exp(-column(decay[...]))
     scale = jnp.sqrt(1.0 - factor * factor)
@@ -1214,24 +1217,27 @@
         def _():
             gres_in(at + 1).start()
 
+        xhat, inverse = norm_parts(wo_s[rows, :].astype(F32))
         nb_s[...] = (
             dot_nt(dq_s[rows, :], q_s[...])
             + dot_nt(dk_s[rows, :], k_s[0:1024, :])
             + dot_nt(dv_s[rows, :], v_s[0:1024, :])
-            + split_dot(
+        )
+
+        @pl.when(at < 2)
+        def _():
+            nb_s[...] = nb_s[...] + split_dot(
                 lambda a, b: lax.dot_general(a, b, (((0,), (1,)), ((), ())), preferred_element_type=F32),
                 gd_s[:, rows], sio_s[...], 3,
             )
-        )
 
         @pl.when(at == 1)
         def _():
             half = pl.ds(128, CTX)
             nb_s[half, :] = nb_s[half, :] + skip[...] * gctx_s[...]
 
-        run(group_at, 6 + 3 * at, 9 + 3 * at)
-
-        xhat, inverse = norm_parts(wo_s[rows, :].astype(F32))
+        run(group_at, 5 + 3 * at, 8 + 3 * at)
+
         grad = nb_s[...]
         gain = jnp.sum(grad * xhat, axis=0, keepdims=True)
         shift = jnp.sum(grad, axis=0, keepdims=True)
@@ -1247,11 +1253,11 @@
 
     each_device(lambda away: share(away).start())
     part_s[...] = sum_s[tile(me)]
-    run(group_at, 18, 21)
+    run(group_at, 17, 20)
     each_device(add_in)
     each_device(lambda away: spread(away).start())
     sums_o[tile(me)] = part_s[...]
-    run(group_at, 21, 27)
+    run(group_at, 20, 24)
 
     for which in (3 * rep, 1, 2, 4):
         big.finish(which).wait_send()
@@ -1325,11 +1331,27 @@
 
 
 def outputs_kernel(
-    finb, finrb, fing, finrg, find, findr, sums,
-    dup_o, do_o, dq_o, dk_o, dv_o, ddown_o, gfg_o, gfb_o, gskip_o, gsg_o, gsb_o, gdb_o, gub_o, grate_o,
-    gsi_o, gso_o,
+    result, gtok, finb, finrb, fing, finrg, find, findr, sums,
+    result_o, gtok_o, dup_o, do_o, dq_o, dk_o, dv_o, ddown_o, gfg_o, gfb_o, gskip_o, gsg_o, gsb_o, gdb_o, gub_o, grate_o,
+    gsi_o, gso_o, held, came, left,
 ):
     rep, shard = lax.axis_index("rep"), lax.axis_index("shard")
+    pairs = ((result, result_o), (gtok, gtok_o))
+
+    def take(which, at):
+        rows = pl.ds(at * 256, 256)
+        return pltpu.make_async_copy(pairs[which][0].at[rows], held.at[which, rows], came.at[which, at])
+
+    def give(which, at):
+        rows = pl.ds(at * 256, 256)
+        return pltpu.make_async_copy(held.at[which, rows], pairs[which][1].at[rows], left.at[which, at])
+
+    every = [(which, at) for which in range(2) for at in range(4)]
+    for each in every:
+        take(*each).start()
+    for each in every:
+        take(*each).wait()
+        give(*each).start()
     for i in range(4):
         dup_o[:, i * 1024 : (i + 1) * 1024] = finb[i].astype(F32) + finrb[i].astype(F32)
     do_o[...] = finb[4].astype(F32) + finrb[4].astype(F32)
@@ -1347,10 +1369,12 @@
     for at in range(4):
         gub_o[:, at * 1024 : (at + 1) * 1024] = sums[38 + at : 39 + at, :]
     same = lax.broadcasted_iota(jnp.int32, (16, 128), 0) == lax.broadcasted_iota(jnp.int32, (16, 128), 1)
-    grate_o[...] = jnp.sum(jnp.where(same, sums[48:64, 0:128], 0.0), axis=0, keepdims=True)
+    grate_o[...] = jnp.sum(jnp.where(same, sums[48:64, 0:128], 0.0), axis=0)[0:16]
     shift = (1024 - 64 * shard) % 1024
     gsi_o[...] = pltpu.roll(sums[0:16, :], shift, 1)[:, 0:64]
     gso_o[...] = pltpu.roll(sums[16:32, :], shift, 1)[:, 0:64]
+    for each in every:
+        give(*each).wait()
 
 
 def run_outputs(*operands):
@@ -1361,12 +1385,17 @@
         outputs_kernel,
         name="outputs_part",
         out_shape=(
+            shape((1024, 1024), BF16), shape((1024, 1024), BF16),
             shape((64, 4096), F32), part, part, part, part, shape((256, 1024), F32),
-            row, row, row, row, row, row, shape((1, 4096), F32), shape((1, 128), F32),
+            row, row, row, row, row, row, shape((1, 4096), F32), shape((16,), F32),
             shape((16, 64), F32), shape((16, 64), F32),
         ),
-        in_specs=vmem_spec(7),
-        out_specs=vmem_spec(16),
+        in_specs=any_spec(2) + vmem_spec(7),
+        out_specs=any_spec(2) + vmem_spec(16),
+        scratch_shapes=[
+            pltpu.VMEM((2, 1024, 1024), BF16),
+            pltpu.SemaphoreType.DMA((2, 4)), pltpu.SemaphoreType.DMA((2, 4)),
+        ],
         compiler_params=pltpu.CompilerParams(vmem_limit_bytes=VMEM_LIMIT),
     )(*operands)
 
@@ -1395,11 +1424,13 @@
         dwown, dwmate, find, gatt, att, wall, q, kx, vx, rnd, p, tok, sio,
         u, st, fg, fb, skip, decay, gsg, gsb, gdb, gub,
     )
-    dup, do, dq, dk, dv, ddown, *rest = run_outputs(finb, finrb, fing, finrg, find, findr, sums)
+    result, gtok, dup, do, dq, dk, dv, ddown, *rest = run_outputs(
+        result, gtok, finb, finrb, fing, finrg, find, findr, sums
+    )
     gfg, gfb, gskip, gsg, gsb, gdb, gub, grate, gsi, gso = rest
     return (
         result.reshape(1, 1024, 1024), gtok.reshape(1, 1024, 1024), gfg[0], gfb[0],
-        grate[0, 0:16], gsi, gso, gskip[0], dq, dk, dv, do, gsg[0], gsb[0], dup, gub[0], ddown, gdb[0],
+        grate, gsi, gso, gskip[0], dq, dk, dv, do, gsg[0], gsb[0], dup, gub[0], ddown, gdb[0],
     )
 
 

time: 295 us -> 284 us (0.963)
  local copies, waits for them, and re-layouts: 5.72 us -> 0 us
  Pallas kernels: 287 us -> 282 us
    pallas_call x1, Pallas kernels: 103 us -> 97.9 us  [run_backward(): pl.pallas_call(backward_kernel, name='backward_part', out_shape=(shape(fu...]
    unnamed x4 -> x0, local copies, waits for them, and re-layouts: 4.55 us -> none
    pallas_call x1, Pallas kernels: 3.63 us -> 7.1 us  [run_outputs(): pl.pallas_call(outputs_kernel, name='outputs_part', out_shape=(shape((102...]
where the time goes in v4:
time: 284 us
  Pallas kernels  282 us (99%)
    pallas_call x1, Pallas kernels, run_backward(): pl.pallas_call(backward_kernel, name='backward_part', out_shape=(shape(fu...  97.9 us
    pallas_call x1, Pallas kernels, run_feed(): pl.pallas_call(feed_kernel, name='feed_part', out_shape=(shape(big, BF16)...  93.2 us
    pallas_call x1, Pallas kernels, run_forward(): pl.pallas_call(forward_kernel, name='forward_part', out_shape=(shape((8,)...  84.1 us
    pallas_call x1, Pallas kernels, run_outputs(): pl.pallas_call(outputs_kernel, name='outputs_part', out_shape=(shape((102...  7.1 us

profile of v4, /device:TPU:0, one launch (start us, length us, event | category | flops | bytes accessed | tf_op | source)
XLA Modules:
  0.0 283.8 jit_solution(5524288031052510151)
XLA Ops:
  1.3 84.1 %forward_part.1 = (bf16[8,1024,1024]{2,1,0:T(8,128)(2,1)}, bf16[2,256,1024]{2,1,0:T(8,128)(2,1)}, bf16[1024,128]{1,0:T(8,128)(2,1)}, bf16[1152,1024]{1,0:T(8,128...) custom-call(bf16[1024,1024]{1,0:T(8,128)(2,1)} %bitcast.19, ...), custom_call_target="tpu_custom_call" | custom-call | tf_op jit(solution)/shard_map/forward_part/pallas_call | solution.py:451
  85.4 93.2 %feed_part.1 = (bf16[1024,1024]{1,0:T(8,128)(2,1)}, bf16[1024,1024]{1,0:T(8,128)(2,1)}, bf16[4,8,64,1024]{3,2,1,0:T(8,128)(2,1)}, bf16[4,8,64,1024]{3,2,1,0:T(8,...) custom-call(bf16[1024,1024]{1,0:T(8,128)(2,1)} %get-tuple-element.65, ...), custom_call_target="tpu_custom_call" | custom-call | tf_op jit(solution)/shard_map/feed_part/pallas_call | solution.py:831
  178.6 97.9 %backward_part.1 = (bf16[1024,1024]{1,0:T(8,128)(2,1)}, bf16[192,1024]{1,0:T(8,128)(2,1)}, bf16[5,64,1024]{2,1,0:T(8,128)(2,1)}, bf16[5,64,1024]{2,1,0:T(8,128)(...) custom-call(bf16[4,8,64,1024]{3,2,1,0:T(8,128)(2,1)} %get-tuple-element.70.dwown, ...), custom_call_target="tpu_custom_call" | custom-call | tf_op jit(solution)/shard_map/backward_part/pallas_call | solution.py:1303
  276.5 7.1 %outputs_part.1 = (bf16[1024,1024]{1,0:T(8,128)(2,1)}, bf16[1024,1024]{1,0:T(8,128)(2,1)}, f32[64,4096]{1,0:T(8,128)}, f32[64,1024]{1,0:T(8,128)}, f32[64,1024]{...) custom-call(bf16[1024,1024]{1,0:T(8,128)(2,1)} %get-tuple-element.69, ...), custom_call_target="tpu_custom_call" | custom-call | tf_op jit(solution)/shard_map/outputs_part/pallas_call | solution.py:1384

commit v5 on v4

--- a/solution.py
+++ b/solution.py
@@ -241,7 +241,7 @@
             for later in range(2):
                 for each in range(2):
                     ring_own((2 if n == 12 else 4) + later, each)
-        if owed and n - owed[0][0] >= 6:
+        if owed and n - owed[0][0] >= 4:
             serve_in(0, *owed.pop(0)[1:])
     first_norm(7)
     for each in owed:
@@ -667,42 +667,34 @@
         def bias(shard):
             return upb[:, pl.ds(pl.multiple_of(shard * 256, 256), 256)]
 
-        def middle(half, shard, at):
-            for block_at in range(1):
-                rows = pl.ds(pl.multiple_of(at * 512 + block_at * 256, 256), 512)
-                cols = pl.ds(half * 256, 256)
-                hidden = dot_nn(sec_s[rows, :], up(shard)) + bias(shard)
-                grad = dot_nt(gb_s[rows, :], wd_s[block(shard), :])
-                square = hidden * hidden
-                bent = jnp.tanh(hidden * (GELU_C + (GELU_C * GELU_A) * square))
-                half_up = 0.5 + 0.5 * bent
-                act_s[rows, cols] = (hidden * half_up).astype(BF16)
-                slope = half_up + (0.5 * hidden) * (1.0 - bent * bent) * (
-                    GELU_C + (3.0 * GELU_C * GELU_A) * square
-                )
-                gh_s[rows, cols] = (grad * slope).astype(BF16)
-
         @pl.loop(0, 2)
-        def _(at):
-            middle(0, a, at)
-
-        @pl.when(step < NC - 2)
-        def _():
-            serve(2 * rep, step + 1)
-
-        @pl.when(step >= 1)
-        def _():
-            for j in range(3):
-                mate_ring(j, index, b).wait_recv()
-            mate_sole(index, b, 1 - rep).wait_recv()
-
-        @pl.loop(0, 2)
-        def _(at):
-            middle(1, b, at)
+        def _(half):
+            @pl.when((half == 1) & (step >= 1))
+            def _():
+                for j in range(3):
+                    mate_ring(j, index, b).wait_recv()
+                mate_sole(index, b, 1 - rep).wait_recv()
+
+            shard = a + half * (b - a)
+            cols = pl.ds(pl.multiple_of(half * 256, 256), 256)
+            hidden = dot_nn(sec_s[...], up(shard)) + bias(shard)
+            grad = dot_nt(gb_s[...], wd_s[block(shard), :])
+            square = hidden * hidden
+            bent = jnp.tanh(hidden * (GELU_C + (GELU_C * GELU_A) * square))
+            half_up = 0.5 + 0.5 * bent
+            act_s[:, cols] = (hidden * half_up).astype(BF16)
+            slope = half_up + (0.5 * hidden) * (1.0 - bent * bent) * (
+                GELU_C + (3.0 * GELU_C * GELU_A) * square
+            )
+            gh_s[:, cols] = (grad * slope).astype(BF16)
 
             @pl.when(step < NC - 2)
             def _():
-                serve((2 * rep + 1 + at) % 3, step + 1)
+                serve((2 * rep + half) % 3, step + 1)
+
+            @pl.when((half == 1) & (step < NC - 2))
+            def _():
+                serve((2 * rep + 2) % 3, step + 1)
 
         made = dot_tn(act_s[...], gb_s[...])
 
@@ -733,10 +725,15 @@
         @pl.loop(0, 2)
         def _(at):
             rows = pl.ds(pl.multiple_of(at * 512, 512), 512)
-            down = jnp.concatenate([wd_s[block(a), :], wd_s[block(b), :]], axis=0)
-            br_s[rows, :] = br_s[rows, :] + dot_nn(act_s[rows, :], down)
-            rise = jnp.concatenate([up(a), up(b)], axis=1)
-            gs_s[rows, :] = gs_s[rows, :] + dot_nt(gh_s[rows, :], rise)
+
+            def rise_of(shard):
+                cols = pl.ds(pl.multiple_of((shard % 4) * 256, 256), 256)
+                return wup_s[shard // 4, rows, cols]
+
+            down = jnp.concatenate([wd_s[block(a), rows], wd_s[block(b), rows]], axis=0)
+            br_s[:, rows] = br_s[:, rows] + dot_nn(act_s[...], down)
+            rise = jnp.concatenate([rise_of(a), rise_of(b)], axis=1)
+            gs_s[:, rows] = gs_s[:, rows] + dot_nt(gh_s[...], rise)
 
             @pl.when(step >= 1)
             def _():
@@ -1349,11 +1346,11 @@
     every = [(which, at) for which in range(2) for at in range(4)]
     for each in every:
         take(*each).start()
+    for i in range(4):
+        dup_o[:, i * 1024 : (i + 1) * 1024] = finb[i].astype(F32) + finrb[i].astype(F32)
     for each in every:
         take(*each).wait()
         give(*each).start()
-    for i in range(4):
-        dup_o[:, i * 1024 : (i + 1) * 1024] = finb[i].astype(F32) + finrb[i].astype(F32)
     do_o[...] = finb[4].astype(F32) + finrb[4].astype(F32)
     for g in range(4):
         for i, out in enumerate((dq_o, dk_o, dv_o)):

time: 284 us -> 282 us (level)
  no operation moved by 1% of the time
where the time goes in v5:
time: 282 us
  Pallas kernels  280 us (99%)
    pallas_call x1, Pallas kernels, run_backward(): pl.pallas_call(backward_kernel, name='backward_part', out_shape=(shape(fu...  98.1 us
    pallas_call x1, Pallas kernels, run_feed(): pl.pallas_call(feed_kernel, name='feed_part', out_shape=(shape(big, BF16)...  91.2 us
    pallas_call x1, Pallas kernels, run_forward(): pl.pallas_call(forward_kernel, name='forward_part', out_shape=(shape((8,)...  84.1 us
    pallas_call x1, Pallas kernels, run_outputs(): pl.pallas_call(outputs_kernel, name='outputs_part', out_shape=(shape((102...  7.1 us

profile of v5, /device:TPU:0, one launch (start us, length us, event | category | flops | bytes accessed | tf_op | source)
XLA Modules:
  0.0 281.9 jit_solution(13850570811071268674)
XLA Ops:
  1.3 84.1 %forward_part.1 = (bf16[8,1024,1024]{2,1,0:T(8,128)(2,1)}, bf16[2,256,1024]{2,1,0:T(8,128)(2,1)}, bf16[1024,128]{1,0:T(8,128)(2,1)}, bf16[1152,1024]{1,0:T(8,128...) custom-call(bf16[1024,1024]{1,0:T(8,128)(2,1)} %bitcast.19, ...), custom_call_target="tpu_custom_call" | custom-call | tf_op jit(solution)/shard_map/forward_part/pallas_call | solution.py:451
  85.4 91.2 %feed_part.1 = (bf16[1024,1024]{1,0:T(8,128)(2,1)}, bf16[1024,1024]{1,0:T(8,128)(2,1)}, bf16[4,8,64,1024]{3,2,1,0:T(8,128)(2,1)}, bf16[4,8,64,1024]{3,2,1,0:T(8,...) custom-call(bf16[1024,1024]{1,0:T(8,128)(2,1)} %get-tuple-element.65, ...), custom_call_target="tpu_custom_call" | custom-call | tf_op jit(solution)/shard_map/feed_part/pallas_call | solution.py:828
  176.5 98.1 %backward_part.1 = (bf16[1024,1024]{1,0:T(8,128)(2,1)}, bf16[192,1024]{1,0:T(8,128)(2,1)}, bf16[5,64,1024]{2,1,0:T(8,128)(2,1)}, bf16[5,64,1024]{2,1,0:T(8,128)(...) custom-call(bf16[4,8,64,1024]{3,2,1,0:T(8,128)(2,1)} %get-tuple-element.70.dwown, ...), custom_call_target="tpu_custom_call" | custom-call | tf_op jit(solution)/shard_map/backward_part/pallas_call | solution.py:1300
  274.6 7.1 %outputs_part.1 = (bf16[1024,1024]{1,0:T(8,128)(2,1)}, bf16[1024,1024]{1,0:T(8,128)(2,1)}, f32[64,4096]{1,0:T(8,128)}, f32[64,1024]{1,0:T(8,128)}, f32[64,1024]{...) custom-call(bf16[1024,1024]{1,0:T(8,128)(2,1)} %get-tuple-element.69, ...), custom_call_target="tpu_custom_call" | custom-call | tf_op jit(solution)/shard_map/outputs_part/pallas_call | solution.py:1381

commit v6 on v5

--- a/solution.py
+++ b/solution.py
@@ -618,37 +618,52 @@
     def combine(step):
         slot = step % 2
         to_mate(step).wait_recv()
-        a_s[slot] = a_s[slot] + prec[step].astype(F32)
 
         @pl.when(step >= 2)
         def _():
             to_twin(step - 2).wait_send()
 
-        xsend[slot] = a_s[slot, sole_theirs, :].astype(BF16)
+        xsend[slot] = (a_s[slot, sole_theirs, :] + prec[step, sole_theirs, :].astype(F32)).astype(BF16)
         to_twin(step).start()
 
     def forward(j, step):
         slot = step % 2
         rows = pl.ds(pl.multiple_of((rep + j) * part, part), part)
 
+        def both():
+            return a_s[slot, rows, :] + prec[step, rows, :].astype(F32)
+
+        def with_ring():
+            return both() + rrec[step - 1, j].astype(F32)
+
         @pl.when(j == 2 * rep)
         def _():
             to_twin(step).wait_recv()
             a_s[slot, rows, :] = a_s[slot, rows, :] + xrec[step].astype(F32)
 
+        @pl.when(step == 0)
+        def _():
+            rsend[slot, j] = both().astype(BF16)
+
         @pl.when(step >= 1)
         def _():
             to_ring(j, step - 1).wait_recv()
-            a_s[slot, rows, :] = a_s[slot, rows, :] + rrec[step - 1, j].astype(F32)
 
         @pl.when((step >= 2) & (step < NC - 1))
         def _():
             to_ring(j, step - 2).wait_send()
 
+        @pl.when((step >= 1) & (step < NC - 1))
+        def _():
+            rsend[slot, j] = with_ring().astype(BF16)
+
         @pl.when(step < NC - 1)
         def _():
-            rsend[slot, j] = a_s[slot, rows, :].astype(BF16)
             to_ring(j, step).start()
+
+        @pl.when(step == NC - 1)
+        def _():
+            a_s[slot, rows, :] = with_ring()
 
     @pl.loop(0, NC)
     def _(step):

time: 282 us -> 282 us (level)
  no operation moved by 1% of the time
where the time goes in v6:
time: 282 us
  Pallas kernels  280 us (99%)
    pallas_call x1, Pallas kernels, run_backward(): pl.pallas_call(backward_kernel, name='backward_part', out_shape=(shape(fu...  98 us
    pallas_call x1, Pallas kernels, run_feed(): pl.pallas_call(feed_kernel, name='feed_part', out_shape=(shape(big, BF16)...  91.1 us
    pallas_call x1, Pallas kernels, run_forward(): pl.pallas_call(forward_kernel, name='forward_part', out_shape=(shape((8,)...  84.1 us
    pallas_call x1, Pallas kernels, run_outputs(): pl.pallas_call(outputs_kernel, name='outputs_part', out_shape=(shape((102...  7.1 us

profile of v6, /device:TPU:0, one launch (start us, length us, event | category | flops | bytes accessed | tf_op | source)
XLA Modules:
  0.0 281.8 jit_solution(8239798315811582310)
XLA Ops:
  1.3 84.1 %forward_part.1 = (bf16[8,1024,1024]{2,1,0:T(8,128)(2,1)}, bf16[2,256,1024]{2,1,0:T(8,128)(2,1)}, bf16[1024,128]{1,0:T(8,128)(2,1)}, bf16[1152,1024]{1,0:T(8,128...) custom-call(bf16[1024,1024]{1,0:T(8,128)(2,1)} %bitcast.19, ...), custom_call_target="tpu_custom_call" | custom-call | tf_op jit(solution)/shard_map/forward_part/pallas_call | solution.py:451
  85.4 91.1 %feed_part.1 = (bf16[1024,1024]{1,0:T(8,128)(2,1)}, bf16[1024,1024]{1,0:T(8,128)(2,1)}, bf16[4,8,64,1024]{3,2,1,0:T(8,128)(2,1)}, bf16[4,8,64,1024]{3,2,1,0:T(8,...) custom-call(bf16[1024,1024]{1,0:T(8,128)(2,1)} %get-tuple-element.65, ...), custom_call_target="tpu_custom_call" | custom-call | tf_op jit(solution)/shard_map/feed_part/pallas_call | solution.py:843
  176.5 98.0 %backward_part.1 = (bf16[1024,1024]{1,0:T(8,128)(2,1)}, bf16[192,1024]{1,0:T(8,128)(2,1)}, bf16[5,64,1024]{2,1,0:T(8,128)(2,1)}, bf16[5,64,1024]{2,1,0:T(8,128)(...) custom-call(bf16[4,8,64,1024]{3,2,1,0:T(8,128)(2,1)} %get-tuple-element.70.dwown, ...), custom_call_target="tpu_custom_call" | custom-call | tf_op jit(solution)/shard_map/backward_part/pallas_call | solution.py:1315
  274.5 7.1 %outputs_part.1 = (bf16[1024,1024]{1,0:T(8,128)(2,1)}, bf16[1024,1024]{1,0:T(8,128)(2,1)}, f32[64,4096]{1,0:T(8,128)}, f32[64,1024]{1,0:T(8,128)}, f32[64,1024]{...) custom-call(bf16[1024,1024]{1,0:T(8,128)(2,1)} %get-tuple-element.69, ...), custom_call_target="tpu_custom_call" | custom-call | tf_op jit(solution)/shard_map/outputs_part/pallas_call | solution.py:1396
